TPU v7x, 512 devices: a whole 4x8x8 slice. The times are simulated.
512 devices in a mesh: grp: 8 (over x, core), ep: 64 (over z, y).
Axes of the slice: x: 4, y: 8, z: 8, core: 2. Of those that a mesh axis runs over, the one named last changes fastest.
Arguments:
- resid: bfloat16 [8192, 2048], P('ep', 'grp'), may hold values from -6 to 6
- query: bfloat16 [8192, 2048], P('ep', 'grp'), may hold values from -6 to 6
- key_new: bfloat16 [8192, 2048], P('ep', 'grp'), may hold values from -6 to 6
- value_new: bfloat16 [8192, 2048], P('ep', 'grp'), may hold values from -6 to 6
- cache_kv: bfloat16 [2, 65536, 2048], P(None, 'ep', 'grp'), may hold values from -6 to 6
- cache_len: int32 [64], replicated, may hold values from 1 to 1024, 16384 in all
- w_out: bfloat16 [2048, 2048], P('grp'), may hold values from -0.125 to 0.125
- norm_gain: bfloat16 [2048], replicated, may hold values from 0.099609375 to 1.8984375
- w_router: bfloat16 [2048, 64], replicated, may hold values from -7 to 7
- routes: int32 [8192, 4], P('ep'), may hold values from 0 to 63, all different within a row; in each aligned block of 128 rows (0 to 127, 128 to 255, ...) at most 16 rows name the same one
- w_gate_up: bfloat16 [64, 2, 2048, 1408], P('ep', None, None, 'grp'), may hold values from -0.125 to 0.125
- w_down: bfloat16 [64, 1408, 2048], P('ep', 'grp'), may hold values from -0.15625 to 0.15625
Outputs:
- after_attention: bfloat16 [8192, 2048], P('ep', 'grp')
- expert_mix: bfloat16 [8192, 2048], P('ep', 'grp')
Inputs may be any that keep to these rules, and one draw needn't show every extreme that they name: `routes`: in each aligned block of 128 rows (one request's tokens), no expert is named by more than 16 of the pairs, and in every draw some expert is named by exactly 16. Request r's cache fills the first cache_len[r] rows of its slab, rows r * 1024 onward of cache_kv; the rest of the slab is unused; the lengths sum to 16384 and the longest is exactly 1024.
All inputs are finite; a program needn't handle non-finite values.
Results may differ from a plain program's by a relative error of at most 0.013.
Values may be sent and summed in bfloat16 or wider, within the bound.
No kernel may reach another device: no remote copies, remote signals or barrier semaphores. Data moves between devices by JAX's collectives and lax.ppermute only.
A program may use at most 64 MiB of HBM per device.

v0:
```python
import jax
import jax.numpy as jnp
from jax import lax
from jax.sharding import PartitionSpec as P

D = 2048
HD = 128
TOP = 4


EPS = 1e-06
MASKED = -1e30


def expert_rows(arrived, w_gate_up, w_down):
    features = arrived.shape[-1]
    flat_rows = arrived.reshape(-1, features)
    gate_value = jnp.dot(flat_rows, w_gate_up[0, 0], preferred_element_type=jnp.float32)
    up_value = jnp.dot(flat_rows, w_gate_up[0, 1], preferred_element_type=jnp.float32)
    hidden = (jax.nn.silu(gate_value) * up_value).astype(jnp.bfloat16)
    partial_value = jnp.dot(hidden, w_down[0], preferred_element_type=jnp.float32).astype(
        jnp.bfloat16
    )
    return partial_value.reshape(arrived.shape)


def send_back(answered):
    return lax.all_to_all(answered, "ep", split_axis=0, concat_axis=0, tiled=True)


def body(
    resid,
    query,
    key_new,
    value_new,
    cache_kv,
    cache_len,
    w_out,
    norm_gain,
    w_router,
    routes,
    w_gate_up,
    w_down,
):
    tokens_here = query.shape[0]
    heads_here = query.shape[1] // HD
    experts_all = w_router.shape[1]
    column_width = resid.shape[1]
    group_index = lax.axis_index("grp")
    request = lax.axis_index("ep")
    capacity = max(2, 8 * tokens_here // lax.axis_size("ep"))
    score_scale = float(HD) ** (-0.5)
    column_start = group_index * column_width
    queries = query.reshape(tokens_here, heads_here, HD)
    new_keys = key_new.reshape(tokens_here, heads_here, HD)
    new_values = value_new.reshape(tokens_here, heads_here, HD)
    cache_rows = cache_kv.shape[1]
    cache_keys = cache_kv[0].reshape(cache_rows, heads_here, HD)
    cache_values = cache_kv[1].reshape(cache_rows, heads_here, HD)
    own_length = lax.dynamic_index_in_dim(cache_len, request, 0, keepdims=False)
    position = jnp.arange(tokens_here, dtype=jnp.int32)
    causal = (position[:, None] >= position[None, :])[:, None, :]
    new_scores = (
        jnp.einsum("qhd,khd->qhk", queries, new_keys, preferred_element_type=jnp.float32)
        * score_scale
    )
    new_scores = jnp.where(causal, new_scores, MASKED)
    live_rows = (jnp.arange(cache_rows, dtype=jnp.int32) < own_length)[None, None, :]
    old_scores = (
        jnp.einsum("qhd,khd->qhk", queries, cache_keys, preferred_element_type=jnp.float32)
        * score_scale
    )
    old_scores = jnp.where(live_rows, old_scores, MASKED)
    row_max = jnp.maximum(jnp.max(new_scores, axis=-1), jnp.max(old_scores, axis=-1))
    new_probs = jnp.exp(new_scores - row_max[..., None])
    old_probs = jnp.exp(old_scores - row_max[..., None])
    denominator = jnp.sum(new_probs, axis=-1) + jnp.sum(old_probs, axis=-1)
    weighted = jnp.einsum(
        "qhk,khd->qhd",
        new_probs.astype(jnp.bfloat16),
        new_values,
        preferred_element_type=jnp.float32,
    )
    weighted = weighted + jnp.einsum(
        "qhk,khd->qhd",
        old_probs.astype(jnp.bfloat16),
        cache_values,
        preferred_element_type=jnp.float32,
    )
    attended = (
        (weighted / denominator[..., None])
        .astype(jnp.bfloat16)
        .reshape(tokens_here, heads_here * HD)
    )
    projected = jnp.dot(attended, w_out, preferred_element_type=jnp.float32)
    attn_share = lax.psum_scatter(projected, "grp", scatter_dimension=1, tiled=True)
    after_cols = (resid.astype(jnp.float32) + attn_share).astype(jnp.bfloat16)
    after_wide = after_cols.astype(jnp.float32)
    squares = lax.psum(jnp.sum(after_wide * after_wide, axis=1), "grp")
    inverse = lax.rsqrt(squares / D + EPS)
    gain_cols = lax.dynamic_slice_in_dim(norm_gain, column_start, column_width, 0)
    normed_cols = (after_wide * inverse[:, None] * gain_cols.astype(jnp.float32)[None, :]).astype(
        jnp.bfloat16
    )
    router_cols = lax.dynamic_slice_in_dim(w_router, column_start, column_width, 0)
    logits = lax.psum(jnp.dot(normed_cols, router_cols, preferred_element_type=jnp.float32), "grp")
    normed_full = lax.all_gather(normed_cols, "grp", axis=1, tiled=True)
    route_hits = routes[:, :, None] == jnp.arange(experts_all, dtype=jnp.int32)[None, None, :]
    chosen = jnp.sum(jnp.where(route_hits, logits[:, None, :], 0.0), axis=-1)
    route_weight = jax.nn.softmax(chosen, axis=-1).astype(jnp.bfloat16)
    flat_hits = route_hits.reshape(tokens_here * TOP, experts_all).astype(jnp.int32)
    earlier = jnp.cumsum(flat_hits, axis=0) - flat_hits
    slot_index = jnp.sum(earlier * flat_hits, axis=1)
    slot_row = (routes.reshape(-1) * capacity + slot_index).reshape(tokens_here, TOP)
    slot_ids = jnp.arange(experts_all * capacity, dtype=jnp.int32)
    matches = slot_row[:, :, None] == slot_ids[None, None, :]
    selection = jnp.any(matches, axis=1).astype(jnp.bfloat16)
    combine = jnp.sum(
        jnp.where(matches, route_weight[:, :, None], jnp.zeros((), jnp.bfloat16)), axis=1
    )
    outgoing = jnp.einsum(
        "tj,td->jd", selection, normed_full, preferred_element_type=jnp.float32
    ).astype(jnp.bfloat16)
    outgoing = outgoing.reshape(experts_all, capacity, D)
    returned = send_back(
        expert_rows(
            lax.all_to_all(outgoing, "ep", split_axis=0, concat_axis=0, tiled=True),
            w_gate_up,
            w_down,
        )
    )
    mixed_part = jnp.dot(
        combine, returned.reshape(experts_all * capacity, D), preferred_element_type=jnp.float32
    )
    mixed_cols = lax.psum_scatter(mixed_part, "grp", scatter_dimension=1, tiled=True)
    return (after_cols, mixed_cols.astype(jnp.bfloat16))


def solution(mesh):
    return jax.shard_map(
        body,
        mesh=mesh,
        in_specs=(
            P("ep", "grp"),
            P("ep", "grp"),
            P("ep", "grp"),
            P("ep", "grp"),
            P(None, "ep", "grp"),
            P(),
            P("grp", None),
            P(),
            P(),
            P("ep", None),
            P("ep", None, None, "grp"),
            P("ep", "grp", None),
        ),
        out_specs=(P("ep", "grp"), P("ep", "grp")),
        check_vma=False,
    )
```

profile of v0, /device:TPU:7, one launch (start us, length us, event | category | flops | bytes accessed | tf_op | source)
XLA Modules:
  0.0 401.0 jit_solution(10585007642774497526)
XLA Ops:
  7.3 1.3 dynamic_slice.10
  8.6 0.6 iota_compare_fusion.5
  9.3 1.3 fusion.52
  10.5 0.2 copy.72
  10.8 1.3 fusion.54
  12.1 0.2 fusion.53
  12.3 0.2 fusion.11
  12.6 0.2 fusion.38
  12.8 0.2 copy.62
  13.0 0.3 fusion.9
  13.3 1.3 fusion.55
  15.1 1.2 reduce-window.6
  16.3 0.2 slice_reduce_fusion
  16.8 0.8 dynamic-slice_convert_fusion
  17.6 0.4 fusion
  18.0 37.9 %reduce-scatter.3.cloned.1.call-done = f32[128,256]{1,0:T(8,128)} async-done(((f32[128,2048]{1,0:T(8,128)}), f32[128,256]{1,0:T(8,128)}) %reduce-scatter.3.cloned.1.call-update) | async-done | bytes 131088 | tf_op jit(solution)/shard_map/reduce_scatter | solution.py:96
  55.9 1.0 fusion.29
  56.9 11.9 %psum.14 = f32[128]{0:T(128)S(1)} all-reduce(f32[128]{0:T(128)S(1)} %get-tuple-element.2), channel_id=1, replica_groups=mesh['grp'=8,'ep'=64] {'grp'}, use_global_device_ids=true, to_apply=%region_9.10 | all-reduce | flops 128 | bytes 1024 | tf_op jit(solution)/shard_map/psum | solution.py:99
  68.9 13.8 %all_gather.3 = bf16[128,2048]{1,0:T(8,128)(2,1)S(1)} all-gather(bf16[128,256]{1,0:T(8,128)(2,1)S(1)} %fusion.31), channel_id=1, replica_groups=mesh['grp'=8,'ep'=64] {'grp'}, dimensions={1}, use_global_device_ids=true | all-gather | bytes 589824 | tf_op jit(solution)/shard_map/all_gather | solution.py:107
  82.6 1.3 convolution_convert_fusion.1
  84.0 108.1 %all_to_all.10 = bf16[64,16,2048]{2,1,0:T(8,128)(2,1)S(1)} all-to-all(bf16[64,16,2048]{2,1,0:T(8,128)(2,1)S(1)} %bitcast.87), channel_id=1, replica_groups=mesh['grp'=8,'ep'=64] {'ep'}, dimensions={0} | all-to-all | bytes 8388608 | tf_op jit(solution)/shard_map/all_to_all | solution.py:127
  192.0 2.0 copy-done.1
  194.0 2.5 fusion.16
  196.5 7.0 %convolution_convert_fusion = bf16[1024,2048]{1,0:T(8,128)(2,1)} fusion(bf16[1024,2048]{1,0:T(8,128)(2,1)} %bitcast.90, bf16[1,176,2048]{2,1,0:T(8,128)(2,1)S(1)} %copy-done.8, bf16[1,2,2048,176]{2,3,1,0:T(8,128)(2,1)S(1)} %copy-done.7, f32[1024,176]{0,1:T(8,128)} %fusion.16), kind=kOutput, calls=%fused_computation | convolution fusion | flops 1479573504 | bytes 10551296 | tf_op jit(solution)/shard_map/dot_general | solution.py:21
  203.5 14.2 %all-to-all-start.1 = ((bf16[64,16,2048]{2,1,0:T(8,128)(2,1)}), bf16[64,16,2048]{2,1,0:T(8,128)(2,1)}, u32[]{:S(2)}, u32[]{:S(2)}) async-start(bf16[64,16,2048]{2,1,0:T(8,128)(2,1)} %bitcast.88), calls=%async_computation.2 | async-start | bytes 8388608 | tf_op jit(solution)/shard_map/all_to_all | solution.py:28
  217.8 0.9 fusion.47
  218.7 25.3 %psum.15 = f32[128,64]{0,1:T(8,128)S(1)} all-reduce(f32[128,64]{0,1:T(8,128)S(1)} %fusion.47), channel_id=1, replica_groups=mesh['grp'=8,'ep'=64] {'grp'}, use_global_device_ids=true, to_apply=%region_10.11 | all-reduce | flops 8192 | bytes 65536 | tf_op jit(solution)/shard_map/psum | solution.py:106
  244.1 0.3 fusion.10
  244.4 76.0 %all-to-all-done.1 = bf16[64,16,2048]{2,1,0:T(8,128)(2,1)} async-done(((bf16[64,16,2048]{2,1,0:T(8,128)(2,1)}), bf16[64,16,2048]{2,1,0:T(8,128)(2,1)}, u32[]{:S(2)}, u32[]{:S(2)}) %all-to-all-start.1) | async-done | bytes 4194336 | tf_op jit(solution)/shard_map/all_to_all | solution.py:28
  320.4 3.9 fusion.56
  324.3 68.3 %reduce-scatter.5.cloned.1.call-done = f32[128,256]{1,0:T(8,128)} async-done(((f32[128,2048]{1,0:T(8,128)}), f32[128,256]{1,0:T(8,128)}) %reduce-scatter.5.cloned.1.call-update) | async-done | bytes 131088 | tf_op jit(solution)/shard_map/reduce_scatter | solution.py:135
  392.6 1.5 convert_element_type.67
  (44 shorter events, 1.2 us)
Async XLA Ops:
  7.2 6.2 %copy-start = (bf16[256,2048]{1,0:T(8,128)(2,1)S(1)}, bf16[256,2048]{1,0:T(8,128)(2,1)}, u32[]{:S(2)}) copy-start(bf16[256,2048]{1,0:T(8,128)(2,1)} %param.18) | copy-start | bytes 3145732
  7.2 4.8 %copy-start.3 = (bf16[128,256]{1,0:T(8,128)(2,1)S(1)}, bf16[128,256]{1,0:T(8,128)(2,1)}, u32[]{:S(2)}) copy-start(bf16[128,256]{1,0:T(8,128)(2,1)} %param.13) | copy-start | bytes 196612
  7.2 4.8 %copy-start.9 = (bf16[128,256]{1,0:T(8,128)(2,1)S(1)}, bf16[128,256]{1,0:T(8,128)(2,1)}, u32[]{:S(2)}) copy-start(bf16[128,256]{1,0:T(8,128)(2,1)} %param.14) | copy-start | bytes 196612
  7.2 5.3 %copy-start.4 = (bf16[128,256]{1,0:T(8,128)(2,1)S(1)}, bf16[128,256]{1,0:T(8,128)(2,1)}, u32[]{:S(2)}) copy-start(bf16[128,256]{1,0:T(8,128)(2,1)} %param.15) | copy-start | bytes 196612
  7.2 48.7 %reduce-scatter.3.cloned.1.call-start = ((), (), s32[]{:S(2)}) async-start(), calls=%async_computation.4 | async-start | bytes 1179648 | tf_op jit(solution)/shard_map/reduce_scatter | solution.py:96
  12.0 2.7 copy-start.6
  12.2 43.6 %copy-start.5 = (bf16[128,256]{1,0:T(8,128)(2,1)S(1)}, bf16[128,256]{1,0:T(8,128)(2,1)}, u32[]{:S(2)}) copy-start(bf16[128,256]{1,0:T(8,128)(2,1)} %param.12) | copy-start | bytes 196612
  56.9 27.1 %copy-start.2 = (bf16[128,256]{1,0:T(8,128)(2,1)}, bf16[128,256]{1,0:T(8,128)(2,1)S(1)}, u32[]{:S(2)}) copy-start(bf16[128,256]{1,0:T(8,128)(2,1)S(1)} %get-tuple-element.3) | copy-start | bytes 196612
  84.0 110.1 %copy-start.7 = (bf16[1,2,2048,176]{2,3,1,0:T(8,128)(2,1)S(1)}, bf16[1,2,2048,176]{2,3,1,0:T(8,128)(2,1)}, u32[]{:S(2)}) copy-start(bf16[1,2,2048,176]{2,3,1,0:T(8,128)(2,1)} %param.22) | copy-start | bytes 4325380
  192.0 2.0 copy-start.1
  192.0 4.4 %copy-start.8 = (bf16[1,176,2048]{2,1,0:T(8,128)(2,1)S(1)}, bf16[1,176,2048]{2,1,0:T(8,128)(2,1)}, u32[]{:S(2)}) copy-start(bf16[1,176,2048]{2,1,0:T(8,128)(2,1)} %param.23) | copy-start | bytes 2162692
  203.5 116.8 %all-to-all-start.1 = ((bf16[64,16,2048]{2,1,0:T(8,128)(2,1)}), bf16[64,16,2048]{2,1,0:T(8,128)(2,1)}, u32[]{:S(2)}, u32[]{:S(2)}) async-start(bf16[64,16,2048]{2,1,0:T(8,128)(2,1)} %bitcast.88), calls=%async_computation.2 | async-start | bytes 8388608 | tf_op jit(solution)/shard_map/all_to_all | solution.py:28
  217.7 174.9 %reduce-scatter.5.cloned.1.call-start = ((), (), s32[]{:S(2)}) async-start(), calls=%async_computation.5 | async-start | bytes 1179648 | tf_op jit(solution)/shard_map/reduce_scatter | solution.py:135
Sparse Core Ops, SparseCore 0:
  14.8 41.0 reduce-scatter.2
  324.4 68.1 reduce-scatter.4
where the time goes:
time: 402 us; the launch traced here: 401 us
  waiting for transfers between devices  182 us (45%)
  blocking collectives  159 us (40%)
  matrix products  18.9 us (5%)
  starting transfers between devices  14.3 us (4%)
  between operations  14.3 us (4%)
  other arithmetic  6.45 us (2%)
  local copies, waits for them, and re-layouts  5.87 us (1%)
    all_to_all x1, blocking collectives, body(): lax.all_to_all(outgoing, 'ep', split_axis=0, concat_axis=0, tiled=True)  108 us
    all_to_all x1, waiting for transfers between devices, send_back(): lax.all_to_all(answered, 'ep', split_axis=0, concat_axis=0, tiled=True)  76 us
    reduce_scatter x1, waiting for transfers between devices, body(): lax.psum_scatter(mixed_part, 'grp', scatter_dimension=1, tiled=True)  68.3 us
    reduce_scatter x1, waiting for transfers between devices, body(): lax.psum_scatter(projected, 'grp', scatter_dimension=1, tiled=True)  37.9 us
    psum x1, blocking collectives, body(): lax.psum(jnp.dot(normed_cols, router_cols, preferred_element_type=jnp.flo...  25.3 us
    all_to_all x1, starting transfers between devices, send_back(): lax.all_to_all(answered, 'ep', split_axis=0, concat_axis=0, tiled=True)  14.2 us
    all_gather x1, blocking collectives, body(): normed_full = lax.all_gather(normed_cols, 'grp', axis=1, tiled=True)  13.8 us
    psum x1, blocking collectives, body(): squares = lax.psum(jnp.sum(after_wide * after_wide, axis=1), 'grp')  11.9 us
  transfers between devices with their start and end apart: 3, of which 3 were waited for; matrix products, arithmetic and copies ran while one was open for 1% of the time, Pallas kernels for 0%

commit v1 on v0

--- a/solution.py
+++ b/solution.py
@@ -10,22 +10,6 @@
 
 EPS = 1e-06
 MASKED = -1e30
-
-
-def expert_rows(arrived, w_gate_up, w_down):
-    features = arrived.shape[-1]
-    flat_rows = arrived.reshape(-1, features)
-    gate_value = jnp.dot(flat_rows, w_gate_up[0, 0], preferred_element_type=jnp.float32)
-    up_value = jnp.dot(flat_rows, w_gate_up[0, 1], preferred_element_type=jnp.float32)
-    hidden = (jax.nn.silu(gate_value) * up_value).astype(jnp.bfloat16)
-    partial_value = jnp.dot(hidden, w_down[0], preferred_element_type=jnp.float32).astype(
-        jnp.bfloat16
-    )
-    return partial_value.reshape(arrived.shape)
-
-
-def send_back(answered):
-    return lax.all_to_all(answered, "ep", split_axis=0, concat_axis=0, tiled=True)
 
 
 def body(
@@ -95,16 +79,15 @@
     projected = jnp.dot(attended, w_out, preferred_element_type=jnp.float32)
     attn_share = lax.psum_scatter(projected, "grp", scatter_dimension=1, tiled=True)
     after_cols = (resid.astype(jnp.float32) + attn_share).astype(jnp.bfloat16)
-    after_wide = after_cols.astype(jnp.float32)
-    squares = lax.psum(jnp.sum(after_wide * after_wide, axis=1), "grp")
+    after_full = lax.all_gather(after_cols, "grp", axis=1, tiled=True)
+    after_wide = after_full.astype(jnp.float32)
+    squares = jnp.sum(after_wide * after_wide, axis=1)
     inverse = lax.rsqrt(squares / D + EPS)
-    gain_cols = lax.dynamic_slice_in_dim(norm_gain, column_start, column_width, 0)
-    normed_cols = (after_wide * inverse[:, None] * gain_cols.astype(jnp.float32)[None, :]).astype(
-        jnp.bfloat16
-    )
-    router_cols = lax.dynamic_slice_in_dim(w_router, column_start, column_width, 0)
-    logits = lax.psum(jnp.dot(normed_cols, router_cols, preferred_element_type=jnp.float32), "grp")
-    normed_full = lax.all_gather(normed_cols, "grp", axis=1, tiled=True)
+    normed_full = (
+        after_wide * inverse[:, None] * norm_gain.astype(jnp.float32)[None, :]
+    ).astype(jnp.bfloat16)
+    normed_cols = lax.dynamic_slice_in_dim(normed_full, column_start, column_width, 1)
+    logits = jnp.dot(normed_full, w_router, preferred_element_type=jnp.float32)
     route_hits = routes[:, :, None] == jnp.arange(experts_all, dtype=jnp.int32)[None, None, :]
     chosen = jnp.sum(jnp.where(route_hits, logits[:, None, :], 0.0), axis=-1)
     route_weight = jax.nn.softmax(chosen, axis=-1).astype(jnp.bfloat16)
@@ -116,23 +99,37 @@
     matches = slot_row[:, :, None] == slot_ids[None, None, :]
     selection = jnp.any(matches, axis=1).astype(jnp.bfloat16)
     combine = jnp.sum(
-        jnp.where(matches, route_weight[:, :, None], jnp.zeros((), jnp.bfloat16)), axis=1
+        jnp.where(matches, route_weight[:, :, None].astype(jnp.float32), 0.0), axis=1
     )
     outgoing = jnp.einsum(
-        "tj,td->jd", selection, normed_full, preferred_element_type=jnp.float32
+        "tj,td->jd", selection, normed_cols, preferred_element_type=jnp.float32
     ).astype(jnp.bfloat16)
-    outgoing = outgoing.reshape(experts_all, capacity, D)
-    returned = send_back(
-        expert_rows(
-            lax.all_to_all(outgoing, "ep", split_axis=0, concat_axis=0, tiled=True),
-            w_gate_up,
-            w_down,
-        )
+    outgoing = outgoing.reshape(experts_all, capacity, column_width)
+    arrived = lax.all_to_all(outgoing, "ep", split_axis=0, concat_axis=0, tiled=True)
+    arrived = arrived.reshape(experts_all * capacity, column_width)
+    groups = lax.axis_size("grp")
+    gathered = lax.all_gather(arrived, "grp", axis=0, tiled=False)
+    slice_width = w_gate_up.shape[-1]
+    gate_up = w_gate_up[0].reshape(2, groups, column_width, slice_width)
+    gate_value = jnp.einsum(
+        "gnc,gch->nh", gathered, gate_up[0], preferred_element_type=jnp.float32
     )
-    mixed_part = jnp.dot(
-        combine, returned.reshape(experts_all * capacity, D), preferred_element_type=jnp.float32
+    up_value = jnp.einsum("gnc,gch->nh", gathered, gate_up[1], preferred_element_type=jnp.float32)
+    hidden = (jax.nn.silu(gate_value) * up_value).astype(jnp.bfloat16)
+    down = w_down[0].reshape(slice_width, groups, column_width)
+    slice_out = jnp.einsum(
+        "nh,hgc->gnc", hidden, down, preferred_element_type=jnp.float32
+    ).astype(jnp.bfloat16)
+    slices_here = lax.all_to_all(slice_out, "grp", split_axis=0, concat_axis=0, tiled=True)
+    expert_out = jnp.sum(slices_here.astype(jnp.float32), axis=0)
+    expert_out = expert_out.reshape(experts_all, capacity, column_width)
+    returned = lax.all_to_all(expert_out, "ep", split_axis=0, concat_axis=0, tiled=True)
+    mixed_cols = jnp.dot(
+        combine,
+        returned.reshape(experts_all * capacity, column_width),
+        precision=lax.Precision.HIGHEST,
+        preferred_element_type=jnp.float32,
     )
-    mixed_cols = lax.psum_scatter(mixed_part, "grp", scatter_dimension=1, tiled=True)
     return (after_cols, mixed_cols.astype(jnp.bfloat16))
 
 

time: 402 us -> 252 us (0.63)
  waiting for transfers between devices: 182 us -> 93.5 us
  blocking collectives: 159 us -> 96.1 us
    all_to_all x1, blocking collectives: 108 us -> 30.7 us  [body(): lax.all_to_all(outgoing, 'ep', split_axis=0, concat_axis=0, tiled=True)]
    reduce_scatter x1 -> x0, waiting for transfers between devices: 68.3 us -> none  [body(): lax.psum_scatter(mixed_part, 'grp', scatter_dimension=1, tiled=True)]
    all_to_all x0 -> x1, blocking collectives: none -> 53.4 us  [body(): lax.all_to_all(slice_out, 'grp', split_axis=0, concat_axis=0, tiled=True)]
    all_to_all x1, waiting for transfers between devices: 76 us -> 26.1 us  [body(): lax.all_to_all(expert_out, 'ep', split_axis=0, concat_axis=0, tiled=True)]
    psum x2 -> x0, blocking collectives: 37.2 us -> none  [the longest x1 25.3 us: body(): lax.psum(jnp.dot(normed_cols, router_cols, preferred_element_type=jnp.flo...]
    all_gather x0 -> x1, waiting for transfers between devices: none -> 28.8 us  [body(): gathered = lax.all_gather(arrived, 'grp', axis=0, tiled=False)]
  transfers between devices with their start and end apart: 3 -> 3, of which waited for: 3 -> 3; matrix products, arithmetic and copies ran while one was open for 1% -> 3% of each run, Pallas kernels for 0% -> 0%
where the time goes in v1:
time: 252 us; the launch traced here: 247 us
  blocking collectives  96.1 us (38%)
  waiting for transfers between devices  93.5 us (37%)
  matrix products  16.2 us (6%)
  between operations  14.3 us (6%)
  starting transfers between devices  13.1 us (5%)
  local copies, waits for them, and re-layouts  8.21 us (3%)
  other arithmetic  5.93 us (2%)
    all_to_all x1, blocking collectives, body(): lax.all_to_all(slice_out, 'grp', split_axis=0, concat_axis=0, tiled=True)  53.4 us
    reduce_scatter x1, waiting for transfers between devices, body(): lax.psum_scatter(projected, 'grp', scatter_dimension=1, tiled=True)  38.5 us
    all_to_all x1, blocking collectives, body(): lax.all_to_all(outgoing, 'ep', split_axis=0, concat_axis=0, tiled=True)  30.7 us
    all_gather x1, waiting for transfers between devices, body(): gathered = lax.all_gather(arrived, 'grp', axis=0, tiled=False)  28.8 us
    all_to_all x1, waiting for transfers between devices, body(): lax.all_to_all(expert_out, 'ep', split_axis=0, concat_axis=0, tiled=True)  26.1 us
    all_to_all x1, starting transfers between devices, body(): lax.all_to_all(expert_out, 'ep', split_axis=0, concat_axis=0, tiled=True)  13 us
    all_gather x1, blocking collectives, body(): after_full = lax.all_gather(after_cols, 'grp', axis=1, tiled=True)  12 us
    dot_general x1, matrix products, body(): jnp.einsum('nh,hgc->gnc', hidden, down, preferred_element_type=jnp.float32)  7.06 us
  transfers between devices with their start and end apart: 3, of which 3 were waited for; matrix products, arithmetic and copies ran while one was open for 3% of the time, Pallas kernels for 0%

profile of v1, /device:TPU:7, one launch (start us, length us, event | category | flops | bytes accessed | tf_op | source)
XLA Modules:
  0.0 247.3 jit_solution(18026099072781676729)
XLA Ops:
  7.3 1.3 dynamic_slice.7
  8.6 0.6 iota_compare_fusion.5
  9.3 1.0 copy.117
  10.2 1.3 fusion.49
  11.5 0.2 copy.105
  11.7 0.2 copy.118
  11.9 0.2 fusion.50
  12.1 0.4 fusion.51
  13.0 0.3 fusion.10
  13.3 1.3 fusion.52
  15.1 1.2 reduce-window.6
  16.3 0.2 slice_reduce_fusion
  16.9 0.4 fusion
  17.3 38.5 %reduce-scatter.2.cloned.1.call-done = f32[128,256]{1,0:T(8,128)} async-done(((f32[128,2048]{1,0:T(8,128)}), f32[128,256]{1,0:T(8,128)}) %reduce-scatter.2.cloned.1.call-update) | async-done | bytes 131088 | tf_op jit(solution)/shard_map/reduce_scatter | solution.py:80
  55.9 0.9 add_convert_fusion
  56.8 12.0 %all_gather.6 = bf16[128,2048]{1,0:T(8,128)(2,1)S(1)} all-gather(bf16[128,256]{1,0:T(8,128)(2,1)S(1)} %add_convert_fusion), channel_id=1, replica_groups=mesh['grp'=8,'ep'=64] {'grp'}, dimensions={1}, use_global_device_ids=true | all-gather | bytes 589824 | tf_op jit(solution)/shard_map/all_gather | solution.py:82
  68.8 0.2 fusion.11
  68.9 0.2 fusion.13
  69.2 0.4 convolution_convert_fusion
  69.5 30.7 %all_to_all.15 = bf16[64,16,256]{2,1,0:T(8,128)(2,1)} all-to-all(bf16[64,16,256]{2,1,0:T(8,128)(2,1)S(1)} %bitcast.115), channel_id=1, replica_groups=mesh['grp'=8,'ep'=64] {'ep'}, dimensions={0} | all-to-all | bytes 1048576 | tf_op jit(solution)/shard_map/all_to_all | solution.py:108
  100.2 2.2 copy.124
  102.5 1.0 copy.122
  103.7 28.8 %all-gather.2.cloned.1.call-done = bf16[8,1024,256]{2,1,0:T(8,128)(2,1)} async-done(((bf16[1,1024,256]{2,1,0:T(8,128)(2,1)}), bf16[8,1024,256]{2,1,0:T(8,128)(2,1)}) %all-gather.2.cloned.1.call-update) | async-done | bytes 4194320 | tf_op jit(solution)/shard_map/all_gather | solution.py:111
  132.5 4.8 %convolution_bitcast_fusion.1 = f32[1024,176]{0,1:T(8,128)} fusion(bf16[8,1024,256]{2,1,0:T(8,128)(2,1)} %all-gather.2.cloned.1.call-done, bf16[8,256,176]{1,0,2:T(8,128)(2,1)} %bitcast.120), kind=kOutput, calls=%fused_computation.12 | convolution fusion | flops 738197504 | bytes 5636096 | tf_op jit(solution)/shard_map/gnc,gch->nh/dot_general | solution.py:114
  137.4 7.1 %convert_bitcast_fusion = bf16[8,1024,256]{2,1,0:T(8,128)(2,1)} fusion(bf16[8,1024,256]{2,1,0:T(8,128)(2,1)} %all-gather.2.cloned.1.call-done, bf16[176,8,256]{2,1,0:T(8,128)(2,1)S(1)} %bitcast.118, bf16[8,256,176]{1,0,2:T(8,128)(2,1)S(1)} %bitcast.119, f32[1024,176]{0,1:T(8,128)} %convolution_bitcast_fusion.1), kind=kOutput, calls=%fused_computation.1 | convolution fusion | flops 1479573504 | bytes 10551296 | tf_op jit(solution)/shard_map/nh,hgc->gnc/dot_general | solution.py:120
  144.4 53.4 %all_to_all.16 = bf16[8,1024,256]{2,1,0:T(8,128)(2,1)S(1)} all-to-all(bf16[8,1024,256]{2,1,0:T(8,128)(2,1)} %convert_bitcast_fusion), channel_id=1, replica_groups=mesh['grp'=8,'ep'=64] {'grp'}, dimensions={0} | all-to-all | bytes 8388608 | tf_op jit(solution)/shard_map/all_to_all | solution.py:123
  197.8 1.6 convert_reduce_fusion
  199.4 13.0 %all-to-all-start.2 = ((f32[64,16,256]{2,1,0:T(8,128)}), f32[64,16,256]{2,1,0:T(8,128)S(1)}, u32[]{:S(2)}, u32[]{:S(2)}) async-start(f32[64,16,256]{2,1,0:T(8,128)} %bitcast.15), calls=%async_computation.3 | async-start | bytes 2097152 | tf_op jit(solution)/shard_map/all_to_all | solution.py:126
  212.4 0.3 fusion.53
  212.8 0.3 select_reduce_fusion
  213.1 26.1 %all-to-all-done.2 = f32[64,16,256]{2,1,0:T(8,128)S(1)} async-done(((f32[64,16,256]{2,1,0:T(8,128)}), f32[64,16,256]{2,1,0:T(8,128)S(1)}, u32[]{:S(2)}, u32[]{:S(2)}) %all-to-all-start.2) | async-done | bytes 1048608 | tf_op jit(solution)/shard_map/all_to_all | solution.py:126
  239.2 1.3 convolution_convert_fusion.1
  (48 shorter events, 1.6 us)
Async XLA Ops:
  7.2 6.1 %copy-start = (bf16[256,2048]{1,0:T(8,128)(2,1)S(1)}, bf16[256,2048]{1,0:T(8,128)(2,1)}, u32[]{:S(2)}) copy-start(bf16[256,2048]{1,0:T(8,128)(2,1)} %param.18) | copy-start | bytes 3145732
  7.2 4.7 %copy-start.5 = (bf16[128,256]{1,0:T(8,128)(2,1)S(1)}, bf16[128,256]{1,0:T(8,128)(2,1)}, u32[]{:S(2)}) copy-start(bf16[128,256]{1,0:T(8,128)(2,1)} %param.13) | copy-start | bytes 196612
  7.2 4.7 %copy-start.9 = (bf16[128,256]{1,0:T(8,128)(2,1)S(1)}, bf16[128,256]{1,0:T(8,128)(2,1)}, u32[]{:S(2)}) copy-start(bf16[128,256]{1,0:T(8,128)(2,1)} %param.14) | copy-start | bytes 196612
  7.2 48.6 %reduce-scatter.2.cloned.1.call-start = ((), (), s32[]{:S(2)}) async-start(), calls=%async_computation.4 | async-start | bytes 1179648 | tf_op jit(solution)/shard_map/reduce_scatter | solution.py:80
  11.9 2.8 %copy-start.7 = (s32[128,4]{0,1:T(4,128)S(1)}, s32[128,4]{0,1:T(4,128)}, u32[]{:S(2)}) copy-start(s32[128,4]{0,1:T(4,128)} %param.21) | copy-start | bytes 6148
  12.1 2.9 %copy-start.8 = (bf16[2048]{0:T(1024)(128)(2,1)S(1)}, bf16[2048]{0:T(1024)(128)(2,1)}, u32[]{:S(2)}) copy-start(bf16[2048]{0:T(1024)(128)(2,1)} %param.19) | copy-start | bytes 12292
  12.6 43.3 %copy-start.6 = (bf16[128,256]{1,0:T(8,128)(2,1)S(1)}, bf16[128,256]{1,0:T(8,128)(2,1)}, u32[]{:S(2)}) copy-start(bf16[128,256]{1,0:T(8,128)(2,1)} %param.12) | copy-start | bytes 196612
  14.6 87.7 %copy-start.1 = (bf16[1,2,2048,176]{2,3,1,0:T(8,128)(2,1)S(1)}, bf16[1,2,2048,176]{2,3,1,0:T(8,128)(2,1)}, u32[]{:S(2)}) copy-start(bf16[1,2,2048,176]{2,3,1,0:T(8,128)(2,1)} %param.22) | copy-start | bytes 4325380
  14.7 117.9 %all-gather.2.cloned.1.call-start = ((), (), s32[]{:S(2)}) async-start(), calls=%async_computation.5 | async-start | bytes 4718592 | tf_op jit(solution)/shard_map/all_gather | solution.py:111
  56.8 45.7 %copy-start.4 = (bf16[128,256]{1,0:T(8,128)(2,1)}, bf16[128,256]{1,0:T(8,128)(2,1)S(1)}, u32[]{:S(2)}) copy-start(bf16[128,256]{1,0:T(8,128)(2,1)S(1)} %add_convert_fusion) | copy-start | bytes 196612
  103.5 33.8 %copy-start.2 = (bf16[22,8,8,256]{3,2,1,0:T(8,128)(2,1)S(1)}, bf16[22,8,8,256]{3,2,1,0:T(8,128)(2,1)}, u32[]{:S(2)}) copy-start(bf16[22,8,8,256]{3,2,1,0:T(8,128)(2,1)} %copy.124) | copy-start | bytes 2162692
  197.8 14.6 %copy-start.3 = (bf16[2048,64]{0,1:T(8,128)(2,1)S(1)}, bf16[2048,64]{0,1:T(8,128)(2,1)}, u32[]{:S(2)}) copy-start(bf16[2048,64]{0,1:T(8,128)(2,1)} %param.20) | copy-start | bytes 786436
  199.4 39.8 %all-to-all-start.2 = ((f32[64,16,256]{2,1,0:T(8,128)}), f32[64,16,256]{2,1,0:T(8,128)S(1)}, u32[]{:S(2)}, u32[]{:S(2)}) async-start(f32[64,16,256]{2,1,0:T(8,128)} %bitcast.15), calls=%async_computation.3 | async-start | bytes 2097152 | tf_op jit(solution)/shard_map/all_to_all | solution.py:126
Sparse Core Ops, SparseCore 0:
  14.8 41.0 reduce-scatter.1
  100.3 32.1 all-gather.1

commit v2 on v1

--- a/solution.py
+++ b/solution.py
@@ -77,8 +77,10 @@
         .reshape(tokens_here, heads_here * HD)
     )
     projected = jnp.dot(attended, w_out, preferred_element_type=jnp.float32)
-    attn_share = lax.psum_scatter(projected, "grp", scatter_dimension=1, tiled=True)
-    after_cols = (resid.astype(jnp.float32) + attn_share).astype(jnp.bfloat16)
+    attn_share = lax.psum_scatter(
+        projected.astype(jnp.bfloat16), "grp", scatter_dimension=1, tiled=True
+    )
+    after_cols = (resid.astype(jnp.float32) + attn_share.astype(jnp.float32)).astype(jnp.bfloat16)
     after_full = lax.all_gather(after_cols, "grp", axis=1, tiled=True)
     after_wide = after_full.astype(jnp.float32)
     squares = jnp.sum(after_wide * after_wide, axis=1)
@@ -120,8 +122,7 @@
     slice_out = jnp.einsum(
         "nh,hgc->gnc", hidden, down, preferred_element_type=jnp.float32
     ).astype(jnp.bfloat16)
-    slices_here = lax.all_to_all(slice_out, "grp", split_axis=0, concat_axis=0, tiled=True)
-    expert_out = jnp.sum(slices_here.astype(jnp.float32), axis=0)
+    expert_out = lax.psum_scatter(slice_out, "grp", scatter_dimension=0, tiled=True)
     expert_out = expert_out.reshape(experts_all, capacity, column_width)
     returned = lax.all_to_all(expert_out, "ep", split_axis=0, concat_axis=0, tiled=True)
     mixed_cols = jnp.dot(

time: 252 us -> 226 us (0.90); the launches traced: 247 us -> 225 us
  blocking collectives: 96.1 us -> 42.5 us
  waiting for transfers between devices: 93.5 us -> 128 us
    all_to_all x1 -> x0, blocking collectives: 53.4 us -> none  [body(): lax.all_to_all(slice_out, 'grp', split_axis=0, concat_axis=0, tiled=True)]
    reduce_scatter x1 -> x2, waiting for transfers between devices: 38.5 us -> 81.6 us  [the longest x1 44 us: body(): lax.psum_scatter(slice_out, 'grp', scatter_dimension=0, tiled=True)]
    all_to_all x1, waiting for transfers between devices: 26.1 us -> 17.5 us  [body(): lax.all_to_all(expert_out, 'ep', split_axis=0, concat_axis=0, tiled=True)]
  transfers between devices with their start and end apart: 3 -> 4, of which waited for: 3 -> 4; matrix products, arithmetic and copies ran while one was open for 3% -> 3% of each run, Pallas kernels for 0% -> 0%
where the time goes in v2:
time: 226 us; the launch traced here: 225 us
  waiting for transfers between devices  128 us (57%)
  blocking collectives  42.5 us (19%)
  matrix products  15.8 us (7%)
  between operations  14 us (6%)
  starting transfers between devices  12.5 us (6%)
  local copies, waits for them, and re-layouts  8.21 us (4%)
  other arithmetic  4.3 us (2%)
    reduce_scatter x1, waiting for transfers between devices, body(): lax.psum_scatter(slice_out, 'grp', scatter_dimension=0, tiled=True)  44 us
    reduce_scatter x1, waiting for transfers between devices, body(): lax.psum_scatter(projected.astype(jnp.bfloat16), 'grp', scatter_dimension...  37.7 us
    all_to_all x1, blocking collectives, body(): lax.all_to_all(outgoing, 'ep', split_axis=0, concat_axis=0, tiled=True)  30.5 us
    all_gather x1, waiting for transfers between devices, body(): gathered = lax.all_gather(arrived, 'grp', axis=0, tiled=False)  28.8 us
    all_to_all x1, waiting for transfers between devices, body(): lax.all_to_all(expert_out, 'ep', split_axis=0, concat_axis=0, tiled=True)  17.5 us
    all_to_all x1, starting transfers between devices, body(): lax.all_to_all(expert_out, 'ep', split_axis=0, concat_axis=0, tiled=True)  12.4 us
    all_gather x1, blocking collectives, body(): after_full = lax.all_gather(after_cols, 'grp', axis=1, tiled=True)  12 us
    dot_general x1, matrix products, body(): jnp.einsum('nh,hgc->gnc', hidden, down, preferred_element_type=jnp.float32)  7.06 us
  transfers between devices with their start and end apart: 4, of which 4 were waited for; matrix products, arithmetic and copies ran while one was open for 3% of the time, Pallas kernels for 0%

profile of v2, /device:TPU:7, one launch (start us, length us, event | category | flops | bytes accessed | tf_op | source)
XLA Modules:
  0.0 225.3 jit_solution(5537671944007688496)
XLA Ops:
  7.3 1.3 dynamic_slice.7
  8.6 0.6 iota_compare_fusion.5
  9.3 1.0 copy.117
  10.2 1.3 fusion.49
  11.5 0.2 copy.105
  11.7 0.2 copy.118
  12.0 0.2 fusion.50
  12.2 0.4 fusion.51
  13.0 0.3 fusion.10
  13.3 1.1 convolution_convert_fusion
  14.9 1.2 reduce-window.6
  16.1 0.2 slice_reduce_fusion
  16.7 0.4 fusion
  17.1 37.7 %reduce-scatter.3.cloned.1.call-done = bf16[128,256]{1,0:T(8,128)(2,1)} async-done(((bf16[128,2048]{1,0:T(8,128)(2,1)}), bf16[128,256]{1,0:T(8,128)(2,1)}) %reduce-scatter.3.cloned.1.call-update) | async-done | bytes 65552 | tf_op jit(solution)/shard_map/reduce_scatter | solution.py:80
  54.8 0.9 add_convert_fusion
  55.6 12.0 %all_gather.6 = bf16[128,2048]{1,0:T(8,128)(2,1)S(1)} all-gather(bf16[128,256]{1,0:T(8,128)(2,1)S(1)} %add_convert_fusion), channel_id=1, replica_groups=mesh['grp'=8,'ep'=64] {'grp'}, dimensions={1}, use_global_device_ids=true | all-gather | bytes 589824 | tf_op jit(solution)/shard_map/all_gather | solution.py:84
  67.6 0.2 fusion.11
  67.8 0.2 fusion.13
  68.0 0.4 convolution_convert_fusion.1
  68.4 30.5 %all_to_all.10 = bf16[64,16,256]{2,1,0:T(8,128)(2,1)} all-to-all(bf16[64,16,256]{2,1,0:T(8,128)(2,1)S(1)} %bitcast.115), channel_id=1, replica_groups=mesh['grp'=8,'ep'=64] {'ep'}, dimensions={0} | all-to-all | bytes 1048576 | tf_op jit(solution)/shard_map/all_to_all | solution.py:110
  99.0 2.2 copy.124
  101.2 1.0 copy.122
  102.3 0.2 copy.123
  102.5 28.8 %all-gather.2.cloned.1.call-done = bf16[8,1024,256]{2,1,0:T(8,128)(2,1)} async-done(((bf16[1,1024,256]{2,1,0:T(8,128)(2,1)}), bf16[8,1024,256]{2,1,0:T(8,128)(2,1)}) %all-gather.2.cloned.1.call-update) | async-done | bytes 4194320 | tf_op jit(solution)/shard_map/all_gather | solution.py:113
  131.3 4.8 %convolution_bitcast_fusion.1 = f32[1024,176]{0,1:T(8,128)} fusion(bf16[8,1024,256]{2,1,0:T(8,128)(2,1)} %all-gather.2.cloned.1.call-done, bf16[8,256,176]{1,0,2:T(8,128)(2,1)} %bitcast.120), kind=kOutput, calls=%fused_computation.12 | convolution fusion | flops 738197504 | bytes 5636096 | tf_op jit(solution)/shard_map/gnc,gch->nh/dot_general | solution.py:116
  136.1 7.1 %convert_bitcast_fusion = bf16[8,1024,256]{2,1,0:T(8,128)(2,1)} fusion(bf16[8,1024,256]{2,1,0:T(8,128)(2,1)} %all-gather.2.cloned.1.call-done, bf16[176,8,256]{2,1,0:T(8,128)(2,1)S(1)} %bitcast.118, bf16[8,256,176]{1,0,2:T(8,128)(2,1)S(1)} %bitcast.119, f32[1024,176]{0,1:T(8,128)} %convolution_bitcast_fusion.1), kind=kOutput, calls=%fused_computation | convolution fusion | flops 1479573504 | bytes 10551296 | tf_op jit(solution)/shard_map/nh,hgc->gnc/dot_general | solution.py:122
  143.2 44.0 %reduce-scatter.5.cloned.1.call-done = bf16[1,1024,256]{2,1,0:T(8,128)(2,1)} async-done(((bf16[8,1024,256]{2,1,0:T(8,128)(2,1)}), bf16[1,1024,256]{2,1,0:T(8,128)(2,1)}) %reduce-scatter.5.cloned.1.call-update) | async-done | bytes 524304 | tf_op jit(solution)/shard_map/reduce_scatter | solution.py:125
  187.1 12.4 %all-to-all-start.1 = ((bf16[64,16,256]{2,1,0:T(8,128)(2,1)}), bf16[64,16,256]{2,1,0:T(8,128)(2,1)S(1)}, u32[]{:S(2)}, u32[]{:S(2)}) async-start(bf16[64,16,256]{2,1,0:T(8,128)(2,1)} %bitcast.121), calls=%async_computation.3 | async-start | bytes 1048576 | tf_op jit(solution)/shard_map/all_to_all | solution.py:127
  199.5 0.3 fusion.52
  199.9 0.3 select_reduce_fusion
  200.2 17.5 %all-to-all-done.1 = bf16[64,16,256]{2,1,0:T(8,128)(2,1)S(1)} async-done(((bf16[64,16,256]{2,1,0:T(8,128)(2,1)}), bf16[64,16,256]{2,1,0:T(8,128)(2,1)S(1)}, u32[]{:S(2)}, u32[]{:S(2)}) %all-to-all-start.1) | async-done | bytes 524320 | tf_op jit(solution)/shard_map/all_to_all | solution.py:127
  217.7 1.0 convolution_convert_fusion.2
  (49 shorter events, 1.5 us)
Async XLA Ops:
  7.2 6.1 %copy-start = (bf16[256,2048]{1,0:T(8,128)(2,1)S(1)}, bf16[256,2048]{1,0:T(8,128)(2,1)}, u32[]{:S(2)}) copy-start(bf16[256,2048]{1,0:T(8,128)(2,1)} %param.18) | copy-start | bytes 3145732
  7.2 4.8 %copy-start.5 = (bf16[128,256]{1,0:T(8,128)(2,1)S(1)}, bf16[128,256]{1,0:T(8,128)(2,1)}, u32[]{:S(2)}) copy-start(bf16[128,256]{1,0:T(8,128)(2,1)} %param.13) | copy-start | bytes 196612
  7.2 4.8 %copy-start.9 = (bf16[128,256]{1,0:T(8,128)(2,1)S(1)}, bf16[128,256]{1,0:T(8,128)(2,1)}, u32[]{:S(2)}) copy-start(bf16[128,256]{1,0:T(8,128)(2,1)} %param.14) | copy-start | bytes 196612
  7.2 47.6 %reduce-scatter.3.cloned.1.call-start = ((), (), s32[]{:S(2)}) async-start(), calls=%async_computation.4 | async-start | bytes 589824 | tf_op jit(solution)/shard_map/reduce_scatter | solution.py:80
  11.7 2.8 %copy-start.7 = (s32[128,4]{0,1:T(4,128)S(1)}, s32[128,4]{0,1:T(4,128)}, u32[]{:S(2)}) copy-start(s32[128,4]{0,1:T(4,128)} %param.21) | copy-start | bytes 6148
  11.7 3.2 %copy-start.8 = (bf16[2048]{0:T(1024)(128)(2,1)S(1)}, bf16[2048]{0:T(1024)(128)(2,1)}, u32[]{:S(2)}) copy-start(bf16[2048]{0:T(1024)(128)(2,1)} %param.19) | copy-start | bytes 12292
  12.1 42.6 %copy-start.6 = (bf16[128,256]{1,0:T(8,128)(2,1)S(1)}, bf16[128,256]{1,0:T(8,128)(2,1)}, u32[]{:S(2)}) copy-start(bf16[128,256]{1,0:T(8,128)(2,1)} %param.12) | copy-start | bytes 196612
  14.4 86.7 %copy-start.1 = (bf16[1,2,2048,176]{2,3,1,0:T(8,128)(2,1)S(1)}, bf16[1,2,2048,176]{2,3,1,0:T(8,128)(2,1)}, u32[]{:S(2)}) copy-start(bf16[1,2,2048,176]{2,3,1,0:T(8,128)(2,1)} %param.22) | copy-start | bytes 4325380
  14.5 116.8 %all-gather.2.cloned.1.call-start = ((), (), s32[]{:S(2)}) async-start(), calls=%async_computation.5 | async-start | bytes 4718592 | tf_op jit(solution)/shard_map/all_gather | solution.py:113
  55.6 45.6 %copy-start.4 = (bf16[128,256]{1,0:T(8,128)(2,1)}, bf16[128,256]{1,0:T(8,128)(2,1)S(1)}, u32[]{:S(2)}) copy-start(bf16[128,256]{1,0:T(8,128)(2,1)S(1)} %add_convert_fusion) | copy-start | bytes 196612
  98.9 88.2 %reduce-scatter.5.cloned.1.call-start = ((), (), s32[]{:S(2)}) async-start(), calls=%async_computation.6 | async-start | bytes 4718592 | tf_op jit(solution)/shard_map/reduce_scatter | solution.py:125
  102.3 33.8 %copy-start.2 = (bf16[22,8,8,256]{3,2,1,0:T(8,128)(2,1)S(1)}, bf16[22,8,8,256]{3,2,1,0:T(8,128)(2,1)}, u32[]{:S(2)}) copy-start(bf16[22,8,8,256]{3,2,1,0:T(8,128)(2,1)} %copy.124) | copy-start | bytes 2162692
  143.1 56.4 %copy-start.3 = (bf16[2048,64]{0,1:T(8,128)(2,1)S(1)}, bf16[2048,64]{0,1:T(8,128)(2,1)}, u32[]{:S(2)}) copy-start(bf16[2048,64]{0,1:T(8,128)(2,1)} %param.20) | copy-start | bytes 786436
  187.1 30.6 %all-to-all-start.1 = ((bf16[64,16,256]{2,1,0:T(8,128)(2,1)}), bf16[64,16,256]{2,1,0:T(8,128)(2,1)S(1)}, u32[]{:S(2)}, u32[]{:S(2)}) async-start(bf16[64,16,256]{2,1,0:T(8,128)(2,1)} %bitcast.121), calls=%async_computation.3 | async-start | bytes 1048576 | tf_op jit(solution)/shard_map/all_to_all | solution.py:127
Sparse Core Ops, SparseCore 0:
  14.6 40.1 reduce-scatter.2
  99.0 32.1 all-gather.1
  143.3 43.8 reduce-scatter.4

commit v3 on v2

--- a/solution.py
+++ b/solution.py
@@ -77,11 +77,10 @@
         .reshape(tokens_here, heads_here * HD)
     )
     projected = jnp.dot(attended, w_out, preferred_element_type=jnp.float32)
-    attn_share = lax.psum_scatter(
-        projected.astype(jnp.bfloat16), "grp", scatter_dimension=1, tiled=True
-    )
-    after_cols = (resid.astype(jnp.float32) + attn_share.astype(jnp.float32)).astype(jnp.bfloat16)
-    after_full = lax.all_gather(after_cols, "grp", axis=1, tiled=True)
+    projected_full = lax.psum(projected, "grp")
+    resid_full = lax.all_gather(resid, "grp", axis=1, tiled=True)
+    after_full = (resid_full.astype(jnp.float32) + projected_full).astype(jnp.bfloat16)
+    after_cols = lax.dynamic_slice_in_dim(after_full, column_start, column_width, 1)
     after_wide = after_full.astype(jnp.float32)
     squares = jnp.sum(after_wide * after_wide, axis=1)
     inverse = lax.rsqrt(squares / D + EPS)

time: 226 us -> 252 us (1.12)
  waiting for transfers between devices: 128 us -> 145 us
  blocking collectives: 42.5 us -> 47.3 us
    psum x0 -> x1, waiting for transfers between devices: none -> 57.2 us  [body(): projected_full = lax.psum(projected, 'grp')]
    reduce_scatter x1 -> x0, waiting for transfers between devices: 37.7 us -> none  [body(): lax.psum_scatter(projected.astype(jnp.bfloat16), 'grp', scatter_dimension...]
    all_gather x1, blocking collectives: 12 us -> 16.6 us  [body(): resid_full = lax.all_gather(resid, 'grp', axis=1, tiled=True)]
where the time goes in v3:
time: 252 us; the launch traced here: 250 us
  waiting for transfers between devices  145 us (58%)
  blocking collectives  47.3 us (19%)
  matrix products  16.9 us (7%)
  between operations  14 us (6%)
  starting transfers between devices  12.5 us (5%)
  local copies, waits for them, and re-layouts  8.84 us (4%)
  other arithmetic  5.39 us (2%)
    psum x1, waiting for transfers between devices, body(): projected_full = lax.psum(projected, 'grp')  57.2 us
    reduce_scatter x1, waiting for transfers between devices, body(): lax.psum_scatter(slice_out, 'grp', scatter_dimension=0, tiled=True)  44 us
    all_to_all x1, blocking collectives, body(): lax.all_to_all(outgoing, 'ep', split_axis=0, concat_axis=0, tiled=True)  30.7 us
    all_gather x1, waiting for transfers between devices, body(): gathered = lax.all_gather(arrived, 'grp', axis=0, tiled=False)  27.3 us
    all_to_all x1, waiting for transfers between devices, body(): lax.all_to_all(expert_out, 'ep', split_axis=0, concat_axis=0, tiled=True)  17 us
    all_gather x1, blocking collectives, body(): resid_full = lax.all_gather(resid, 'grp', axis=1, tiled=True)  16.6 us
    all_to_all x1, starting transfers between devices, body(): lax.all_to_all(expert_out, 'ep', split_axis=0, concat_axis=0, tiled=True)  12.4 us
    dot_general x1, matrix products, body(): jnp.einsum('nh,hgc->gnc', hidden, down, preferred_element_type=jnp.float32)  7.06 us
  transfers between devices with their start and end apart: 4, of which 4 were waited for; matrix products, arithmetic and copies ran while one was open for 3% of the time, Pallas kernels for 0%

profile of v3, /device:TPU:7, one launch (start us, length us, event | category | flops | bytes accessed | tf_op | source)
XLA Modules:
  0.0 250.4 jit_solution(6483863232802401198)
XLA Ops:
  7.3 1.3 dynamic_slice.10
  8.6 0.6 iota_compare_fusion.5
  9.3 1.0 copy.117
  10.2 1.3 fusion.49
  11.5 0.2 copy.105
  11.7 0.2 copy.118
  11.9 0.2 fusion.50
  12.1 0.4 fusion.51
  13.0 0.3 fusion.10
  13.3 1.4 fusion.52
  15.1 1.2 reduce-window.6
  16.3 0.2 slice_reduce_fusion
  16.9 1.1 fusion
  18.0 16.6 %all_gather.6 = bf16[128,2048]{1,0:T(8,128)(2,1)S(1)} all-gather(bf16[128,256]{1,0:T(8,128)(2,1)} %param.12), channel_id=1, replica_groups=mesh['grp'=8,'ep'=64] {'grp'}, dimensions={1}, use_global_device_ids=true | all-gather | bytes 589824 | tf_op jit(solution)/shard_map/all_gather | solution.py:81
  34.6 57.2 %all-reduce.2.cloned.1.call-done = f32[128,2048]{1,0:T(8,128)} async-done(((f32[128,2048]{1,0:T(8,128)}), f32[128,2048]{1,0:T(8,128)}) %all-reduce.2.cloned.1.call-update) | async-done | bytes 1048592 | tf_op jit(solution)/shard_map/psum | solution.py:80
  91.8 1.5 fusion.11
  93.3 0.2 fusion.13
  93.5 1.3 convolution_convert_fusion
  94.8 30.7 %all_to_all.10 = bf16[64,16,256]{2,1,0:T(8,128)(2,1)} all-to-all(bf16[64,16,256]{2,1,0:T(8,128)(2,1)S(1)} %bitcast.115), channel_id=1, replica_groups=mesh['grp'=8,'ep'=64] {'ep'}, dimensions={0} | all-to-all | bytes 1048576 | tf_op jit(solution)/shard_map/all_to_all | solution.py:109
  125.5 2.2 copy.124
  127.8 1.0 copy.122
  128.8 0.2 copy.123
  129.0 27.3 %all-gather.2.cloned.1.call-done = bf16[8,1024,256]{2,1,0:T(8,128)(2,1)} async-done(((bf16[1,1024,256]{2,1,0:T(8,128)(2,1)}), bf16[8,1024,256]{2,1,0:T(8,128)(2,1)}) %all-gather.2.cloned.1.call-update) | async-done | bytes 4194320 | tf_op jit(solution)/shard_map/all_gather | solution.py:112
  156.3 4.8 %convolution_bitcast_fusion.1 = f32[1024,176]{0,1:T(8,128)} fusion(bf16[8,1024,256]{2,1,0:T(8,128)(2,1)} %all-gather.2.cloned.1.call-done, bf16[8,256,176]{1,0,2:T(8,128)(2,1)} %bitcast.120), kind=kOutput, calls=%fused_computation.11 | convolution fusion | flops 738197504 | bytes 5636096 | tf_op jit(solution)/shard_map/gnc,gch->nh/dot_general | solution.py:115
  161.1 7.1 %convert_bitcast_fusion = bf16[8,1024,256]{2,1,0:T(8,128)(2,1)} fusion(bf16[8,1024,256]{2,1,0:T(8,128)(2,1)} %all-gather.2.cloned.1.call-done, bf16[176,8,256]{2,1,0:T(8,128)(2,1)S(1)} %bitcast.118, bf16[8,256,176]{1,0,2:T(8,128)(2,1)S(1)} %bitcast.119, f32[1024,176]{0,1:T(8,128)} %convolution_bitcast_fusion.1), kind=kOutput, calls=%fused_computation | convolution fusion | flops 1479573504 | bytes 10551296 | tf_op jit(solution)/shard_map/nh,hgc->gnc/dot_general | solution.py:121
  168.2 44.0 %reduce-scatter.2.cloned.1.call-done = bf16[1,1024,256]{2,1,0:T(8,128)(2,1)} async-done(((bf16[8,1024,256]{2,1,0:T(8,128)(2,1)}), bf16[1,1024,256]{2,1,0:T(8,128)(2,1)}) %reduce-scatter.2.cloned.1.call-update) | async-done | bytes 524304 | tf_op jit(solution)/shard_map/reduce_scatter | solution.py:124
  212.2 12.4 %all-to-all-start.1 = ((bf16[64,16,256]{2,1,0:T(8,128)(2,1)}), bf16[64,16,256]{2,1,0:T(8,128)(2,1)S(1)}, u32[]{:S(2)}, u32[]{:S(2)}) async-start(bf16[64,16,256]{2,1,0:T(8,128)(2,1)} %bitcast.121), calls=%async_computation.2 | async-start | bytes 1048576 | tf_op jit(solution)/shard_map/all_to_all | solution.py:126
  224.6 0.3 fusion.53
  224.9 0.6 constant_dynamic-slice_fusion
  225.6 0.3 select_reduce_fusion
  225.9 17.0 %all-to-all-done.1 = bf16[64,16,256]{2,1,0:T(8,128)(2,1)S(1)} async-done(((bf16[64,16,256]{2,1,0:T(8,128)(2,1)}), bf16[64,16,256]{2,1,0:T(8,128)(2,1)S(1)}, u32[]{:S(2)}, u32[]{:S(2)}) %all-to-all-start.1) | async-done | bytes 524320 | tf_op jit(solution)/shard_map/all_to_all | solution.py:126
  242.9 1.0 convolution_convert_fusion.1
  (45 shorter events, 1.5 us)
Async XLA Ops:
  7.2 6.1 %copy-start = (bf16[256,2048]{1,0:T(8,128)(2,1)S(1)}, bf16[256,2048]{1,0:T(8,128)(2,1)}, u32[]{:S(2)}) copy-start(bf16[256,2048]{1,0:T(8,128)(2,1)} %param.18) | copy-start | bytes 3145732
  7.2 4.7 %copy-start.4 = (bf16[128,256]{1,0:T(8,128)(2,1)S(1)}, bf16[128,256]{1,0:T(8,128)(2,1)}, u32[]{:S(2)}) copy-start(bf16[128,256]{1,0:T(8,128)(2,1)} %param.13) | copy-start | bytes 196612
  7.2 4.7 %copy-start.7 = (bf16[128,256]{1,0:T(8,128)(2,1)S(1)}, bf16[128,256]{1,0:T(8,128)(2,1)}, u32[]{:S(2)}) copy-start(bf16[128,256]{1,0:T(8,128)(2,1)} %param.14) | copy-start | bytes 196612
  7.2 84.6 %all-reduce.2.cloned.1.call-start = ((), (), s32[]{:S(2)}) async-start(), calls=%async_computation.3 | async-start | bytes 2097152 | tf_op jit(solution)/shard_map/psum | solution.py:80
  11.9 2.8 %copy-start.5 = (s32[128,4]{0,1:T(4,128)S(1)}, s32[128,4]{0,1:T(4,128)}, u32[]{:S(2)}) copy-start(s32[128,4]{0,1:T(4,128)} %param.21) | copy-start | bytes 6148
  12.1 3.0 %copy-start.6 = (bf16[2048]{0:T(1024)(128)(2,1)S(1)}, bf16[2048]{0:T(1024)(128)(2,1)}, u32[]{:S(2)}) copy-start(bf16[2048]{0:T(1024)(128)(2,1)} %param.19) | copy-start | bytes 12292
  14.7 141.6 %all-gather.2.cloned.1.call-start = ((), (), s32[]{:S(2)}) async-start(), calls=%async_computation.4 | async-start | bytes 4718592 | tf_op jit(solution)/shard_map/all_gather | solution.py:112
  15.1 112.6 %copy-start.1 = (bf16[1,2,2048,176]{2,3,1,0:T(8,128)(2,1)S(1)}, bf16[1,2,2048,176]{2,3,1,0:T(8,128)(2,1)}, u32[]{:S(2)}) copy-start(bf16[1,2,2048,176]{2,3,1,0:T(8,128)(2,1)} %param.22) | copy-start | bytes 4325380
  125.5 86.7 %reduce-scatter.2.cloned.1.call-start = ((), (), s32[]{:S(2)}) async-start(), calls=%async_computation.5 | async-start | bytes 4718592 | tf_op jit(solution)/shard_map/reduce_scatter | solution.py:124
  128.8 32.3 %copy-start.2 = (bf16[22,8,8,256]{3,2,1,0:T(8,128)(2,1)S(1)}, bf16[22,8,8,256]{3,2,1,0:T(8,128)(2,1)}, u32[]{:S(2)}) copy-start(bf16[22,8,8,256]{3,2,1,0:T(8,128)(2,1)} %copy.124) | copy-start | bytes 2162692
  168.2 56.4 %copy-start.3 = (bf16[2048,64]{0,1:T(8,128)(2,1)S(1)}, bf16[2048,64]{0,1:T(8,128)(2,1)}, u32[]{:S(2)}) copy-start(bf16[2048,64]{0,1:T(8,128)(2,1)} %param.20) | copy-start | bytes 786436
  212.2 30.7 %all-to-all-start.1 = ((bf16[64,16,256]{2,1,0:T(8,128)(2,1)}), bf16[64,16,256]{2,1,0:T(8,128)(2,1)S(1)}, u32[]{:S(2)}, u32[]{:S(2)}) async-start(bf16[64,16,256]{2,1,0:T(8,128)(2,1)} %bitcast.121), calls=%async_computation.2 | async-start | bytes 1048576 | tf_op jit(solution)/shard_map/all_to_all | solution.py:126
Sparse Core Ops, SparseCore 0:
  14.8 76.9 all-reduce.1
  125.6 30.6 all-gather.1
  168.3 43.8 reduce-scatter.1

commit v4 on v1

--- a/solution.py
+++ b/solution.py
@@ -1,6 +1,7 @@
 import jax
 import jax.numpy as jnp
 from jax import lax
+from jax.experimental import pallas as pl
 from jax.sharding import PartitionSpec as P
 
 D = 2048
@@ -10,6 +11,40 @@
 
 EPS = 1e-06
 MASKED = -1e30
+
+
+def ffn_kernel(x_ref, gu_ref, down_ref, out_ref):
+    groups, rows, width = x_ref.shape
+    gate = jnp.zeros((rows, gu_ref.shape[-1]), jnp.float32)
+    up = jnp.zeros((rows, gu_ref.shape[-1]), jnp.float32)
+    for g in range(groups):
+        x = x_ref[g]
+        gate = gate + jnp.dot(
+            x, gu_ref[0, g * width:(g + 1) * width, :], preferred_element_type=jnp.float32
+        )
+        up = up + jnp.dot(
+            x, gu_ref[1, g * width:(g + 1) * width, :], preferred_element_type=jnp.float32
+        )
+    hidden = (jax.nn.silu(gate) * up).astype(jnp.bfloat16)
+    for g in range(groups):
+        out_ref[g] = jnp.dot(
+            hidden, down_ref[:, g * width:(g + 1) * width], preferred_element_type=jnp.float32
+        ).astype(out_ref.dtype)
+
+
+def expert_ffn(gathered, gate_up, down, row_tile=256):
+    groups, rows, width = gathered.shape
+    return pl.pallas_call(
+        ffn_kernel,
+        grid=(rows // row_tile,),
+        in_specs=[
+            pl.BlockSpec((groups, row_tile, width), lambda i: (0, i, 0)),
+            pl.BlockSpec(gate_up.shape, lambda i: (0, 0, 0)),
+            pl.BlockSpec(down.shape, lambda i: (0, 0)),
+        ],
+        out_specs=pl.BlockSpec((groups, row_tile, width), lambda i: (0, i, 0)),
+        out_shape=jax.ShapeDtypeStruct(gathered.shape, jnp.bfloat16),
+    )(gathered, gate_up, down)
 
 
 def body(
@@ -109,19 +144,8 @@
     arrived = arrived.reshape(experts_all * capacity, column_width)
     groups = lax.axis_size("grp")
     gathered = lax.all_gather(arrived, "grp", axis=0, tiled=False)
-    slice_width = w_gate_up.shape[-1]
-    gate_up = w_gate_up[0].reshape(2, groups, column_width, slice_width)
-    gate_value = jnp.einsum(
-        "gnc,gch->nh", gathered, gate_up[0], preferred_element_type=jnp.float32
-    )
-    up_value = jnp.einsum("gnc,gch->nh", gathered, gate_up[1], preferred_element_type=jnp.float32)
-    hidden = (jax.nn.silu(gate_value) * up_value).astype(jnp.bfloat16)
-    down = w_down[0].reshape(slice_width, groups, column_width)
-    slice_out = jnp.einsum(
-        "nh,hgc->gnc", hidden, down, preferred_element_type=jnp.float32
-    ).astype(jnp.bfloat16)
-    slices_here = lax.all_to_all(slice_out, "grp", split_axis=0, concat_axis=0, tiled=True)
-    expert_out = jnp.sum(slices_here.astype(jnp.float32), axis=0)
+    slice_out = expert_ffn(gathered, w_gate_up[0], w_down[0])
+    expert_out = lax.psum_scatter(slice_out, "grp", scatter_dimension=0, tiled=True)
     expert_out = expert_out.reshape(experts_all, capacity, column_width)
     returned = lax.all_to_all(expert_out, "ep", split_axis=0, concat_axis=0, tiled=True)
     mixed_cols = jnp.dot(

time: 252 us -> 224 us (0.89); the launches traced: 247 us -> 223 us
  blocking collectives: 96.1 us -> 42.7 us
  waiting for transfers between devices: 93.5 us -> 130 us
  matrix products: 16.2 us -> 4.11 us
  Pallas kernels: 0 us -> 8.02 us
    all_to_all x1 -> x0, blocking collectives: 53.4 us -> none  [body(): lax.all_to_all(slice_out, 'grp', split_axis=0, concat_axis=0, tiled=True)]
    reduce_scatter x0 -> x1, waiting for transfers between devices: none -> 44 us  [body(): lax.psum_scatter(slice_out, 'grp', scatter_dimension=0, tiled=True)]
    dot_general x2 -> x0, matrix products: 11.9 us -> none  [the longest x1 7.06 us: body(): jnp.einsum('nh,hgc->gnc', hidden, down, preferred_element_type=jnp.float32)]
    all_to_all x1, waiting for transfers between devices: 26.1 us -> 17.5 us  [body(): lax.all_to_all(expert_out, 'ep', split_axis=0, concat_axis=0, tiled=True)]
    pallas_call x0 -> x1, Pallas kernels: none -> 8.02 us  [expert_ffn(): pl.pallas_call(ffn_kernel, grid=(rows // row_tile,), in_specs=[pl.BlockSp...]
  transfers between devices with their start and end apart: 3 -> 4, of which waited for: 3 -> 4; matrix products, arithmetic and copies ran while one was open for 3% -> 3% of each run, Pallas kernels for 0% -> 0%
where the time goes in v4:
time: 224 us; the launch traced here: 223 us
  waiting for transfers between devices  130 us (58%)
  blocking collectives  42.7 us (19%)
  between operations  14 us (6%)
  starting transfers between devices  12.5 us (6%)
  Pallas kernels  8.02 us (4%)
  local copies, waits for them, and re-layouts  7.19 us (3%)
  other arithmetic  4.36 us (2%)
  matrix products  4.11 us (2%)
    reduce_scatter x1, waiting for transfers between devices, body(): lax.psum_scatter(slice_out, 'grp', scatter_dimension=0, tiled=True)  44 us
    reduce_scatter x1, waiting for transfers between devices, body(): lax.psum_scatter(projected, 'grp', scatter_dimension=1, tiled=True)  38.5 us
    all_to_all x1, blocking collectives, body(): lax.all_to_all(outgoing, 'ep', split_axis=0, concat_axis=0, tiled=True)  30.6 us
    all_gather x1, waiting for transfers between devices, body(): gathered = lax.all_gather(arrived, 'grp', axis=0, tiled=False)  29.8 us
    all_to_all x1, waiting for transfers between devices, body(): lax.all_to_all(expert_out, 'ep', split_axis=0, concat_axis=0, tiled=True)  17.5 us
    all_to_all x1, starting transfers between devices, body(): lax.all_to_all(expert_out, 'ep', split_axis=0, concat_axis=0, tiled=True)  12.4 us
    all_gather x1, blocking collectives, body(): after_full = lax.all_gather(after_cols, 'grp', axis=1, tiled=True)  12.1 us
    pallas_call x1, Pallas kernels, expert_ffn(): pl.pallas_call(ffn_kernel, grid=(rows // row_tile,), in_specs=[pl.BlockSp...  8.02 us
  transfers between devices with their start and end apart: 4, of which 4 were waited for; matrix products, arithmetic and copies ran while one was open for 3% of the time, Pallas kernels for 0%

profile of v4, /device:TPU:7, one launch (start us, length us, event | category | flops | bytes accessed | tf_op | source)
XLA Modules:
  0.0 222.8 jit_solution(11294067998846975590)
XLA Ops:
  7.3 1.3 dynamic_slice.7
  8.6 0.6 iota_compare_fusion.5
  9.2 1.0 copy.92
  10.2 1.3 fusion.34
  11.5 0.2 copy.82
  11.7 0.2 copy.93
  12.0 0.2 fusion.35
  12.1 0.4 fusion.36
  12.6 0.2 fusion.21
  12.8 0.2 fusion.11
  13.0 0.3 fusion.7
  13.4 1.3 fusion.37
  15.1 1.2 reduce-window.6
  16.3 0.2 slice_reduce_fusion
  16.6 0.1 fusion.17
  16.9 0.4 fusion
  17.3 38.5 %reduce-scatter.3.cloned.1.call-done = f32[128,256]{1,0:T(8,128)} async-done(((f32[128,2048]{1,0:T(8,128)}), f32[128,256]{1,0:T(8,128)}) %reduce-scatter.3.cloned.1.call-update) | async-done | bytes 131088 | tf_op jit(solution)/shard_map/reduce_scatter | solution.py:115
  55.9 0.9 add_convert_fusion
  56.8 12.1 %all_gather.6 = bf16[128,2048]{1,0:T(8,128)(2,1)S(1)} all-gather(bf16[128,256]{1,0:T(8,128)(2,1)S(1)} %add_convert_fusion), channel_id=1, replica_groups=mesh['grp'=8,'ep'=64] {'grp'}, dimensions={1}, use_global_device_ids=true | all-gather | bytes 589824 | tf_op jit(solution)/shard_map/all_gather | solution.py:117
  68.9 0.2 fusion.8
  69.1 0.2 fusion.10
  69.3 0.4 convolution_convert_fusion
  69.7 30.6 %all_to_all.10 = bf16[64,16,256]{2,1,0:T(8,128)(2,1)} all-to-all(bf16[64,16,256]{2,1,0:T(8,128)(2,1)S(1)} %bitcast.81), channel_id=1, replica_groups=mesh['grp'=8,'ep'=64] {'ep'}, dimensions={0} | all-to-all | bytes 1048576 | tf_op jit(solution)/shard_map/all_to_all | solution.py:143
  100.4 2.4 %copy.88 = bf16[1,2,2048,176]{3,2,1,0:T(8,128)(2,1)} copy(bf16[1,2,2048,176]{2,3,1,0:T(8,128)(2,1)S(1)} %copy-done.1) | data formatting | bytes 2883584 | tf_op args[10]
  102.8 29.8 %all-gather.2.cloned.1.call-done.x_ref = bf16[8,1024,256]{2,1,0:T(8,128)(2,1)} async-done(((bf16[1,1024,256]{2,1,0:T(8,128)(2,1)}), bf16[8,1024,256]{2,1,0:T(8,128)(2,1)}) %all-gather.2.cloned.1.call-update) | async-done | bytes 4194320 | tf_op jit(solution)/shard_map/all_gather | solution.py:146
  132.6 8.0 %shard_map.131 = bf16[8,1024,256]{2,1,0:T(8,128)(2,1)} custom-call(bf16[8,1024,256]{2,1,0:T(8,128)(2,1)} %all-gather.2.cloned.1.call-done.x_ref, bf16[2,2048,176]{2,1,0:T(8,128)(2,1)} %bitcast.77, bf16[176,2048]{1,0:T(8,128)(2,1)} %bitcast.83), custom_call_target="tpu_custom_call" | custom-call | tf_op jit(solution)/shard_map/pallas_call | solution.py:37
  140.7 44.0 %reduce-scatter.5.cloned.1.call-done = bf16[1,1024,256]{2,1,0:T(8,128)(2,1)} async-done(((bf16[8,1024,256]{2,1,0:T(8,128)(2,1)}), bf16[1,1024,256]{2,1,0:T(8,128)(2,1)}) %reduce-scatter.5.cloned.1.call-update) | async-done | bytes 524304 | tf_op jit(solution)/shard_map/reduce_scatter | solution.py:148
  184.6 12.4 %all-to-all-start.1 = ((bf16[64,16,256]{2,1,0:T(8,128)(2,1)}), bf16[64,16,256]{2,1,0:T(8,128)(2,1)S(1)}, u32[]{:S(2)}, u32[]{:S(2)}) async-start(bf16[64,16,256]{2,1,0:T(8,128)(2,1)} %bitcast.84), calls=%async_computation.3 | async-start | bytes 1048576 | tf_op jit(solution)/shard_map/all_to_all | solution.py:150
  197.1 0.3 fusion.38
  197.5 0.3 select_reduce_fusion
  197.8 17.5 %all-to-all-done.1 = bf16[64,16,256]{2,1,0:T(8,128)(2,1)S(1)} async-done(((bf16[64,16,256]{2,1,0:T(8,128)(2,1)}), bf16[64,16,256]{2,1,0:T(8,128)(2,1)S(1)}, u32[]{:S(2)}, u32[]{:S(2)}) %all-to-all-start.1) | async-done | bytes 524320 | tf_op jit(solution)/shard_map/all_to_all | solution.py:150
  215.3 1.0 convolution_convert_fusion.1
  (43 shorter events, 1.0 us)
Async XLA Ops:
  7.2 6.2 %copy-start = (bf16[256,2048]{1,0:T(8,128)(2,1)S(1)}, bf16[256,2048]{1,0:T(8,128)(2,1)}, u32[]{:S(2)}) copy-start(bf16[256,2048]{1,0:T(8,128)(2,1)} %param.18) | copy-start | bytes 3145732
  7.2 48.7 %reduce-scatter.3.cloned.1.call-start = ((), (), s32[]{:S(2)}) async-start(), calls=%async_computation.4 | async-start | bytes 1179648 | tf_op jit(solution)/shard_map/reduce_scatter | solution.py:115
  10.2 1.8 copy-start.4
  10.2 1.8 copy-start.8
  13.0 1.8 copy-start.6
  13.3 1.8 copy-start.7
  13.3 42.5 %copy-start.5 = (bf16[128,256]{1,0:T(8,128)(2,1)S(1)}, bf16[128,256]{1,0:T(8,128)(2,1)}, u32[]{:S(2)}) copy-start(bf16[128,256]{1,0:T(8,128)(2,1)} %param.12) | copy-start | bytes 196612
  14.7 117.9 %all-gather.2.cloned.1.call-start = ((), (), s32[]{:S(2)}) async-start(), calls=%async_computation.5 | async-start | bytes 4718592 | tf_op jit(solution)/shard_map/all_gather | solution.py:146
  56.8 43.5 %copy-start.3 = (bf16[128,256]{1,0:T(8,128)(2,1)}, bf16[128,256]{1,0:T(8,128)(2,1)S(1)}, u32[]{:S(2)}) copy-start(bf16[128,256]{1,0:T(8,128)(2,1)S(1)} %add_convert_fusion) | copy-start | bytes 196612
  56.8 43.5 %copy-start.1 = (bf16[1,2,2048,176]{2,3,1,0:T(8,128)(2,1)S(1)}, bf16[1,2,2048,176]{2,3,1,0:T(8,128)(2,1)}, u32[]{:S(2)}) copy-start(bf16[1,2,2048,176]{2,3,1,0:T(8,128)(2,1)} %param.22) | copy-start | bytes 4325380
  100.3 84.3 %reduce-scatter.5.cloned.1.call-start = ((), (), s32[]{:S(2)}) async-start(), calls=%async_computation.6 | async-start | bytes 4718592 | tf_op jit(solution)/shard_map/reduce_scatter | solution.py:148
  140.7 56.4 %copy-start.2 = (bf16[2048,64]{0,1:T(8,128)(2,1)S(1)}, bf16[2048,64]{0,1:T(8,128)(2,1)}, u32[]{:S(2)}) copy-start(bf16[2048,64]{0,1:T(8,128)(2,1)} %param.20) | copy-start | bytes 786436
  184.6 30.6 %all-to-all-start.1 = ((bf16[64,16,256]{2,1,0:T(8,128)(2,1)}), bf16[64,16,256]{2,1,0:T(8,128)(2,1)S(1)}, u32[]{:S(2)}, u32[]{:S(2)}) async-start(bf16[64,16,256]{2,1,0:T(8,128)(2,1)} %bitcast.84), calls=%async_computation.3 | async-start | bytes 1048576 | tf_op jit(solution)/shard_map/all_to_all | solution.py:150
Sparse Core Ops, SparseCore 0:
  14.8 41.0 reduce-scatter.2
  100.4 32.1 all-gather.1
  140.8 43.7 reduce-scatter.4

commit v5 on v4

--- a/solution.py
+++ b/solution.py
@@ -1,7 +1,10 @@
+import math
+
 import jax
 import jax.numpy as jnp
 from jax import lax
 from jax.experimental import pallas as pl
+from jax.sharding import Mesh
 from jax.sharding import PartitionSpec as P
 
 D = 2048
@@ -66,8 +69,9 @@
     experts_all = w_router.shape[1]
     column_width = resid.shape[1]
     group_index = lax.axis_index("grp")
-    request = lax.axis_index("ep")
-    capacity = max(2, 8 * tokens_here // lax.axis_size("ep"))
+    request = lax.axis_index("ez") * lax.axis_size("ey") + lax.axis_index("ey")
+    ep_size = lax.axis_size("ez") * lax.axis_size("ey")
+    capacity = max(2, 8 * tokens_here // ep_size)
     score_scale = float(HD) ** (-0.5)
     column_start = group_index * column_width
     queries = query.reshape(tokens_here, heads_here, HD)
@@ -139,15 +143,19 @@
     outgoing = jnp.einsum(
         "tj,td->jd", selection, normed_cols, preferred_element_type=jnp.float32
     ).astype(jnp.bfloat16)
-    outgoing = outgoing.reshape(experts_all, capacity, column_width)
-    arrived = lax.all_to_all(outgoing, "ep", split_axis=0, concat_axis=0, tiled=True)
+    outgoing = outgoing.reshape(lax.axis_size("ez"), lax.axis_size("ey"), capacity, column_width)
+    arrived = lax.all_to_all(outgoing, "ey", split_axis=1, concat_axis=1, tiled=True)
+    arrived = lax.all_to_all(arrived, "ez", split_axis=0, concat_axis=0, tiled=True)
     arrived = arrived.reshape(experts_all * capacity, column_width)
     groups = lax.axis_size("grp")
     gathered = lax.all_gather(arrived, "grp", axis=0, tiled=False)
     slice_out = expert_ffn(gathered, w_gate_up[0], w_down[0])
     expert_out = lax.psum_scatter(slice_out, "grp", scatter_dimension=0, tiled=True)
-    expert_out = expert_out.reshape(experts_all, capacity, column_width)
-    returned = lax.all_to_all(expert_out, "ep", split_axis=0, concat_axis=0, tiled=True)
+    expert_out = expert_out.reshape(
+        lax.axis_size("ez"), lax.axis_size("ey"), capacity, column_width
+    )
+    returned = lax.all_to_all(expert_out, "ez", split_axis=0, concat_axis=0, tiled=True)
+    returned = lax.all_to_all(returned, "ey", split_axis=1, concat_axis=1, tiled=True)
     mixed_cols = jnp.dot(
         combine,
         returned.reshape(experts_all * capacity, column_width),
@@ -157,24 +165,30 @@
     return (after_cols, mixed_cols.astype(jnp.bfloat16))
 
 
+EP = ("ez", "ey")
+
+
 def solution(mesh):
+    grp_size, ep_size = mesh.devices.shape
+    side = math.isqrt(ep_size)
+    fine = Mesh(mesh.devices.reshape(grp_size, ep_size // side, side), ("grp", "ez", "ey"))
     return jax.shard_map(
         body,
-        mesh=mesh,
+        mesh=fine,
         in_specs=(
-            P("ep", "grp"),
-            P("ep", "grp"),
-            P("ep", "grp"),
-            P("ep", "grp"),
-            P(None, "ep", "grp"),
+            P(EP, "grp"),
+            P(EP, "grp"),
+            P(EP, "grp"),
+            P(EP, "grp"),
+            P(None, EP, "grp"),
             P(),
             P("grp", None),
             P(),
             P(),
-            P("ep", None),
-            P("ep", None, None, "grp"),
-            P("ep", "grp", None),
+            P(EP, None),
+            P(EP, None, None, "grp"),
+            P(EP, "grp", None),
         ),
-        out_specs=(P("ep", "grp"), P("ep", "grp")),
+        out_specs=(P(EP, "grp"), P(EP, "grp")),
         check_vma=False,
     )

time: 224 us -> 256 us (1.14)
  blocking collectives: 42.7 us -> 82.9 us
  starting transfers between devices: 12.5 us -> 6.57 us
  waiting for transfers between devices: 130 us -> 127 us
    all_to_all x1 -> x3, blocking collectives: 30.6 us -> 71 us  [the longest x1 24.2 us: body(): lax.all_to_all(outgoing, 'ey', split_axis=1, concat_axis=1, tiled=True)]
    all_to_all x1, starting transfers between devices: 12.4 us -> 6.45 us  [body(): lax.all_to_all(returned, 'ey', split_axis=1, concat_axis=1, tiled=True)]
    all_gather x1, waiting for transfers between devices: 29.8 us -> 27 us  [body(): gathered = lax.all_gather(arrived, 'grp', axis=0, tiled=False)]
  transfers between devices with their start and end apart: 4 -> 4, of which waited for: 4 -> 4; matrix products, arithmetic and copies ran while one was open for 3% -> 2% of each run, Pallas kernels for 0% -> 0%
where the time goes in v5:
time: 256 us; the launch traced here: 255 us
  waiting for transfers between devices  127 us (50%)
  blocking collectives  82.9 us (32%)
  between operations  14 us (5%)
  local copies, waits for them, and re-layouts  8.15 us (3%)
  Pallas kernels  8.03 us (3%)
  starting transfers between devices  6.57 us (3%)
  other arithmetic  4.36 us (2%)
  matrix products  4.14 us (2%)
    reduce_scatter x1, waiting for transfers between devices, body(): lax.psum_scatter(slice_out, 'grp', scatter_dimension=0, tiled=True)  44 us
    reduce_scatter x1, waiting for transfers between devices, body(): lax.psum_scatter(projected, 'grp', scatter_dimension=1, tiled=True)  38.6 us
    all_gather x1, waiting for transfers between devices, body(): gathered = lax.all_gather(arrived, 'grp', axis=0, tiled=False)  27 us
    all_to_all x1, blocking collectives, body(): lax.all_to_all(outgoing, 'ey', split_axis=1, concat_axis=1, tiled=True)  24.2 us
    all_to_all x1, blocking collectives, body(): lax.all_to_all(expert_out, 'ez', split_axis=0, concat_axis=0, tiled=True)  23.6 us
    all_to_all x1, blocking collectives, body(): lax.all_to_all(arrived, 'ez', split_axis=0, concat_axis=0, tiled=True)  23.1 us
    all_to_all x1, waiting for transfers between devices, body(): lax.all_to_all(returned, 'ey', split_axis=1, concat_axis=1, tiled=True)  17.3 us
    all_gather x1, blocking collectives, body(): after_full = lax.all_gather(after_cols, 'grp', axis=1, tiled=True)  12 us
  transfers between devices with their start and end apart: 4, of which 4 were waited for; matrix products, arithmetic and copies ran while one was open for 2% of the time, Pallas kernels for 0%

profile of v5, /device:TPU:7, one launch (start us, length us, event | category | flops | bytes accessed | tf_op | source)
XLA Modules:
  0.0 255.1 jit_solution(912217339806743866)
XLA Ops:
  7.3 1.3 dynamic_slice.7
  8.6 0.6 iota_compare_fusion.5
  9.2 1.0 copy.144
  10.2 1.3 fusion.34
  11.5 0.2 copy.130
  11.7 0.2 copy.145
  12.0 0.2 fusion.35
  12.2 0.4 fusion.36
  13.0 0.3 fusion.7
  13.4 1.3 fusion.37
  15.1 1.2 reduce-window.6
  16.4 0.2 slice_reduce_fusion
  16.9 0.4 fusion
  17.3 38.6 %reduce-scatter.3.cloned.1.call-done = f32[128,256]{1,0:T(8,128)} async-done(((f32[128,2048]{1,0:T(8,128)}), f32[128,256]{1,0:T(8,128)}) %reduce-scatter.3.cloned.1.call-update) | async-done | bytes 131088 | tf_op jit(solution)/shard_map/reduce_scatter | solution.py:119
  56.0 0.9 add_convert_fusion
  56.9 12.0 %all_gather.6 = bf16[128,2048]{1,0:T(8,128)(2,1)S(1)} all-gather(bf16[128,256]{1,0:T(8,128)(2,1)S(1)} %add_convert_fusion), channel_id=1, replica_groups=mesh['grp'=8,'ez'=8,'ey'=8] {'grp'}, dimensions={1}, use_global_device_ids=true | all-gather | bytes 589824 | tf_op jit(solution)/shard_map/all_gather | solution.py:121
  68.9 0.2 fusion.8
  69.1 0.2 fusion.10
  69.3 0.4 convolution_convert_fusion
  69.7 24.2 %all_to_all.20 = bf16[8,8,16,256]{3,2,0,1:T(8,128)(2,1)S(1)} all-to-all(bf16[8,8,16,256]{3,2,0,1:T(8,128)(2,1)S(1)} %copy.136), channel_id=1, replica_groups=mesh['grp'=8,'ez'=8,'ey'=8] {'ey'}, dimensions={1} | all-to-all | bytes 1048576 | tf_op jit(solution)/shard_map/all_to_all | solution.py:147
  93.9 23.1 %all_to_all.21 = bf16[8,8,16,256]{3,2,1,0:T(8,128)(2,1)} all-to-all(bf16[8,8,16,256]{3,2,1,0:T(8,128)(2,1)S(1)} %copy.137), channel_id=1, replica_groups=mesh['grp'=8,'ez'=8,'ey'=8] {'ez'}, dimensions={0} | all-to-all | bytes 1048576 | tf_op jit(solution)/shard_map/all_to_all | solution.py:148
  117.2 2.4 copy.138
  119.6 27.0 %all-gather.2.cloned.1.call-done.x_ref = bf16[8,1024,256]{2,1,0:T(8,128)(2,1)} async-done(((bf16[1,1024,256]{2,1,0:T(8,128)(2,1)}), bf16[8,1024,256]{2,1,0:T(8,128)(2,1)}) %all-gather.2.cloned.1.call-update) | async-done | bytes 4194320 | tf_op jit(solution)/shard_map/all_gather | solution.py:151
  146.6 8.0 %shard_map.131 = bf16[8,1024,256]{2,1,0:T(8,128)(2,1)} custom-call(bf16[8,1024,256]{2,1,0:T(8,128)(2,1)} %all-gather.2.cloned.1.call-done.x_ref, bf16[2,2048,176]{2,1,0:T(8,128)(2,1)} %bitcast.77, bf16[176,2048]{1,0:T(8,128)(2,1)} %bitcast.83), custom_call_target="tpu_custom_call" | custom-call | tf_op jit(solution)/shard_map/pallas_call | solution.py:40
  154.7 44.0 %reduce-scatter.5.cloned.1.call-done = bf16[1,1024,256]{2,1,0:T(8,128)(2,1)} async-done(((bf16[8,1024,256]{2,1,0:T(8,128)(2,1)}), bf16[1,1024,256]{2,1,0:T(8,128)(2,1)}) %reduce-scatter.5.cloned.1.call-update) | async-done | bytes 524304 | tf_op jit(solution)/shard_map/reduce_scatter | solution.py:153
  198.6 23.6 %all_to_all.22 = bf16[8,8,16,256]{3,2,1,0:T(8,128)(2,1)S(1)} all-to-all(bf16[8,8,16,256]{3,2,1,0:T(8,128)(2,1)} %bitcast.84), channel_id=1, replica_groups=mesh['grp'=8,'ez'=8,'ey'=8] {'ez'}, dimensions={0} | all-to-all | bytes 1048576 | tf_op jit(solution)/shard_map/all_to_all | solution.py:157
  222.3 0.8 copy.139
  223.1 6.5 %all-to-all-start.3 = ((bf16[8,8,16,256]{3,2,0,1:T(8,128)(2,1)}), bf16[8,8,16,256]{3,2,0,1:T(8,128)(2,1)S(1)}, u32[]{:S(2)}, u32[]{:S(2)}) async-start(bf16[8,8,16,256]{3,2,0,1:T(8,128)(2,1)} %copy.139), calls=%async_computation.5 | async-start | bytes 1048576 | tf_op jit(solution)/shard_map/all_to_all | solution.py:158
  229.6 0.3 fusion.38
  230.0 0.3 select_reduce_fusion
  230.3 17.3 %all-to-all-done.3 = bf16[8,8,16,256]{3,2,0,1:T(8,128)(2,1)S(1)} async-done(((bf16[8,8,16,256]{3,2,0,1:T(8,128)(2,1)}), bf16[8,8,16,256]{3,2,0,1:T(8,128)(2,1)S(1)}, u32[]{:S(2)}, u32[]{:S(2)}) %all-to-all-start.3) | async-done | bytes 524320 | tf_op jit(solution)/shard_map/all_to_all | solution.py:158
  247.6 1.0 convolution_convert_fusion.1
  (49 shorter events, 1.5 us)
Async XLA Ops:
  7.2 6.2 %copy-start = (bf16[256,2048]{1,0:T(8,128)(2,1)S(1)}, bf16[256,2048]{1,0:T(8,128)(2,1)}, u32[]{:S(2)}) copy-start(bf16[256,2048]{1,0:T(8,128)(2,1)} %param.18) | copy-start | bytes 3145732
  7.2 48.8 %reduce-scatter.3.cloned.1.call-start = ((), (), s32[]{:S(2)}) async-start(), calls=%async_computation.6 | async-start | bytes 1179648 | tf_op jit(solution)/shard_map/reduce_scatter | solution.py:119
  10.2 1.8 copy-start.4
  10.2 1.8 copy-start.8
  13.0 1.8 copy-start.6
  13.3 1.8 copy-start.7
  13.3 42.6 %copy-start.5 = (bf16[128,256]{1,0:T(8,128)(2,1)S(1)}, bf16[128,256]{1,0:T(8,128)(2,1)}, u32[]{:S(2)}) copy-start(bf16[128,256]{1,0:T(8,128)(2,1)} %param.12) | copy-start | bytes 196612
  14.7 131.9 %all-gather.2.cloned.1.call-start = ((), (), s32[]{:S(2)}) async-start(), calls=%async_computation.7 | async-start | bytes 4718592 | tf_op jit(solution)/shard_map/all_gather | solution.py:151
  56.9 37.0 %copy-start.3 = (bf16[128,256]{1,0:T(8,128)(2,1)}, bf16[128,256]{1,0:T(8,128)(2,1)S(1)}, u32[]{:S(2)}) copy-start(bf16[128,256]{1,0:T(8,128)(2,1)S(1)} %add_convert_fusion) | copy-start | bytes 196612
  69.7 47.5 %copy-start.1 = (bf16[1,2,2048,176]{2,3,1,0:T(8,128)(2,1)S(1)}, bf16[1,2,2048,176]{2,3,1,0:T(8,128)(2,1)}, u32[]{:S(2)}) copy-start(bf16[1,2,2048,176]{2,3,1,0:T(8,128)(2,1)} %param.22) | copy-start | bytes 4325380
  117.1 81.5 %reduce-scatter.5.cloned.1.call-start = ((), (), s32[]{:S(2)}) async-start(), calls=%async_computation.8 | async-start | bytes 4718592 | tf_op jit(solution)/shard_map/reduce_scatter | solution.py:153
  154.7 74.9 %copy-start.2 = (bf16[2048,64]{0,1:T(8,128)(2,1)S(1)}, bf16[2048,64]{0,1:T(8,128)(2,1)}, u32[]{:S(2)}) copy-start(bf16[2048,64]{0,1:T(8,128)(2,1)} %param.20) | copy-start | bytes 786436
  223.1 24.4 %all-to-all-start.3 = ((bf16[8,8,16,256]{3,2,0,1:T(8,128)(2,1)}), bf16[8,8,16,256]{3,2,0,1:T(8,128)(2,1)S(1)}, u32[]{:S(2)}, u32[]{:S(2)}) async-start(bf16[8,8,16,256]{3,2,0,1:T(8,128)(2,1)} %copy.139), calls=%async_computation.5 | async-start | bytes 1048576 | tf_op jit(solution)/shard_map/all_to_all | solution.py:158
Sparse Core Ops, SparseCore 0:
  14.8 41.0 reduce-scatter.2
  117.2 29.3 all-gather.1
  154.8 43.8 reduce-scatter.4

commit v6 on v4

--- a/solution.py
+++ b/solution.py
@@ -2,6 +2,7 @@
 import jax.numpy as jnp
 from jax import lax
 from jax.experimental import pallas as pl
+from jax.experimental.pallas import tpu as pltpu
 from jax.sharding import PartitionSpec as P
 
 D = 2048
@@ -11,6 +12,69 @@
 
 EPS = 1e-06
 MASKED = -1e30
+
+
+def attention_kernel(len_ref, q_ref, kn_ref, vn_ref, cache_ref, wout_ref, out_ref):
+    tokens, width = q_ref.shape
+    cache_rows = cache_ref.shape[1]
+    length = len_ref[0]
+    score_scale = float(HD) ** (-0.5)
+    contract_last = (((1,), (1,)), ((), ()))
+    causal = lax.broadcasted_iota(jnp.int32, (tokens, tokens), 0) >= lax.broadcasted_iota(
+        jnp.int32, (tokens, tokens), 1
+    )
+    live = lax.broadcasted_iota(jnp.int32, (tokens, cache_rows), 1) < length
+    heads = []
+    for h in range(width // HD):
+        cols = slice(h * HD, (h + 1) * HD)
+        q = q_ref[:, cols]
+        new_scores = (
+            lax.dot_general(q, kn_ref[:, cols], contract_last, preferred_element_type=jnp.float32)
+            * score_scale
+        )
+        new_scores = jnp.where(causal, new_scores, MASKED)
+        old_scores = (
+            lax.dot_general(
+                q, cache_ref[0, :, cols], contract_last, preferred_element_type=jnp.float32
+            )
+            * score_scale
+        )
+        old_scores = jnp.where(live, old_scores, MASKED)
+        row_max = jnp.maximum(
+            jnp.max(new_scores, axis=1, keepdims=True), jnp.max(old_scores, axis=1, keepdims=True)
+        )
+        new_probs = jnp.exp(new_scores - row_max)
+        old_probs = jnp.exp(old_scores - row_max)
+        denominator = jnp.sum(new_probs, axis=1, keepdims=True) + jnp.sum(
+            old_probs, axis=1, keepdims=True
+        )
+        weighted = jnp.dot(
+            new_probs.astype(jnp.bfloat16), vn_ref[:, cols], preferred_element_type=jnp.float32
+        ) + jnp.dot(
+            old_probs.astype(jnp.bfloat16), cache_ref[1, :, cols], preferred_element_type=jnp.float32
+        )
+        heads.append((weighted / denominator).astype(jnp.bfloat16))
+    attended = jnp.concatenate(heads, axis=1)
+    out_ref[...] = jnp.dot(attended, wout_ref[...], preferred_element_type=jnp.float32)
+
+
+def attention_projected(own_length, query, key_new, value_new, cache_kv, w_out):
+    tokens = query.shape[0]
+    whole = lambda shape: pl.BlockSpec(shape, lambda i: (0,) * len(shape))
+    return pl.pallas_call(
+        attention_kernel,
+        grid=(1,),
+        in_specs=[
+            pl.BlockSpec(memory_space=pltpu.SMEM),
+            whole(query.shape),
+            whole(key_new.shape),
+            whole(value_new.shape),
+            whole(cache_kv.shape),
+            whole(w_out.shape),
+        ],
+        out_specs=whole((tokens, w_out.shape[1])),
+        out_shape=jax.ShapeDtypeStruct((tokens, w_out.shape[1]), jnp.float32),
+    )(own_length, query, key_new, value_new, cache_kv, w_out)
 
 
 def ffn_kernel(x_ref, gu_ref, down_ref, out_ref):
@@ -70,48 +134,8 @@
     capacity = max(2, 8 * tokens_here // lax.axis_size("ep"))
     score_scale = float(HD) ** (-0.5)
     column_start = group_index * column_width
-    queries = query.reshape(tokens_here, heads_here, HD)
-    new_keys = key_new.reshape(tokens_here, heads_here, HD)
-    new_values = value_new.reshape(tokens_here, heads_here, HD)
-    cache_rows = cache_kv.shape[1]
-    cache_keys = cache_kv[0].reshape(cache_rows, heads_here, HD)
-    cache_values = cache_kv[1].reshape(cache_rows, heads_here, HD)
-    own_length = lax.dynamic_index_in_dim(cache_len, request, 0, keepdims=False)
-    position = jnp.arange(tokens_here, dtype=jnp.int32)
-    causal = (position[:, None] >= position[None, :])[:, None, :]
-    new_scores = (
-        jnp.einsum("qhd,khd->qhk", queries, new_keys, preferred_element_type=jnp.float32)
-        * score_scale
-    )
-    new_scores = jnp.where(causal, new_scores, MASKED)
-    live_rows = (jnp.arange(cache_rows, dtype=jnp.int32) < own_length)[None, None, :]
-    old_scores = (
-        jnp.einsum("qhd,khd->qhk", queries, cache_keys, preferred_element_type=jnp.float32)
-        * score_scale
-    )
-    old_scores = jnp.where(live_rows, old_scores, MASKED)
-    row_max = jnp.maximum(jnp.max(new_scores, axis=-1), jnp.max(old_scores, axis=-1))
-    new_probs = jnp.exp(new_scores - row_max[..., None])
-    old_probs = jnp.exp(old_scores - row_max[..., None])
-    denominator = jnp.sum(new_probs, axis=-1) + jnp.sum(old_probs, axis=-1)
-    weighted = jnp.einsum(
-        "qhk,khd->qhd",
-        new_probs.astype(jnp.bfloat16),
-        new_values,
-        preferred_element_type=jnp.float32,
-    )
-    weighted = weighted + jnp.einsum(
-        "qhk,khd->qhd",
-        old_probs.astype(jnp.bfloat16),
-        cache_values,
-        preferred_element_type=jnp.float32,
-    )
-    attended = (
-        (weighted / denominator[..., None])
-        .astype(jnp.bfloat16)
-        .reshape(tokens_here, heads_here * HD)
-    )
-    projected = jnp.dot(attended, w_out, preferred_element_type=jnp.float32)
+    own_length = lax.dynamic_slice_in_dim(cache_len, request, 1, 0)
+    projected = attention_projected(own_length, query, key_new, value_new, cache_kv, w_out)
     attn_share = lax.psum_scatter(projected, "grp", scatter_dimension=1, tiled=True)
     after_cols = (resid.astype(jnp.float32) + attn_share).astype(jnp.bfloat16)
     after_full = lax.all_gather(after_cols, "grp", axis=1, tiled=True)

time: 224 us -> 222 us (level)
  Pallas kernels: 8.02 us -> 12.5 us
  local copies, waits for them, and re-layouts: 7.19 us -> 4.46 us
  matrix products: 4.11 us -> 1.68 us
    pallas_call x0 -> x1, Pallas kernels: none -> 4.52 us  [attention_projected(): pl.pallas_call(attention_kernel, grid=(1,), in_specs=[pl.BlockSpec(memory...]
    dot_general x5 -> x0, matrix products: 2.43 us -> none  [the longest x1 1.33 us: body(): projected = jnp.dot(attended, w_out, preferred_element_type=jnp.float32)]
where the time goes in v6:
time: 222 us; the launch traced here: 221 us
  waiting for transfers between devices  130 us (59%)
  blocking collectives  42.7 us (19%)
  between operations  13.9 us (6%)
  starting transfers between devices  12.5 us (6%)
  Pallas kernels  12.5 us (6%)
  local copies, waits for them, and re-layouts  4.46 us (2%)
  other arithmetic  3.48 us (2%)
    reduce_scatter x1, waiting for transfers between devices, body(): lax.psum_scatter(slice_out, 'grp', scatter_dimension=0, tiled=True)  44 us
    reduce_scatter x1, waiting for transfers between devices, body(): lax.psum_scatter(projected, 'grp', scatter_dimension=1, tiled=True)  38.6 us
    all_to_all x1, blocking collectives, body(): lax.all_to_all(outgoing, 'ep', split_axis=0, concat_axis=0, tiled=True)  30.6 us
    all_gather x1, waiting for transfers between devices, body(): gathered = lax.all_gather(arrived, 'grp', axis=0, tiled=False)  29.7 us
    all_to_all x1, waiting for transfers between devices, body(): lax.all_to_all(expert_out, 'ep', split_axis=0, concat_axis=0, tiled=True)  17.6 us
    all_to_all x1, starting transfers between devices, body(): lax.all_to_all(expert_out, 'ep', split_axis=0, concat_axis=0, tiled=True)  12.4 us
    all_gather x1, blocking collectives, body(): after_full = lax.all_gather(after_cols, 'grp', axis=1, tiled=True)  12.1 us
    pallas_call x1, Pallas kernels, expert_ffn(): pl.pallas_call(ffn_kernel, grid=(rows // row_tile,), in_specs=[pl.BlockSp...  8.02 us
  transfers between devices with their start and end apart: 4, of which 4 were waited for; matrix products, arithmetic and copies ran while one was open for 3% of the time, Pallas kernels for 0%

profile of v6, /device:TPU:7, one launch (start us, length us, event | category | flops | bytes accessed | tf_op | source)
XLA Modules:
  0.0 221.2 jit_solution(13279992478398331614)
XLA Ops:
  7.2 0.0 reduce-scatter.3.cloned.1.call-start
  7.2 1.3 dynamic_slice.6.len_ref
  8.5 4.5 %shard_map.131 = f32[128,2048]{1,0:T(8,128)} custom-call(s32[1]{0:T(128)} %dynamic_slice.6.len_ref, bf16[128,256]{1,0:T(8,128)(2,1)} %q_ref.1, bf16[128,256]{1,0:T(8,128)(2,1)} %kn_ref.1, bf16[128,256]{1,0:T(8,128)(2,1)} %vn_ref.1, bf16[2,1024,256]{2,1,0:T(8,128)(2,1)} %cache_ref.1, bf16[256,2048]{1,0:T(8,128)(2,1)} %wout_ref.1), custom_call_target="tpu_custom_call" | custom-call | tf_op jit(solution)/shard_map/pallas_call | solution.py:64
  13.1 0.0 all-gather.2.cloned.1.call-start
  13.1 0.1 copy.41
  13.2 0.1 eq.49
  13.3 0.1 eq.45
  13.5 1.2 reduce-window.6
  14.7 0.2 slice_reduce_fusion
  15.0 0.1 fusion.6
  15.1 0.1 reduce_sum.48
  15.2 0.1 copy.44
  15.3 0.4 fusion
  15.7 38.6 %reduce-scatter.3.cloned.1.call-done = f32[128,256]{1,0:T(8,128)} async-done(((f32[128,2048]{1,0:T(8,128)}), f32[128,256]{1,0:T(8,128)}) %reduce-scatter.3.cloned.1.call-update) | async-done | bytes 131088 | tf_op jit(solution)/shard_map/reduce_scatter | solution.py:139
  54.3 0.9 add_convert_fusion
  55.3 12.1 %all_gather.6 = bf16[128,2048]{1,0:T(8,128)(2,1)S(1)} all-gather(bf16[128,256]{1,0:T(8,128)(2,1)S(1)} %add_convert_fusion), channel_id=1, replica_groups=mesh['grp'=8,'ep'=64] {'grp'}, dimensions={1}, use_global_device_ids=true | all-gather | bytes 589824 | tf_op jit(solution)/shard_map/all_gather | solution.py:141
  67.4 0.2 fusion.1
  67.6 0.2 fusion.3
  67.8 0.4 convolution_convert_fusion
  68.1 30.6 %all_to_all.10 = bf16[64,16,256]{2,1,0:T(8,128)(2,1)} all-to-all(bf16[64,16,256]{2,1,0:T(8,128)(2,1)S(1)} %bitcast.33), channel_id=1, replica_groups=mesh['grp'=8,'ep'=64] {'ep'}, dimensions={0} | all-to-all | bytes 1048576 | tf_op jit(solution)/shard_map/all_to_all | solution.py:167
  98.8 0.0 all-gather.2.cloned.1.call-update
  98.8 0.0 reduce-scatter.5.cloned.1.call-start
  98.9 2.4 %copy.45 = bf16[1,2,2048,176]{3,2,1,0:T(8,128)(2,1)} copy(bf16[1,2,2048,176]{2,3,1,0:T(8,128)(2,1)S(1)} %copy-done.1) | data formatting | bytes 2883584 | tf_op args[10]
  101.3 29.7 %all-gather.2.cloned.1.call-done.x_ref = bf16[8,1024,256]{2,1,0:T(8,128)(2,1)} async-done(((bf16[1,1024,256]{2,1,0:T(8,128)(2,1)}), bf16[8,1024,256]{2,1,0:T(8,128)(2,1)}) %all-gather.2.cloned.1.call-update) | async-done | bytes 4194320 | tf_op jit(solution)/shard_map/all_gather | solution.py:170
  131.0 8.0 %shard_map.132 = bf16[8,1024,256]{2,1,0:T(8,128)(2,1)} custom-call(bf16[8,1024,256]{2,1,0:T(8,128)(2,1)} %all-gather.2.cloned.1.call-done.x_ref, bf16[2,2048,176]{2,1,0:T(8,128)(2,1)} %bitcast.30, bf16[176,2048]{1,0:T(8,128)(2,1)} %bitcast.34), custom_call_target="tpu_custom_call" | custom-call | tf_op jit(solution)/shard_map/pallas_call | solution.py:101
  139.0 0.0 reduce-scatter.5.cloned.1.call-update
  139.0 44.0 %reduce-scatter.5.cloned.1.call-done = bf16[1,1024,256]{2,1,0:T(8,128)(2,1)} async-done(((bf16[8,1024,256]{2,1,0:T(8,128)(2,1)}), bf16[1,1024,256]{2,1,0:T(8,128)(2,1)}) %reduce-scatter.5.cloned.1.call-update) | async-done | bytes 524304 | tf_op jit(solution)/shard_map/reduce_scatter | solution.py:172
  183.0 12.4 %all-to-all-start.1 = ((bf16[64,16,256]{2,1,0:T(8,128)(2,1)}), bf16[64,16,256]{2,1,0:T(8,128)(2,1)S(1)}, u32[]{:S(2)}, u32[]{:S(2)}) async-start(bf16[64,16,256]{2,1,0:T(8,128)(2,1)} %bitcast.35), calls=%async_computation.3 | async-start | bytes 1048576 | tf_op jit(solution)/shard_map/all_to_all | solution.py:174
  195.4 0.3 fusion.12
  195.8 0.3 select_reduce_fusion
  196.1 17.6 %all-to-all-done.1 = bf16[64,16,256]{2,1,0:T(8,128)(2,1)S(1)} async-done(((bf16[64,16,256]{2,1,0:T(8,128)(2,1)}), bf16[64,16,256]{2,1,0:T(8,128)(2,1)S(1)}, u32[]{:S(2)}, u32[]{:S(2)}) %all-to-all-start.1) | async-done | bytes 524320 | tf_op jit(solution)/shard_map/all_to_all | solution.py:174
  213.7 1.0 convolution_convert_fusion.1
  (23 shorter events, 0.2 us)
Async XLA Ops:
  7.2 188.2 %copy-start = (bf16[2048,64]{0,1:T(8,128)(2,1)S(1)}, bf16[2048,64]{0,1:T(8,128)(2,1)}, u32[]{:S(2)}) copy-start(bf16[2048,64]{0,1:T(8,128)(2,1)} %param.20) | copy-start | bytes 786436
  7.2 47.1 %reduce-scatter.3.cloned.1.call-start = ((), (), s32[]{:S(2)}) async-start(), calls=%async_computation.4 | async-start | bytes 1179648 | tf_op jit(solution)/shard_map/reduce_scatter | solution.py:139
  8.5 4.6 %copy-start.4 = (s32[128,4]{0,1:T(4,128)S(1)}, s32[128,4]{0,1:T(4,128)}, u32[]{:S(2)}) copy-start(s32[128,4]{0,1:T(4,128)} %param.21) | copy-start | bytes 6148
  8.5 4.9 %copy-start.5 = (bf16[2048]{0:T(1024)(128)(2,1)S(1)}, bf16[2048]{0:T(1024)(128)(2,1)}, u32[]{:S(2)}) copy-start(bf16[2048]{0:T(1024)(128)(2,1)} %param.19) | copy-start | bytes 12292
  8.5 45.8 %copy-start.3 = (bf16[128,256]{1,0:T(8,128)(2,1)S(1)}, bf16[128,256]{1,0:T(8,128)(2,1)}, u32[]{:S(2)}) copy-start(bf16[128,256]{1,0:T(8,128)(2,1)} %param.12) | copy-start | bytes 196612
  13.1 117.9 %all-gather.2.cloned.1.call-start = ((), (), s32[]{:S(2)}) async-start(), calls=%async_computation.5 | async-start | bytes 4718592 | tf_op jit(solution)/shard_map/all_gather | solution.py:170
  55.2 43.6 %copy-start.2 = (bf16[128,256]{1,0:T(8,128)(2,1)}, bf16[128,256]{1,0:T(8,128)(2,1)S(1)}, u32[]{:S(2)}) copy-start(bf16[128,256]{1,0:T(8,128)(2,1)S(1)} %add_convert_fusion) | copy-start | bytes 196612
  55.2 43.6 %copy-start.1 = (bf16[1,2,2048,176]{2,3,1,0:T(8,128)(2,1)S(1)}, bf16[1,2,2048,176]{2,3,1,0:T(8,128)(2,1)}, u32[]{:S(2)}) copy-start(bf16[1,2,2048,176]{2,3,1,0:T(8,128)(2,1)} %param.22) | copy-start | bytes 4325380
  98.8 84.2 %reduce-scatter.5.cloned.1.call-start = ((), (), s32[]{:S(2)}) async-start(), calls=%async_computation.6 | async-start | bytes 4718592 | tf_op jit(solution)/shard_map/reduce_scatter | solution.py:172
  183.0 30.7 %all-to-all-start.1 = ((bf16[64,16,256]{2,1,0:T(8,128)(2,1)}), bf16[64,16,256]{2,1,0:T(8,128)(2,1)S(1)}, u32[]{:S(2)}, u32[]{:S(2)}) async-start(bf16[64,16,256]{2,1,0:T(8,128)(2,1)} %bitcast.35), calls=%async_computation.3 | async-start | bytes 1048576 | tf_op jit(solution)/shard_map/all_to_all | solution.py:174
Sparse Core Ops, SparseCore 0:
  13.2 41.0 reduce-scatter.2
  98.9 32.0 all-gather.1
  139.1 43.7 reduce-scatter.4

commit v7 on v6

--- a/solution.py
+++ b/solution.py
@@ -14,10 +14,10 @@
 MASKED = -1e30
 
 
-def attention_kernel(len_ref, q_ref, kn_ref, vn_ref, cache_ref, wout_ref, out_ref):
+def attention_kernel(len_ref, q_ref, kn_ref, vn_ref, cache_ref, out_ref):
     tokens, width = q_ref.shape
     cache_rows = cache_ref.shape[1]
-    length = len_ref[0]
+    length = len_ref[lax.axis_index("ep")]
     score_scale = float(HD) ** (-0.5)
     contract_last = (((1,), (1,)), ((), ()))
     causal = lax.broadcasted_iota(jnp.int32, (tokens, tokens), 0) >= lax.broadcasted_iota(
@@ -54,12 +54,10 @@
             old_probs.astype(jnp.bfloat16), cache_ref[1, :, cols], preferred_element_type=jnp.float32
         )
         heads.append((weighted / denominator).astype(jnp.bfloat16))
-    attended = jnp.concatenate(heads, axis=1)
-    out_ref[...] = jnp.dot(attended, wout_ref[...], preferred_element_type=jnp.float32)
-
-
-def attention_projected(own_length, query, key_new, value_new, cache_kv, w_out):
-    tokens = query.shape[0]
+    out_ref[...] = jnp.concatenate(heads, axis=1)
+
+
+def attention(cache_len, query, key_new, value_new, cache_kv):
     whole = lambda shape: pl.BlockSpec(shape, lambda i: (0,) * len(shape))
     return pl.pallas_call(
         attention_kernel,
@@ -70,11 +68,10 @@
             whole(key_new.shape),
             whole(value_new.shape),
             whole(cache_kv.shape),
-            whole(w_out.shape),
         ],
-        out_specs=whole((tokens, w_out.shape[1])),
-        out_shape=jax.ShapeDtypeStruct((tokens, w_out.shape[1]), jnp.float32),
-    )(own_length, query, key_new, value_new, cache_kv, w_out)
+        out_specs=whole(query.shape),
+        out_shape=jax.ShapeDtypeStruct(query.shape, jnp.bfloat16),
+    )(cache_len, query, key_new, value_new, cache_kv)
 
 
 def ffn_kernel(x_ref, gu_ref, down_ref, out_ref):
@@ -134,9 +131,13 @@
     capacity = max(2, 8 * tokens_here // lax.axis_size("ep"))
     score_scale = float(HD) ** (-0.5)
     column_start = group_index * column_width
-    own_length = lax.dynamic_slice_in_dim(cache_len, request, 1, 0)
-    projected = attention_projected(own_length, query, key_new, value_new, cache_kv, w_out)
-    attn_share = lax.psum_scatter(projected, "grp", scatter_dimension=1, tiled=True)
+    groups = lax.axis_size("grp")
+    out_blocks = w_out.reshape(w_out.shape[0], groups, column_width)
+    out_cols = lax.all_to_all(out_blocks, "grp", split_axis=1, concat_axis=0, tiled=True)
+    out_cols = out_cols.reshape(groups * w_out.shape[0], column_width)
+    attended = attention(cache_len, query, key_new, value_new, cache_kv)
+    attended_full = lax.all_gather(attended, "grp", axis=1, tiled=True)
+    attn_share = jnp.dot(attended_full, out_cols, preferred_element_type=jnp.float32)
     after_cols = (resid.astype(jnp.float32) + attn_share).astype(jnp.bfloat16)
     after_full = lax.all_gather(after_cols, "grp", axis=1, tiled=True)
     after_wide = after_full.astype(jnp.float32)
@@ -166,7 +167,6 @@
     outgoing = outgoing.reshape(experts_all, capacity, column_width)
     arrived = lax.all_to_all(outgoing, "ep", split_axis=0, concat_axis=0, tiled=True)
     arrived = arrived.reshape(experts_all * capacity, column_width)
-    groups = lax.axis_size("grp")
     gathered = lax.all_gather(arrived, "grp", axis=0, tiled=False)
     slice_out = expert_ffn(gathered, w_gate_up[0], w_down[0])
     expert_out = lax.psum_scatter(slice_out, "grp", scatter_dimension=0, tiled=True)

time: 222 us -> 208 us (0.937)
  waiting for transfers between devices: 130 us -> 90.1 us
  blocking collectives: 42.7 us -> 59.2 us
  starting transfers between devices: 12.5 us -> 22.1 us
    reduce_scatter x1 -> x0, waiting for transfers between devices: 38.6 us -> none  [body(): lax.psum_scatter(projected, 'grp', scatter_dimension=1, tiled=True)]
    all_gather x0 -> x1, blocking collectives: none -> 16.5 us  [body(): attended_full = lax.all_gather(attended, 'grp', axis=1, tiled=True)]
    all_to_all x0 -> x1, starting transfers between devices: none -> 9.66 us  [body(): lax.all_to_all(out_blocks, 'grp', split_axis=1, concat_axis=0, tiled=True)]
    unnamed x14 -> x15, local copies, waits for them, and re-layouts: 2.57 us -> 4.89 us
  transfers between devices with their start and end apart: 4 -> 4, of which waited for: 4 -> 3; matrix products, arithmetic and copies ran while one was open for 3% -> 3% of each run, Pallas kernels for 0% -> 1%
where the time goes in v7:
time: 208 us; the launch traced here: 207 us
  waiting for transfers between devices  90.1 us (43%)
  blocking collectives  59.2 us (28%)
  starting transfers between devices  22.1 us (11%)
  between operations  14.2 us (7%)
  Pallas kernels  11 us (5%)
  local copies, waits for them, and re-layouts  6.02 us (3%)
  other arithmetic  2.54 us (1%)
    reduce_scatter x1, waiting for transfers between devices, body(): lax.psum_scatter(slice_out, 'grp', scatter_dimension=0, tiled=True)  44 us
    all_to_all x1, blocking collectives, body(): lax.all_to_all(outgoing, 'ep', split_axis=0, concat_axis=0, tiled=True)  29.5 us
    all_gather x1, waiting for transfers between devices, body(): gathered = lax.all_gather(arrived, 'grp', axis=0, tiled=False)  28.6 us
    all_to_all x1, waiting for transfers between devices, body(): lax.all_to_all(expert_out, 'ep', split_axis=0, concat_axis=0, tiled=True)  17.5 us
    all_gather x1, blocking collectives, body(): attended_full = lax.all_gather(attended, 'grp', axis=1, tiled=True)  16.5 us
    all_gather x1, blocking collectives, body(): after_full = lax.all_gather(after_cols, 'grp', axis=1, tiled=True)  13.2 us
    all_to_all x1, starting transfers between devices, body(): lax.all_to_all(expert_out, 'ep', split_axis=0, concat_axis=0, tiled=True)  12.4 us
    all_to_all x1, starting transfers between devices, body(): lax.all_to_all(out_blocks, 'grp', split_axis=1, concat_axis=0, tiled=True)  9.66 us
  transfers between devices with their start and end apart: 4, of which 3 were waited for; matrix products, arithmetic and copies ran while one was open for 3% of the time, Pallas kernels for 1%

profile of v7, /device:TPU:7, one launch (start us, length us, event | category | flops | bytes accessed | tf_op | source)
XLA Modules:
  0.0 207.2 jit_solution(9576496446468646888)
XLA Ops:
  7.2 2.3 %copy.55 = bf16[256,2048]{0,1:T(8,128)(2,1)} copy(bf16[256,2048]{1,0:T(8,128)(2,1)} %param.18) | data formatting | bytes 2097152 | tf_op args[6]
  9.5 9.7 %all-to-all-start = ((bf16[256,8,256]{0,2,1:T(8,128)(2,1)}), bf16[256,8,256]{0,2,1:T(8,128)(2,1)S(1)}, u32[]{:S(2)}, u32[]{:S(2)}) async-start(bf16[256,8,256]{0,2,1:T(8,128)(2,1)} %bitcast), calls=%async_computation | async-start | bytes 2097152 | tf_op jit(solution)/shard_map/all_to_all | solution.py:136
  19.2 0.1 copy.57
  19.3 0.1 eq.49
  19.4 0.1 eq.45
  19.6 1.2 reduce-window.6
  20.8 0.2 slice_reduce_fusion
  21.0 0.1 fusion.7
  21.2 0.1 reduce_sum.48
  21.3 0.1 copy.60
  21.4 3.0 %shard_map.131 = bf16[128,256]{1,0:T(8,128)(2,1)} custom-call(s32[64]{0:T(128)} %len_ref.1, bf16[128,256]{1,0:T(8,128)(2,1)} %q_ref.1, bf16[128,256]{1,0:T(8,128)(2,1)} %kn_ref.1, bf16[128,256]{1,0:T(8,128)(2,1)} %vn_ref.1, bf16[2,1024,256]{2,1,0:T(8,128)(2,1)} %cache_ref.1), custom_call_target="tpu_custom_call" | custom-call | tf_op jit(solution)/shard_map/pallas_call | solution.py:62
  24.3 0.4 fusion
  24.7 16.5 %all_gather.9 = bf16[128,2048]{1,0:T(8,128)(2,1)S(1)} all-gather(bf16[128,256]{1,0:T(8,128)(2,1)} %shard_map.131), channel_id=1, replica_groups=mesh['grp'=8,'ep'=64] {'grp'}, dimensions={1}, use_global_device_ids=true | all-gather | bytes 589824 | tf_op jit(solution)/shard_map/all_gather | solution.py:139
  41.3 0.5 copy.56
  41.8 0.3 fusion.1
  42.1 13.2 %all_gather.10 = bf16[128,2048]{1,0:T(8,128)(2,1)S(1)} all-gather(bf16[128,256]{1,0:T(8,128)(2,1)S(1)} %fusion.1), channel_id=1, replica_groups=mesh['grp'=8,'ep'=64] {'grp'}, dimensions={1}, use_global_device_ids=true | all-gather | bytes 589824 | tf_op jit(solution)/shard_map/all_gather | solution.py:142
  55.4 0.2 fusion.2
  55.6 0.2 fusion.4
  55.8 0.4 convolution_convert_fusion
  56.1 29.5 %all_to_all.25 = bf16[64,16,256]{2,1,0:T(8,128)(2,1)} all-to-all(bf16[64,16,256]{2,1,0:T(8,128)(2,1)S(1)} %bitcast.42), channel_id=1, replica_groups=mesh['grp'=8,'ep'=64] {'ep'}, dimensions={0} | all-to-all | bytes 1048576 | tf_op jit(solution)/shard_map/all_to_all | solution.py:168
  85.6 0.0 all-gather.2.cloned.1.call-update
  85.6 0.0 reduce-scatter.2.cloned.1.call-start
  85.7 2.4 %copy.61 = bf16[1,2,2048,176]{3,2,1,0:T(8,128)(2,1)} copy(bf16[1,2,2048,176]{2,3,1,0:T(8,128)(2,1)S(1)} %copy-done.1) | data formatting | bytes 2883584 | tf_op args[10]
  88.1 28.6 %all-gather.2.cloned.1.call-done.x_ref = bf16[8,1024,256]{2,1,0:T(8,128)(2,1)} async-done(((bf16[1,1024,256]{2,1,0:T(8,128)(2,1)}), bf16[8,1024,256]{2,1,0:T(8,128)(2,1)}) %all-gather.2.cloned.1.call-update) | async-done | bytes 4194320 | tf_op jit(solution)/shard_map/all_gather | solution.py:170
  116.7 8.0 %shard_map.132 = bf16[8,1024,256]{2,1,0:T(8,128)(2,1)} custom-call(bf16[8,1024,256]{2,1,0:T(8,128)(2,1)} %all-gather.2.cloned.1.call-done.x_ref, bf16[2,2048,176]{2,1,0:T(8,128)(2,1)} %bitcast.37, bf16[176,2048]{1,0:T(8,128)(2,1)} %bitcast.43), custom_call_target="tpu_custom_call" | custom-call | tf_op jit(solution)/shard_map/pallas_call | solution.py:98
  124.8 0.0 reduce-scatter.2.cloned.1.call-update
  124.8 44.0 %reduce-scatter.2.cloned.1.call-done = bf16[1,1024,256]{2,1,0:T(8,128)(2,1)} async-done(((bf16[8,1024,256]{2,1,0:T(8,128)(2,1)}), bf16[1,1024,256]{2,1,0:T(8,128)(2,1)}) %reduce-scatter.2.cloned.1.call-update) | async-done | bytes 524304 | tf_op jit(solution)/shard_map/reduce_scatter | solution.py:172
  168.7 12.4 %all-to-all-start.2 = ((bf16[64,16,256]{2,1,0:T(8,128)(2,1)}), bf16[64,16,256]{2,1,0:T(8,128)(2,1)S(1)}, u32[]{:S(2)}, u32[]{:S(2)}) async-start(bf16[64,16,256]{2,1,0:T(8,128)(2,1)} %bitcast.44), calls=%async_computation.3 | async-start | bytes 1048576 | tf_op jit(solution)/shard_map/all_to_all | solution.py:174
  181.2 0.3 fusion.13
  181.5 0.3 select_reduce_fusion
  181.9 17.5 %all-to-all-done.2 = bf16[64,16,256]{2,1,0:T(8,128)(2,1)S(1)} async-done(((bf16[64,16,256]{2,1,0:T(8,128)(2,1)}), bf16[64,16,256]{2,1,0:T(8,128)(2,1)S(1)}, u32[]{:S(2)}, u32[]{:S(2)}) %all-to-all-start.2) | async-done | bytes 524320 | tf_op jit(solution)/shard_map/all_to_all | solution.py:174
  199.3 1.0 convolution_convert_fusion.1
  (24 shorter events, 0.2 us)
Async XLA Ops:
  7.2 174.0 %copy-start = (bf16[2048,64]{0,1:T(8,128)(2,1)S(1)}, bf16[2048,64]{0,1:T(8,128)(2,1)}, u32[]{:S(2)}) copy-start(bf16[2048,64]{0,1:T(8,128)(2,1)} %param.20) | copy-start | bytes 786436
  7.2 12.0 %copy-start.4 = (s32[128,4]{0,1:T(4,128)S(1)}, s32[128,4]{0,1:T(4,128)}, u32[]{:S(2)}) copy-start(s32[128,4]{0,1:T(4,128)} %param.21) | copy-start | bytes 6148
  7.2 12.4 %copy-start.5 = (bf16[2048]{0:T(1024)(128)(2,1)S(1)}, bf16[2048]{0:T(1024)(128)(2,1)}, u32[]{:S(2)}) copy-start(bf16[2048]{0:T(1024)(128)(2,1)} %param.19) | copy-start | bytes 12292
  9.5 31.7 %all-to-all-start = ((bf16[256,8,256]{0,2,1:T(8,128)(2,1)}), bf16[256,8,256]{0,2,1:T(8,128)(2,1)S(1)}, u32[]{:S(2)}, u32[]{:S(2)}) async-start(bf16[256,8,256]{0,2,1:T(8,128)(2,1)} %bitcast), calls=%async_computation | async-start | bytes 2097152 | tf_op jit(solution)/shard_map/all_to_all | solution.py:136
  19.2 97.6 %all-gather.2.cloned.1.call-start = ((), (), s32[]{:S(2)}) async-start(), calls=%async_computation.4 | async-start | bytes 4718592 | tf_op jit(solution)/shard_map/all_gather | solution.py:170
  21.3 20.5 %copy-start.3 = (bf16[128,256]{1,0:T(8,128)(2,1)S(1)}, bf16[128,256]{1,0:T(8,128)(2,1)}, u32[]{:S(2)}) copy-start(bf16[128,256]{1,0:T(8,128)(2,1)} %param.12) | copy-start | bytes 196612
  42.1 43.5 %copy-start.2 = (bf16[128,256]{1,0:T(8,128)(2,1)}, bf16[128,256]{1,0:T(8,128)(2,1)S(1)}, u32[]{:S(2)}) copy-start(bf16[128,256]{1,0:T(8,128)(2,1)S(1)} %fusion.1) | copy-start | bytes 196612
  42.1 43.6 %copy-start.1 = (bf16[1,2,2048,176]{2,3,1,0:T(8,128)(2,1)S(1)}, bf16[1,2,2048,176]{2,3,1,0:T(8,128)(2,1)}, u32[]{:S(2)}) copy-start(bf16[1,2,2048,176]{2,3,1,0:T(8,128)(2,1)} %param.22) | copy-start | bytes 4325380
  85.6 83.1 %reduce-scatter.2.cloned.1.call-start = ((), (), s32[]{:S(2)}) async-start(), calls=%async_computation.5 | async-start | bytes 4718592 | tf_op jit(solution)/shard_map/reduce_scatter | solution.py:172
  168.7 30.6 %all-to-all-start.2 = ((bf16[64,16,256]{2,1,0:T(8,128)(2,1)}), bf16[64,16,256]{2,1,0:T(8,128)(2,1)S(1)}, u32[]{:S(2)}, u32[]{:S(2)}) async-start(bf16[64,16,256]{2,1,0:T(8,128)(2,1)} %bitcast.44), calls=%async_computation.3 | async-start | bytes 1048576 | tf_op jit(solution)/shard_map/all_to_all | solution.py:174
Sparse Core Ops, SparseCore 0:
  85.7 30.9 all-gather.1
  124.9 43.7 reduce-scatter.1

commit v8 on v7

--- a/solution.py
+++ b/solution.py
@@ -74,12 +74,17 @@
     )(cache_len, query, key_new, value_new, cache_kv)
 
 
-def ffn_kernel(x_ref, gu_ref, down_ref, out_ref):
+def ffn_kernel(x_ref, gain_ref, gu_ref, down_ref, out_ref):
     groups, rows, width = x_ref.shape
+    squares = jnp.zeros((rows, 1), jnp.float32)
+    for g in range(groups):
+        wide = x_ref[g].astype(jnp.float32)
+        squares = squares + jnp.sum(wide * wide, axis=1, keepdims=True)
+    inverse = lax.rsqrt(squares / D + EPS)
     gate = jnp.zeros((rows, gu_ref.shape[-1]), jnp.float32)
     up = jnp.zeros((rows, gu_ref.shape[-1]), jnp.float32)
     for g in range(groups):
-        x = x_ref[g]
+        x = (x_ref[g].astype(jnp.float32) * inverse * gain_ref[g:g + 1, :]).astype(jnp.bfloat16)
         gate = gate + jnp.dot(
             x, gu_ref[0, g * width:(g + 1) * width, :], preferred_element_type=jnp.float32
         )
@@ -93,19 +98,20 @@
         ).astype(out_ref.dtype)
 
 
-def expert_ffn(gathered, gate_up, down, row_tile=256):
+def expert_ffn(gathered, gain_blocks, gate_up, down, row_tile=256):
     groups, rows, width = gathered.shape
     return pl.pallas_call(
         ffn_kernel,
         grid=(rows // row_tile,),
         in_specs=[
             pl.BlockSpec((groups, row_tile, width), lambda i: (0, i, 0)),
+            pl.BlockSpec(gain_blocks.shape, lambda i: (0, 0)),
             pl.BlockSpec(gate_up.shape, lambda i: (0, 0, 0)),
             pl.BlockSpec(down.shape, lambda i: (0, 0)),
         ],
         out_specs=pl.BlockSpec((groups, row_tile, width), lambda i: (0, i, 0)),
         out_shape=jax.ShapeDtypeStruct(gathered.shape, jnp.bfloat16),
-    )(gathered, gate_up, down)
+    )(gathered, gain_blocks, gate_up, down)
 
 
 def body(
@@ -146,7 +152,6 @@
     normed_full = (
         after_wide * inverse[:, None] * norm_gain.astype(jnp.float32)[None, :]
     ).astype(jnp.bfloat16)
-    normed_cols = lax.dynamic_slice_in_dim(normed_full, column_start, column_width, 1)
     logits = jnp.dot(normed_full, w_router, preferred_element_type=jnp.float32)
     route_hits = routes[:, :, None] == jnp.arange(experts_all, dtype=jnp.int32)[None, None, :]
     chosen = jnp.sum(jnp.where(route_hits, logits[:, None, :], 0.0), axis=-1)
@@ -162,13 +167,14 @@
         jnp.where(matches, route_weight[:, :, None].astype(jnp.float32), 0.0), axis=1
     )
     outgoing = jnp.einsum(
-        "tj,td->jd", selection, normed_cols, preferred_element_type=jnp.float32
+        "tj,td->jd", selection, after_cols, preferred_element_type=jnp.float32
     ).astype(jnp.bfloat16)
     outgoing = outgoing.reshape(experts_all, capacity, column_width)
     arrived = lax.all_to_all(outgoing, "ep", split_axis=0, concat_axis=0, tiled=True)
     arrived = arrived.reshape(experts_all * capacity, column_width)
     gathered = lax.all_gather(arrived, "grp", axis=0, tiled=False)
-    slice_out = expert_ffn(gathered, w_gate_up[0], w_down[0])
+    gain_blocks = norm_gain.astype(jnp.float32).reshape(groups, column_width)
+    slice_out = expert_ffn(gathered, gain_blocks, w_gate_up[0], w_down[0])
     expert_out = lax.psum_scatter(slice_out, "grp", scatter_dimension=0, tiled=True)
     expert_out = expert_out.reshape(experts_all, capacity, column_width)
     returned = lax.all_to_all(expert_out, "ep", split_axis=0, concat_axis=0, tiled=True)

time: 208 us -> 196 us (0.942)
  waiting for transfers between devices: 90.1 us -> 76.1 us
    reduce_scatter x1, waiting for transfers between devices: 44 us -> 30.5 us  [body(): lax.psum_scatter(slice_out, 'grp', scatter_dimension=0, tiled=True)]
  transfers between devices with their start and end apart: 4 -> 4, of which waited for: 3 -> 3; matrix products, arithmetic and copies ran while one was open for 3% -> 3% of each run, Pallas kernels for 1% -> 2%
where the time goes in v8:
time: 196 us; the launch traced here: 195 us
  waiting for transfers between devices  76.1 us (39%)
  blocking collectives  59.4 us (30%)
  starting transfers between devices  22.1 us (11%)
  between operations  14.2 us (7%)
  Pallas kernels  11.8 us (6%)
  local copies, waits for them, and re-layouts  6.61 us (3%)
  other arithmetic  2.34 us (1%)
  matrix products  2.05 us (1%)
    reduce_scatter x1, waiting for transfers between devices, body(): lax.psum_scatter(slice_out, 'grp', scatter_dimension=0, tiled=True)  30.5 us
    all_to_all x1, blocking collectives, body(): lax.all_to_all(outgoing, 'ep', split_axis=0, concat_axis=0, tiled=True)  29.6 us
    all_gather x1, waiting for transfers between devices, body(): gathered = lax.all_gather(arrived, 'grp', axis=0, tiled=False)  28.1 us
    all_to_all x1, waiting for transfers between devices, body(): lax.all_to_all(expert_out, 'ep', split_axis=0, concat_axis=0, tiled=True)  17.5 us
    all_gather x1, blocking collectives, body(): attended_full = lax.all_gather(attended, 'grp', axis=1, tiled=True)  16.6 us
    all_gather x1, blocking collectives, body(): after_full = lax.all_gather(after_cols, 'grp', axis=1, tiled=True)  13.2 us
    all_to_all x1, starting transfers between devices, body(): lax.all_to_all(expert_out, 'ep', split_axis=0, concat_axis=0, tiled=True)  12.4 us
    all_to_all x1, starting transfers between devices, body(): lax.all_to_all(out_blocks, 'grp', split_axis=1, concat_axis=0, tiled=True)  9.66 us
  transfers between devices with their start and end apart: 4, of which 3 were waited for; matrix products, arithmetic and copies ran while one was open for 3% of the time, Pallas kernels for 2%

profile of v8, /device:TPU:7, one launch (start us, length us, event | category | flops | bytes accessed | tf_op | source)
XLA Modules:
  0.0 194.6 jit_solution(7665901173901629621)
XLA Ops:
  7.2 2.3 %copy.55 = bf16[256,2048]{0,1:T(8,128)(2,1)} copy(bf16[256,2048]{1,0:T(8,128)(2,1)} %param.18) | data formatting | bytes 2097152 | tf_op args[6]
  9.5 9.7 %all-to-all-start = ((bf16[256,8,256]{0,2,1:T(8,128)(2,1)}), bf16[256,8,256]{0,2,1:T(8,128)(2,1)S(1)}, u32[]{:S(2)}, u32[]{:S(2)}) async-start(bf16[256,8,256]{0,2,1:T(8,128)(2,1)} %bitcast), calls=%async_computation | async-start | bytes 2097152 | tf_op jit(solution)/shard_map/all_to_all | solution.py:142
  19.2 0.1 copy.57
  19.3 0.1 eq.49
  19.4 0.1 eq.45
  19.5 1.2 reduce-window.6
  20.7 0.2 slice_reduce_fusion
  21.0 0.1 fusion.11
  21.1 0.1 reduce_sum.48
  21.3 0.1 copy.60
  21.3 3.0 %shard_map.131 = bf16[128,256]{1,0:T(8,128)(2,1)} custom-call(s32[64]{0:T(128)} %len_ref.1, bf16[128,256]{1,0:T(8,128)(2,1)} %q_ref.1, bf16[128,256]{1,0:T(8,128)(2,1)} %kn_ref.1, bf16[128,256]{1,0:T(8,128)(2,1)} %vn_ref.1, bf16[2,1024,256]{2,1,0:T(8,128)(2,1)} %cache_ref.1), custom_call_target="tpu_custom_call" | custom-call | tf_op jit(solution)/shard_map/pallas_call | solution.py:62
  24.3 0.4 fusion
  24.7 16.6 %all_gather.9 = bf16[128,2048]{1,0:T(8,128)(2,1)S(1)} all-gather(bf16[128,256]{1,0:T(8,128)(2,1)} %shard_map.131), channel_id=1, replica_groups=mesh['grp'=8,'ep'=64] {'grp'}, dimensions={1}, use_global_device_ids=true | all-gather | bytes 589824 | tf_op jit(solution)/shard_map/all_gather | solution.py:145
  41.2 0.5 copy.56
  41.8 0.3 fusion.1
  42.1 0.4 convolution_convert_fusion
  42.5 29.6 %all_to_all.25 = bf16[64,16,256]{2,1,0:T(8,128)(2,1)} all-to-all(bf16[64,16,256]{2,1,0:T(8,128)(2,1)S(1)} %bitcast.42), channel_id=1, replica_groups=mesh['grp'=8,'ep'=64] {'ep'}, dimensions={0} | all-to-all | bytes 1048576 | tf_op jit(solution)/shard_map/all_to_all | solution.py:173
  72.1 0.0 all-gather.2.cloned.1.call-update
  72.1 0.0 reduce-scatter.2.cloned.1.call-start
  72.2 0.6 reshape.97.gain_ref
  72.8 2.4 %copy.61 = bf16[1,2,2048,176]{3,2,1,0:T(8,128)(2,1)} copy(bf16[1,2,2048,176]{2,3,1,0:T(8,128)(2,1)S(1)} %copy-done.1) | data formatting | bytes 2883584 | tf_op args[10]
  75.2 28.1 %all-gather.2.cloned.1.call-done.x_ref = bf16[8,1024,256]{2,1,0:T(8,128)(2,1)} async-done(((bf16[1,1024,256]{2,1,0:T(8,128)(2,1)}), bf16[8,1024,256]{2,1,0:T(8,128)(2,1)}) %all-gather.2.cloned.1.call-update) | async-done | bytes 4194320 | tf_op jit(solution)/shard_map/all_gather | solution.py:175
  103.2 8.8 %shard_map.132 = bf16[8,1024,256]{2,1,0:T(8,128)(2,1)} custom-call(bf16[8,1024,256]{2,1,0:T(8,128)(2,1)} %all-gather.2.cloned.1.call-done.x_ref, f32[8,256]{1,0:T(8,128)} %reshape.97.gain_ref, bf16[2,2048,176]{2,1,0:T(8,128)(2,1)} %bitcast.37, bf16[176,2048]{1,0:T(8,128)(2,1)} %bitcast.43), custom_call_target="tpu_custom_call" | custom-call | tf_op jit(solution)/shard_map/pallas_call | solution.py:103
  112.1 0.0 reduce-scatter.2.cloned.1.call-update
  112.1 13.2 %all_gather.10 = bf16[128,2048]{1,0:T(8,128)(2,1)S(1)} all-gather(bf16[128,256]{1,0:T(8,128)(2,1)S(1)} %fusion.1), channel_id=1, replica_groups=mesh['grp'=8,'ep'=64] {'grp'}, dimensions={1}, use_global_device_ids=true | all-gather | bytes 589824 | tf_op jit(solution)/shard_map/all_gather | solution.py:148
  125.3 0.2 fusion.2
  125.5 30.5 %reduce-scatter.2.cloned.1.call-done = bf16[1,1024,256]{2,1,0:T(8,128)(2,1)} async-done(((bf16[8,1024,256]{2,1,0:T(8,128)(2,1)}), bf16[1,1024,256]{2,1,0:T(8,128)(2,1)}) %reduce-scatter.2.cloned.1.call-update) | async-done | bytes 524304 | tf_op jit(solution)/shard_map/reduce_scatter | solution.py:178
  156.0 12.4 %all-to-all-start.2 = ((bf16[64,16,256]{2,1,0:T(8,128)(2,1)}), bf16[64,16,256]{2,1,0:T(8,128)(2,1)S(1)}, u32[]{:S(2)}, u32[]{:S(2)}) async-start(bf16[64,16,256]{2,1,0:T(8,128)(2,1)} %bitcast.44), calls=%async_computation.3 | async-start | bytes 1048576 | tf_op jit(solution)/shard_map/all_to_all | solution.py:180
  168.5 0.4 fusion.5
  168.9 0.3 select_reduce_fusion
  169.2 17.5 %all-to-all-done.2 = bf16[64,16,256]{2,1,0:T(8,128)(2,1)S(1)} async-done(((bf16[64,16,256]{2,1,0:T(8,128)(2,1)}), bf16[64,16,256]{2,1,0:T(8,128)(2,1)S(1)}, u32[]{:S(2)}, u32[]{:S(2)}) %all-to-all-start.2) | async-done | bytes 524320 | tf_op jit(solution)/shard_map/all_to_all | solution.py:180
  186.8 1.0 convolution_convert_fusion.1
  (24 shorter events, 0.2 us)
Async XLA Ops:
  7.2 161.3 %copy-start = (bf16[2048,64]{0,1:T(8,128)(2,1)S(1)}, bf16[2048,64]{0,1:T(8,128)(2,1)}, u32[]{:S(2)}) copy-start(bf16[2048,64]{0,1:T(8,128)(2,1)} %param.20) | copy-start | bytes 786436
  7.2 12.0 %copy-start.4 = (s32[128,4]{0,1:T(4,128)S(1)}, s32[128,4]{0,1:T(4,128)}, u32[]{:S(2)}) copy-start(s32[128,4]{0,1:T(4,128)} %param.21) | copy-start | bytes 6148
  9.5 31.7 %all-to-all-start = ((bf16[256,8,256]{0,2,1:T(8,128)(2,1)}), bf16[256,8,256]{0,2,1:T(8,128)(2,1)S(1)}, u32[]{:S(2)}, u32[]{:S(2)}) async-start(bf16[256,8,256]{0,2,1:T(8,128)(2,1)} %bitcast), calls=%async_computation | async-start | bytes 2097152 | tf_op jit(solution)/shard_map/all_to_all | solution.py:142
  19.2 84.1 %all-gather.2.cloned.1.call-start = ((), (), s32[]{:S(2)}) async-start(), calls=%async_computation.4 | async-start | bytes 4718592 | tf_op jit(solution)/shard_map/all_gather | solution.py:175
  21.3 20.5 %copy-start.3 = (bf16[128,256]{1,0:T(8,128)(2,1)S(1)}, bf16[128,256]{1,0:T(8,128)(2,1)}, u32[]{:S(2)}) copy-start(bf16[128,256]{1,0:T(8,128)(2,1)} %param.12) | copy-start | bytes 196612
  41.8 30.4 %copy-start.5 = (bf16[2048]{0:T(1024)(128)(2,1)S(1)}, bf16[2048]{0:T(1024)(128)(2,1)}, u32[]{:S(2)}) copy-start(bf16[2048]{0:T(1024)(128)(2,1)} %param.19) | copy-start | bytes 12292
  42.1 70.0 %copy-start.2 = (bf16[128,256]{1,0:T(8,128)(2,1)}, bf16[128,256]{1,0:T(8,128)(2,1)S(1)}, u32[]{:S(2)}) copy-start(bf16[128,256]{1,0:T(8,128)(2,1)S(1)} %fusion.1) | copy-start | bytes 196612
  42.1 30.7 %copy-start.1 = (bf16[1,2,2048,176]{2,3,1,0:T(8,128)(2,1)S(1)}, bf16[1,2,2048,176]{2,3,1,0:T(8,128)(2,1)}, u32[]{:S(2)}) copy-start(bf16[1,2,2048,176]{2,3,1,0:T(8,128)(2,1)} %param.22) | copy-start | bytes 4325380
  72.1 83.9 %reduce-scatter.2.cloned.1.call-start = ((), (), s32[]{:S(2)}) async-start(), calls=%async_computation.5 | async-start | bytes 4718592 | tf_op jit(solution)/shard_map/reduce_scatter | solution.py:178
  156.0 30.7 %all-to-all-start.2 = ((bf16[64,16,256]{2,1,0:T(8,128)(2,1)}), bf16[64,16,256]{2,1,0:T(8,128)(2,1)S(1)}, u32[]{:S(2)}, u32[]{:S(2)}) async-start(bf16[64,16,256]{2,1,0:T(8,128)(2,1)} %bitcast.44), calls=%async_computation.3 | async-start | bytes 1048576 | tf_op jit(solution)/shard_map/all_to_all | solution.py:180
Sparse Core Ops, SparseCore 0:
  72.2 30.9 all-gather.1
  112.2 43.7 reduce-scatter.1

commit v9 on v8

--- a/solution.py
+++ b/solution.py
@@ -74,6 +74,24 @@
     )(cache_len, query, key_new, value_new, cache_kv)
 
 
+def blocks_kernel(x_ref, out_ref):
+    width = out_ref.shape[-1]
+    for j in range(out_ref.shape[0]):
+        out_ref[j] = x_ref[:, j * width:(j + 1) * width]
+
+
+def column_blocks(matrix, groups):
+    rows, cols = matrix.shape
+    shape = (groups, rows, cols // groups)
+    return pl.pallas_call(
+        blocks_kernel,
+        grid=(1,),
+        in_specs=[pl.BlockSpec(matrix.shape, lambda i: (0, 0))],
+        out_specs=pl.BlockSpec(shape, lambda i: (0, 0, 0)),
+        out_shape=jax.ShapeDtypeStruct(shape, matrix.dtype),
+    )(matrix)
+
+
 def ffn_kernel(x_ref, gain_ref, gu_ref, down_ref, out_ref):
     groups, rows, width = x_ref.shape
     squares = jnp.zeros((rows, 1), jnp.float32)
@@ -81,15 +99,18 @@
         wide = x_ref[g].astype(jnp.float32)
         squares = squares + jnp.sum(wide * wide, axis=1, keepdims=True)
     inverse = lax.rsqrt(squares / D + EPS)
-    gate = jnp.zeros((rows, gu_ref.shape[-1]), jnp.float32)
-    up = jnp.zeros((rows, gu_ref.shape[-1]), jnp.float32)
+    gate = jnp.zeros((rows, gu_ref.shape[1]), jnp.float32)
+    up = jnp.zeros((rows, gu_ref.shape[1]), jnp.float32)
+    contract_last = (((1,), (1,)), ((), ()))
     for g in range(groups):
         x = (x_ref[g].astype(jnp.float32) * inverse * gain_ref[g:g + 1, :]).astype(jnp.bfloat16)
-        gate = gate + jnp.dot(
-            x, gu_ref[0, g * width:(g + 1) * width, :], preferred_element_type=jnp.float32
-        )
-        up = up + jnp.dot(
-            x, gu_ref[1, g * width:(g + 1) * width, :], preferred_element_type=jnp.float32
+        gate = gate + lax.dot_general(
+            x, gu_ref[0, :, g * width:(g + 1) * width], contract_last,
+            preferred_element_type=jnp.float32,
+        )
+        up = up + lax.dot_general(
+            x, gu_ref[1, :, g * width:(g + 1) * width], contract_last,
+            preferred_element_type=jnp.float32,
         )
     hidden = (jax.nn.silu(gate) * up).astype(jnp.bfloat16)
     for g in range(groups):
@@ -138,8 +159,8 @@
     score_scale = float(HD) ** (-0.5)
     column_start = group_index * column_width
     groups = lax.axis_size("grp")
-    out_blocks = w_out.reshape(w_out.shape[0], groups, column_width)
-    out_cols = lax.all_to_all(out_blocks, "grp", split_axis=1, concat_axis=0, tiled=True)
+    out_blocks = column_blocks(w_out, groups)
+    out_cols = lax.all_to_all(out_blocks, "grp", split_axis=0, concat_axis=0, tiled=True)
     out_cols = out_cols.reshape(groups * w_out.shape[0], column_width)
     attended = attention(cache_len, query, key_new, value_new, cache_kv)
     attended_full = lax.all_gather(attended, "grp", axis=1, tiled=True)
@@ -174,7 +195,7 @@
     arrived = arrived.reshape(experts_all * capacity, column_width)
     gathered = lax.all_gather(arrived, "grp", axis=0, tiled=False)
     gain_blocks = norm_gain.astype(jnp.float32).reshape(groups, column_width)
-    slice_out = expert_ffn(gathered, gain_blocks, w_gate_up[0], w_down[0])
+    slice_out = expert_ffn(gathered, gain_blocks, jnp.swapaxes(w_gate_up[0], 1, 2), w_down[0])
     expert_out = lax.psum_scatter(slice_out, "grp", scatter_dimension=0, tiled=True)
     expert_out = expert_out.reshape(experts_all, capacity, column_width)
     returned = lax.all_to_all(expert_out, "ep", split_axis=0, concat_axis=0, tiled=True)

time: 196 us -> 195 us (level)
  local copies, waits for them, and re-layouts: 6.61 us -> 1.36 us
  waiting for transfers between devices: 76.1 us -> 78.6 us
  Pallas kernels: 11.8 us -> 13.9 us
    unnamed x15 -> x11, local copies, waits for them, and re-layouts: 4.88 us -> 0.14 us
    all_gather x1, waiting for transfers between devices: 28.1 us -> 30.5 us  [body(): gathered = lax.all_gather(arrived, 'grp', axis=0, tiled=False)]
    pallas_call x0 -> x1, Pallas kernels: none -> 2.34 us  [column_blocks(): pl.pallas_call(blocks_kernel, grid=(1,), in_specs=[pl.BlockSpec(matrix.sh...]
  transfers between devices with their start and end apart: 4 -> 4, of which waited for: 3 -> 3; matrix products, arithmetic and copies ran while one was open for 3% -> 2% of each run, Pallas kernels for 2% -> 2%
where the time goes in v9:
time: 195 us; the launch traced here: 194 us
  waiting for transfers between devices  78.6 us (40%)
  blocking collectives  59.2 us (30%)
  starting transfers between devices  22.2 us (11%)
  between operations  14.2 us (7%)
  Pallas kernels  13.9 us (7%)
  other arithmetic  2.34 us (1%)
  matrix products  2.05 us (1%)
    reduce_scatter x1, waiting for transfers between devices, body(): lax.psum_scatter(slice_out, 'grp', scatter_dimension=0, tiled=True)  30.6 us
    all_gather x1, waiting for transfers between devices, body(): gathered = lax.all_gather(arrived, 'grp', axis=0, tiled=False)  30.5 us
    all_to_all x1, blocking collectives, body(): lax.all_to_all(outgoing, 'ep', split_axis=0, concat_axis=0, tiled=True)  29.5 us
    all_to_all x1, waiting for transfers between devices, body(): lax.all_to_all(expert_out, 'ep', split_axis=0, concat_axis=0, tiled=True)  17.5 us
    all_gather x1, blocking collectives, body(): attended_full = lax.all_gather(attended, 'grp', axis=1, tiled=True)  16.6 us
    all_gather x1, blocking collectives, body(): after_full = lax.all_gather(after_cols, 'grp', axis=1, tiled=True)  13.2 us
    all_to_all x1, starting transfers between devices, body(): lax.all_to_all(expert_out, 'ep', split_axis=0, concat_axis=0, tiled=True)  12.4 us
    all_to_all x1, starting transfers between devices, body(): lax.all_to_all(out_blocks, 'grp', split_axis=0, concat_axis=0, tiled=True)  9.79 us
  transfers between devices with their start and end apart: 4, of which 3 were waited for; matrix products, arithmetic and copies ran while one was open for 2% of the time, Pallas kernels for 2%

profile of v9, /device:TPU:7, one launch (start us, length us, event | category | flops | bytes accessed | tf_op | source)
XLA Modules:
  0.0 193.9 jit_solution(6795954159898566426)
XLA Ops:
  7.2 0.0 copy-start
  7.2 2.3 %shard_map.132 = bf16[8,256,256]{2,1,0:T(8,128)(2,1)} custom-call(bf16[256,2048]{1,0:T(8,128)(2,1)} %x_ref.1), custom_call_target="tpu_custom_call" | custom-call | tf_op jit(solution)/shard_map/pallas_call | solution.py:86
  9.5 9.8 %all-to-all-start = ((bf16[8,256,256]{2,1,0:T(8,128)(2,1)}), bf16[8,256,256]{2,1,0:T(8,128)(2,1)S(1)}, u32[]{:S(2)}, u32[]{:S(2)}) async-start(bf16[8,256,256]{2,1,0:T(8,128)(2,1)} %shard_map.132), calls=%async_computation | async-start | bytes 2097152 | tf_op jit(solution)/shard_map/all_to_all | solution.py:163
  19.3 0.1 copy.37
  19.4 0.1 eq.49
  19.6 0.1 eq.45
  19.7 1.2 reduce-window.6
  20.9 0.2 slice_reduce_fusion
  21.2 0.1 fusion.11
  21.3 0.1 reduce_sum.48
  21.4 0.1 copy.40
  21.5 3.0 %shard_map.131 = bf16[128,256]{1,0:T(8,128)(2,1)} custom-call(s32[64]{0:T(128)} %len_ref.1, bf16[128,256]{1,0:T(8,128)(2,1)} %q_ref.1, bf16[128,256]{1,0:T(8,128)(2,1)} %kn_ref.1, bf16[128,256]{1,0:T(8,128)(2,1)} %vn_ref.1, bf16[2,1024,256]{2,1,0:T(8,128)(2,1)} %cache_ref.1), custom_call_target="tpu_custom_call" | custom-call | tf_op jit(solution)/shard_map/pallas_call | solution.py:62
  24.4 0.4 fusion
  24.8 16.6 %all_gather.9 = bf16[128,2048]{1,0:T(8,128)(2,1)S(1)} all-gather(bf16[128,256]{1,0:T(8,128)(2,1)} %shard_map.131), channel_id=1, replica_groups=mesh['grp'=8,'ep'=64] {'grp'}, dimensions={1}, use_global_device_ids=true | all-gather | bytes 589824 | tf_op jit(solution)/shard_map/all_gather | solution.py:166
  41.4 0.3 fusion.1
  41.7 0.0 copy-start.1
  41.7 0.4 convolution_convert_fusion
  42.1 29.5 %all_to_all.15 = bf16[64,16,256]{2,1,0:T(8,128)(2,1)} all-to-all(bf16[64,16,256]{2,1,0:T(8,128)(2,1)S(1)} %bitcast.38), channel_id=1, replica_groups=mesh['grp'=8,'ep'=64] {'ep'}, dimensions={0} | all-to-all | bytes 1048576 | tf_op jit(solution)/shard_map/all_to_all | solution.py:194
  71.5 0.0 all-gather.2.cloned.1.call-update
  71.6 0.0 reduce-scatter.2.cloned.1.call-start
  71.6 0.6 reshape.92.gain_ref
  72.2 30.5 %all-gather.2.cloned.1.call-done.x_ref = bf16[8,1024,256]{2,1,0:T(8,128)(2,1)} async-done(((bf16[1,1024,256]{2,1,0:T(8,128)(2,1)}), bf16[8,1024,256]{2,1,0:T(8,128)(2,1)}) %all-gather.2.cloned.1.call-update) | async-done | bytes 4194320 | tf_op jit(solution)/shard_map/all_gather | solution.py:196
  102.7 8.6 %shard_map.133 = bf16[8,1024,256]{2,1,0:T(8,128)(2,1)} custom-call(bf16[8,1024,256]{2,1,0:T(8,128)(2,1)} %all-gather.2.cloned.1.call-done.x_ref, f32[8,256]{1,0:T(8,128)} %reshape.92.gain_ref, bf16[2,176,2048]{2,1,0:T(8,128)(2,1)} %bitcast.39, bf16[176,2048]{1,0:T(8,128)(2,1)} %bitcast.40), custom_call_target="tpu_custom_call" | custom-call | tf_op jit(solution)/shard_map/pallas_call | solution.py:124
  111.3 0.0 reduce-scatter.2.cloned.1.call-update
  111.4 13.2 %all_gather.10 = bf16[128,2048]{1,0:T(8,128)(2,1)S(1)} all-gather(bf16[128,256]{1,0:T(8,128)(2,1)S(1)} %fusion.1), channel_id=1, replica_groups=mesh['grp'=8,'ep'=64] {'grp'}, dimensions={1}, use_global_device_ids=true | all-gather | bytes 589824 | tf_op jit(solution)/shard_map/all_gather | solution.py:169
  124.6 0.2 fusion.2
  124.8 30.6 %reduce-scatter.2.cloned.1.call-done = bf16[1,1024,256]{2,1,0:T(8,128)(2,1)} async-done(((bf16[8,1024,256]{2,1,0:T(8,128)(2,1)}), bf16[1,1024,256]{2,1,0:T(8,128)(2,1)}) %reduce-scatter.2.cloned.1.call-update) | async-done | bytes 524304 | tf_op jit(solution)/shard_map/reduce_scatter | solution.py:199
  155.4 12.4 %all-to-all-start.2 = ((bf16[64,16,256]{2,1,0:T(8,128)(2,1)}), bf16[64,16,256]{2,1,0:T(8,128)(2,1)S(1)}, u32[]{:S(2)}, u32[]{:S(2)}) async-start(bf16[64,16,256]{2,1,0:T(8,128)(2,1)} %bitcast.41), calls=%async_computation.3 | async-start | bytes 1048576 | tf_op jit(solution)/shard_map/all_to_all | solution.py:201
  167.8 0.4 fusion.5
  168.2 0.3 select_reduce_fusion
  168.5 17.5 %all-to-all-done.2 = bf16[64,16,256]{2,1,0:T(8,128)(2,1)S(1)} async-done(((bf16[64,16,256]{2,1,0:T(8,128)(2,1)}), bf16[64,16,256]{2,1,0:T(8,128)(2,1)S(1)}, u32[]{:S(2)}, u32[]{:S(2)}) %all-to-all-start.2) | async-done | bytes 524320 | tf_op jit(solution)/shard_map/all_to_all | solution.py:201
  186.1 1.0 convolution_convert_fusion.1
  (20 shorter events, 0.2 us)
Async XLA Ops:
  7.2 160.6 %copy-start = (bf16[2048,64]{0,1:T(8,128)(2,1)S(1)}, bf16[2048,64]{0,1:T(8,128)(2,1)}, u32[]{:S(2)}) copy-start(bf16[2048,64]{0,1:T(8,128)(2,1)} %param.20) | copy-start | bytes 786436
  7.2 12.1 %copy-start.3 = (s32[128,4]{0,1:T(4,128)S(1)}, s32[128,4]{0,1:T(4,128)}, u32[]{:S(2)}) copy-start(s32[128,4]{0,1:T(4,128)} %param.21) | copy-start | bytes 6148
  9.5 31.9 %copy-start.2 = (bf16[128,256]{1,0:T(8,128)(2,1)S(1)}, bf16[128,256]{1,0:T(8,128)(2,1)}, u32[]{:S(2)}) copy-start(bf16[128,256]{1,0:T(8,128)(2,1)} %param.12) | copy-start | bytes 196612
  9.5 31.8 %all-to-all-start = ((bf16[8,256,256]{2,1,0:T(8,128)(2,1)}), bf16[8,256,256]{2,1,0:T(8,128)(2,1)S(1)}, u32[]{:S(2)}, u32[]{:S(2)}) async-start(bf16[8,256,256]{2,1,0:T(8,128)(2,1)} %shard_map.132), calls=%async_computation | async-start | bytes 2097152 | tf_op jit(solution)/shard_map/all_to_all | solution.py:163
  19.3 83.4 %all-gather.2.cloned.1.call-start = ((), (), s32[]{:S(2)}) async-start(), calls=%async_computation.4 | async-start | bytes 4718592 | tf_op jit(solution)/shard_map/all_gather | solution.py:196
  41.4 30.2 %copy-start.4 = (bf16[2048]{0:T(1024)(128)(2,1)S(1)}, bf16[2048]{0:T(1024)(128)(2,1)}, u32[]{:S(2)}) copy-start(bf16[2048]{0:T(1024)(128)(2,1)} %param.19) | copy-start | bytes 12292
  41.7 69.7 %copy-start.1 = (bf16[128,256]{1,0:T(8,128)(2,1)}, bf16[128,256]{1,0:T(8,128)(2,1)S(1)}, u32[]{:S(2)}) copy-start(bf16[128,256]{1,0:T(8,128)(2,1)S(1)} %fusion.1) | copy-start | bytes 196612
  71.6 83.8 %reduce-scatter.2.cloned.1.call-start = ((), (), s32[]{:S(2)}) async-start(), calls=%async_computation.5 | async-start | bytes 4718592 | tf_op jit(solution)/shard_map/reduce_scatter | solution.py:199
  155.4 30.7 %all-to-all-start.2 = ((bf16[64,16,256]{2,1,0:T(8,128)(2,1)}), bf16[64,16,256]{2,1,0:T(8,128)(2,1)S(1)}, u32[]{:S(2)}, u32[]{:S(2)}) async-start(bf16[64,16,256]{2,1,0:T(8,128)(2,1)} %bitcast.41), calls=%async_computation.3 | async-start | bytes 1048576 | tf_op jit(solution)/shard_map/all_to_all | solution.py:201
Sparse Core Ops, SparseCore 0:
  71.7 30.9 all-gather.1
  111.5 43.8 reduce-scatter.1

commit v10 on v9

--- a/solution.py
+++ b/solution.py
@@ -1,8 +1,11 @@
+import functools
+
 import jax
 import jax.numpy as jnp
 from jax import lax
 from jax.experimental import pallas as pl
 from jax.experimental.pallas import tpu as pltpu
+from jax.sharding import Mesh
 from jax.sharding import PartitionSpec as P
 
 D = 2048
@@ -74,6 +77,9 @@
     )(cache_len, query, key_new, value_new, cache_kv)
 
 
+GRP = ("gx", "gc")
+
+
 def blocks_kernel(x_ref, out_ref):
     width = out_ref.shape[-1]
     for j in range(out_ref.shape[0]):
@@ -92,8 +98,10 @@
     )(matrix)
 
 
-def ffn_kernel(x_ref, gain_ref, gu_ref, down_ref, out_ref):
+def ffn_kernel(x_ref, gain_ref, gu_ref, down_ref, out_ref, cores):
     groups, rows, width = x_ref.shape
+    chips = groups // cores
+    block_of = [(i % chips) * cores + i // chips for i in range(groups)]
     squares = jnp.zeros((rows, 1), jnp.float32)
     for g in range(groups):
         wide = x_ref[g].astype(jnp.float32)
@@ -105,24 +113,26 @@
     for g in range(groups):
         x = (x_ref[g].astype(jnp.float32) * inverse * gain_ref[g:g + 1, :]).astype(jnp.bfloat16)
         gate = gate + lax.dot_general(
-            x, gu_ref[0, :, g * width:(g + 1) * width], contract_last,
+            x, gu_ref[0, :, block_of[g] * width:(block_of[g] + 1) * width], contract_last,
             preferred_element_type=jnp.float32,
         )
         up = up + lax.dot_general(
-            x, gu_ref[1, :, g * width:(g + 1) * width], contract_last,
+            x, gu_ref[1, :, block_of[g] * width:(block_of[g] + 1) * width], contract_last,
             preferred_element_type=jnp.float32,
         )
     hidden = (jax.nn.silu(gate) * up).astype(jnp.bfloat16)
     for g in range(groups):
         out_ref[g] = jnp.dot(
-            hidden, down_ref[:, g * width:(g + 1) * width], preferred_element_type=jnp.float32
+            hidden,
+            down_ref[:, block_of[g] * width:(block_of[g] + 1) * width],
+            preferred_element_type=jnp.float32,
         ).astype(out_ref.dtype)
 
 
-def expert_ffn(gathered, gain_blocks, gate_up, down, row_tile=256):
+def expert_ffn(gathered, gain_blocks, gate_up, down, cores, row_tile=256):
     groups, rows, width = gathered.shape
     return pl.pallas_call(
-        ffn_kernel,
+        functools.partial(ffn_kernel, cores=cores),
         grid=(rows // row_tile,),
         in_specs=[
             pl.BlockSpec((groups, row_tile, width), lambda i: (0, i, 0)),
@@ -153,20 +163,20 @@
     heads_here = query.shape[1] // HD
     experts_all = w_router.shape[1]
     column_width = resid.shape[1]
-    group_index = lax.axis_index("grp")
+    group_index = lax.axis_index("gx") * lax.axis_size("gc") + lax.axis_index("gc")
     request = lax.axis_index("ep")
     capacity = max(2, 8 * tokens_here // lax.axis_size("ep"))
     score_scale = float(HD) ** (-0.5)
     column_start = group_index * column_width
-    groups = lax.axis_size("grp")
+    groups = lax.axis_size("gx") * lax.axis_size("gc")
     out_blocks = column_blocks(w_out, groups)
-    out_cols = lax.all_to_all(out_blocks, "grp", split_axis=0, concat_axis=0, tiled=True)
+    out_cols = lax.all_to_all(out_blocks, GRP, split_axis=0, concat_axis=0, tiled=True)
     out_cols = out_cols.reshape(groups * w_out.shape[0], column_width)
     attended = attention(cache_len, query, key_new, value_new, cache_kv)
-    attended_full = lax.all_gather(attended, "grp", axis=1, tiled=True)
+    attended_full = lax.all_gather(attended, GRP, axis=1, tiled=True)
     attn_share = jnp.dot(attended_full, out_cols, preferred_element_type=jnp.float32)
     after_cols = (resid.astype(jnp.float32) + attn_share).astype(jnp.bfloat16)
-    after_full = lax.all_gather(after_cols, "grp", axis=1, tiled=True)
+    after_full = lax.all_gather(after_cols, GRP, axis=1, tiled=True)
     after_wide = after_full.astype(jnp.float32)
     squares = jnp.sum(after_wide * after_wide, axis=1)
     inverse = lax.rsqrt(squares / D + EPS)
@@ -193,10 +203,19 @@
     outgoing = outgoing.reshape(experts_all, capacity, column_width)
     arrived = lax.all_to_all(outgoing, "ep", split_axis=0, concat_axis=0, tiled=True)
     arrived = arrived.reshape(experts_all * capacity, column_width)
-    gathered = lax.all_gather(arrived, "grp", axis=0, tiled=False)
+    gathered = lax.all_gather(arrived, "gx", axis=0, tiled=False)
+    gathered = lax.all_gather(gathered, "gc", axis=0, tiled=False)
+    gathered = gathered.reshape(groups, experts_all * capacity, column_width)
+    cores = lax.axis_size("gc")
     gain_blocks = norm_gain.astype(jnp.float32).reshape(groups, column_width)
-    slice_out = expert_ffn(gathered, gain_blocks, jnp.swapaxes(w_gate_up[0], 1, 2), w_down[0])
-    expert_out = lax.psum_scatter(slice_out, "grp", scatter_dimension=0, tiled=True)
+    gain_blocks = gain_blocks.reshape(groups // cores, cores, column_width)
+    gain_blocks = jnp.swapaxes(gain_blocks, 0, 1).reshape(groups, column_width)
+    slice_out = expert_ffn(
+        gathered, gain_blocks, jnp.swapaxes(w_gate_up[0], 1, 2), w_down[0], cores
+    )
+    slice_out = slice_out.reshape(cores, groups // cores, experts_all * capacity, column_width)
+    expert_out = lax.psum_scatter(slice_out, "gc", scatter_dimension=0, tiled=True)
+    expert_out = lax.psum_scatter(expert_out, "gx", scatter_dimension=1, tiled=True)
     expert_out = expert_out.reshape(experts_all, capacity, column_width)
     returned = lax.all_to_all(expert_out, "ep", split_axis=0, concat_axis=0, tiled=True)
     mixed_cols = jnp.dot(
@@ -209,23 +228,26 @@
 
 
 def solution(mesh):
+    grp_size, ep_size = mesh.devices.shape
+    cores = 2
+    fine = Mesh(mesh.devices.reshape(grp_size // cores, cores, ep_size), ("gx", "gc", "ep"))
     return jax.shard_map(
         body,
-        mesh=mesh,
+        mesh=fine,
         in_specs=(
-            P("ep", "grp"),
-            P("ep", "grp"),
-            P("ep", "grp"),
-            P("ep", "grp"),
-            P(None, "ep", "grp"),
+            P("ep", GRP),
+            P("ep", GRP),
+            P("ep", GRP),
+            P("ep", GRP),
+            P(None, "ep", GRP),
             P(),
-            P("grp", None),
+            P(GRP, None),
             P(),
             P(),
             P("ep", None),
-            P("ep", None, None, "grp"),
-            P("ep", "grp", None),
+            P("ep", None, None, GRP),
+            P("ep", GRP, None),
         ),
-        out_specs=(P("ep", "grp"), P("ep", "grp")),
+        out_specs=(P("ep", GRP), P("ep", GRP)),
         check_vma=False,
     )

time: 195 us -> 237 us (1.22); the launches traced: 194 us -> 233 us
  waiting for transfers between devices: 78.6 us -> 117 us
    all_gather x1 -> x2, waiting for transfers between devices: 30.5 us -> 55 us  [the longest x1 29.4 us: body(): gathered = lax.all_gather(arrived, 'gx', axis=0, tiled=False)]
    reduce_scatter x1 -> x2, waiting for transfers between devices: 30.6 us -> 45.2 us  [the longest x1 23.7 us: body(): lax.psum_scatter(expert_out, 'gx', scatter_dimension=1, tiled=True)]
  transfers between devices with their start and end apart: 4 -> 6, of which waited for: 3 -> 5; matrix products, arithmetic and copies ran while one was open for 2% -> 2% of each run, Pallas kernels for 2% -> 1%
where the time goes in v10:
time: 237 us; the launch traced here: 233 us
  waiting for transfers between devices  117 us (49%)
  blocking collectives  59.3 us (25%)
  starting transfers between devices  22.9 us (10%)
  Pallas kernels  13.9 us (6%)
  between operations  13.9 us (6%)
    all_to_all x1, blocking collectives, body(): lax.all_to_all(outgoing, 'ep', split_axis=0, concat_axis=0, tiled=True)  29.5 us
    all_gather x1, waiting for transfers between devices, body(): gathered = lax.all_gather(arrived, 'gx', axis=0, tiled=False)  29.4 us
    all_gather x1, waiting for transfers between devices, body(): gathered = lax.all_gather(gathered, 'gc', axis=0, tiled=False)  25.6 us
    reduce_scatter x1, waiting for transfers between devices, body(): lax.psum_scatter(expert_out, 'gx', scatter_dimension=1, tiled=True)  23.7 us
    reduce_scatter x1, waiting for transfers between devices, body(): lax.psum_scatter(slice_out, 'gc', scatter_dimension=0, tiled=True)  21.6 us
    all_to_all x1, waiting for transfers between devices, body(): lax.all_to_all(expert_out, 'ep', split_axis=0, concat_axis=0, tiled=True)  16.6 us
    all_gather x1, blocking collectives, body(): attended_full = lax.all_gather(attended, GRP, axis=1, tiled=True)  16.6 us
    all_gather x1, blocking collectives, body(): after_full = lax.all_gather(after_cols, GRP, axis=1, tiled=True)  13.3 us
  transfers between devices with their start and end apart: 6, of which 5 were waited for; matrix products, arithmetic and copies ran while one was open for 2% of the time, Pallas kernels for 1%

profile of v10, /device:TPU:7, one launch (start us, length us, event | category | flops | bytes accessed | tf_op | source)
XLA Modules:
  0.0 232.7 jit_solution(17524626096707693728)
XLA Ops:
  7.2 2.3 %shard_map.132 = bf16[8,256,256]{2,1,0:T(8,128)(2,1)} custom-call(bf16[256,2048]{1,0:T(8,128)(2,1)} %x_ref.1), custom_call_target="tpu_custom_call" | custom-call | tf_op jit(solution)/shard_map/pallas_call | solution.py:92
  9.5 9.8 %all-to-all-start = ((bf16[8,256,256]{2,1,0:T(8,128)(2,1)}), bf16[8,256,256]{2,1,0:T(8,128)(2,1)S(1)}, u32[]{:S(2)}, u32[]{:S(2)}) async-start(bf16[8,256,256]{2,1,0:T(8,128)(2,1)} %shard_map.132), calls=%async_computation | async-start | bytes 2097152 | tf_op jit(solution)/shard_map/all_to_all | solution.py:173
  19.3 0.1 copy.40
  19.4 0.1 eq.49
  19.6 0.1 eq.45
  19.7 1.2 reduce-window.6
  20.9 0.2 slice_reduce_fusion
  21.2 0.1 fusion.11
  21.3 0.1 reduce_sum.48
  21.4 0.1 copy.43
  21.5 3.0 %shard_map.131 = bf16[128,256]{1,0:T(8,128)(2,1)} custom-call(s32[64]{0:T(128)} %len_ref.1, bf16[128,256]{1,0:T(8,128)(2,1)} %q_ref.1, bf16[128,256]{1,0:T(8,128)(2,1)} %kn_ref.1, bf16[128,256]{1,0:T(8,128)(2,1)} %vn_ref.1, bf16[2,1024,256]{2,1,0:T(8,128)(2,1)} %cache_ref.1), custom_call_target="tpu_custom_call" | custom-call | tf_op jit(solution)/shard_map/pallas_call | solution.py:65
  24.4 0.4 fusion
  24.8 16.6 %all_gather.15 = bf16[128,2048]{1,0:T(8,128)(2,1)S(1)} all-gather(bf16[128,256]{1,0:T(8,128)(2,1)} %shard_map.131), channel_id=1, replica_groups=mesh['gx'=4,'gc'=2,'ep'=64] {'gx','gc'}, dimensions={1}, use_global_device_ids=true | all-gather | bytes 589824 | tf_op jit(solution)/shard_map/all_gather | solution.py:176
  41.4 0.3 fusion.1
  41.7 0.4 convolution_convert_fusion
  42.1 29.5 %all_to_all.15 = bf16[64,16,256]{2,1,0:T(8,128)(2,1)} all-to-all(bf16[64,16,256]{2,1,0:T(8,128)(2,1)S(1)} %bitcast.41), channel_id=1, replica_groups=mesh['gx'=4,'gc'=2,'ep'=64] {'ep'}, dimensions={0} | all-to-all | bytes 1048576 | tf_op jit(solution)/shard_map/all_to_all | solution.py:204
  71.6 0.0 all-gather.6.cloned.1.call-start
  71.6 29.4 %all-gather.4.cloned.1.call-done = bf16[4,1024,256]{2,1,0:T(8,128)(2,1)} async-done(((bf16[1,1024,256]{2,1,0:T(8,128)(2,1)}), bf16[4,1024,256]{2,1,0:T(8,128)(2,1)}) %all-gather.4.cloned.1.call-update) | async-done | bytes 2097168 | tf_op jit(solution)/shard_map/all_gather | solution.py:206
  101.0 0.0 reduce-scatter.3.cloned.1.call-start
  101.1 0.6 reshape.99.gain_ref
  101.7 25.6 %all-gather.6.cloned.1.call-done.x_ref = bf16[8,1024,256]{2,1,0:T(8,128)(2,1)} async-done(((bf16[4,1024,256]{2,1,0:T(8,128)(2,1)}), bf16[8,1024,256]{2,1,0:T(8,128)(2,1)}) %all-gather.6.cloned.1.call-update) | async-done | bytes 4194320 | tf_op jit(solution)/shard_map/all_gather | solution.py:207
  127.3 8.6 %shard_map.133 = bf16[8,1024,256]{2,1,0:T(8,128)(2,1)} custom-call(bf16[8,1024,256]{2,1,0:T(8,128)(2,1)} %all-gather.6.cloned.1.call-done.x_ref, f32[8,256]{1,0:T(8,128)} %reshape.99.gain_ref, bf16[2,176,2048]{2,1,0:T(8,128)(2,1)} %bitcast.42, bf16[176,2048]{1,0:T(8,128)(2,1)} %bitcast.43), custom_call_target="tpu_custom_call" | custom-call | tf_op jit(solution)/shard_map/pallas_call | solution.py:134
  136.0 0.0 reduce-scatter.5.cloned.1.call-start
  136.1 21.6 %reduce-scatter.3.cloned.1.call-done = bf16[1,4,1024,256]{3,2,1,0:T(8,128)(2,1)} async-done(((bf16[2,4,1024,256]{3,2,1,0:T(8,128)(2,1)}), bf16[1,4,1024,256]{3,2,1,0:T(8,128)(2,1)}) %reduce-scatter.3.cloned.1.call-update) | async-done | bytes 2097168 | tf_op jit(solution)/shard_map/reduce_scatter | solution.py:217
  157.7 13.3 %all_gather.16 = bf16[128,2048]{1,0:T(8,128)(2,1)S(1)} all-gather(bf16[128,256]{1,0:T(8,128)(2,1)S(1)} %fusion.1), channel_id=1, replica_groups=mesh['gx'=4,'gc'=2,'ep'=64] {'gx','gc'}, dimensions={1}, use_global_device_ids=true | all-gather | bytes 589824 | tf_op jit(solution)/shard_map/all_gather | solution.py:179
  170.9 0.2 fusion.2
  171.1 23.7 %reduce-scatter.5.cloned.1.call-done = bf16[1,1,1024,256]{3,2,1,0:T(8,128)(2,1)} async-done(((bf16[1,4,1024,256]{3,2,1,0:T(8,128)(2,1)}), bf16[1,1,1024,256]{3,2,1,0:T(8,128)(2,1)}) %reduce-scatter.5.cloned.1.call-update) | async-done | bytes 524304 | tf_op jit(solution)/shard_map/reduce_scatter | solution.py:218
  194.8 13.0 %all-to-all-start.2 = ((bf16[64,16,256]{2,1,0:T(8,128)(2,1)}), bf16[64,16,256]{2,1,0:T(8,128)(2,1)S(1)}, u32[]{:S(2)}, u32[]{:S(2)}) async-start(bf16[64,16,256]{2,1,0:T(8,128)(2,1)} %bitcast.44), calls=%async_computation.4 | async-start | bytes 1048576 | tf_op jit(solution)/shard_map/all_to_all | solution.py:220
  207.8 0.4 fusion.5
  208.3 0.3 select_reduce_fusion
  208.6 16.6 %all-to-all-done.2 = bf16[64,16,256]{2,1,0:T(8,128)(2,1)S(1)} async-done(((bf16[64,16,256]{2,1,0:T(8,128)(2,1)}), bf16[64,16,256]{2,1,0:T(8,128)(2,1)S(1)}, u32[]{:S(2)}, u32[]{:S(2)}) %all-to-all-start.2) | async-done | bytes 524320 | tf_op jit(solution)/shard_map/all_to_all | solution.py:220
  225.2 1.0 convolution_convert_fusion.1
  (28 shorter events, 0.3 us)
Async XLA Ops:
  7.2 200.7 %copy-start = (bf16[2048,64]{0,1:T(8,128)(2,1)S(1)}, bf16[2048,64]{0,1:T(8,128)(2,1)}, u32[]{:S(2)}) copy-start(bf16[2048,64]{0,1:T(8,128)(2,1)} %param.20) | copy-start | bytes 786436
  7.2 12.1 %copy-start.3 = (s32[128,4]{0,1:T(4,128)S(1)}, s32[128,4]{0,1:T(4,128)}, u32[]{:S(2)}) copy-start(s32[128,4]{0,1:T(4,128)} %param.21) | copy-start | bytes 6148
  9.5 31.9 %copy-start.2 = (bf16[128,256]{1,0:T(8,128)(2,1)S(1)}, bf16[128,256]{1,0:T(8,128)(2,1)}, u32[]{:S(2)}) copy-start(bf16[128,256]{1,0:T(8,128)(2,1)} %param.12) | copy-start | bytes 196612
  9.5 31.8 %all-to-all-start = ((bf16[8,256,256]{2,1,0:T(8,128)(2,1)}), bf16[8,256,256]{2,1,0:T(8,128)(2,1)S(1)}, u32[]{:S(2)}, u32[]{:S(2)}) async-start(bf16[8,256,256]{2,1,0:T(8,128)(2,1)} %shard_map.132), calls=%async_computation | async-start | bytes 2097152 | tf_op jit(solution)/shard_map/all_to_all | solution.py:173
  19.3 81.7 %all-gather.4.cloned.1.call-start = ((), (), s32[]{:S(2)}) async-start(), calls=%async_computation.5 | async-start | bytes 2621440 | tf_op jit(solution)/shard_map/all_gather | solution.py:206
  41.7 116.0 %copy-start.1 = (bf16[128,256]{1,0:T(8,128)(2,1)}, bf16[128,256]{1,0:T(8,128)(2,1)S(1)}, u32[]{:S(2)}) copy-start(bf16[128,256]{1,0:T(8,128)(2,1)S(1)} %fusion.1) | copy-start | bytes 196612
  41.7 59.4 %copy-start.4 = (bf16[2048]{0:T(1024)(128)(2,1)S(1)}, bf16[2048]{0:T(1024)(128)(2,1)}, u32[]{:S(2)}) copy-start(bf16[2048]{0:T(1024)(128)(2,1)} %param.19) | copy-start | bytes 12292
  71.6 55.7 %all-gather.6.cloned.1.call-start = ((), (), s32[]{:S(2)}) async-start(), calls=%async_computation.8 | async-start | bytes 6291456 | tf_op jit(solution)/shard_map/all_gather | solution.py:207
  101.0 56.6 %reduce-scatter.3.cloned.1.call-start = ((), (), s32[]{:S(2)}) async-start(), calls=%async_computation.6 | async-start | bytes 6291456 | tf_op jit(solution)/shard_map/reduce_scatter | solution.py:217
  136.0 58.8 %reduce-scatter.5.cloned.1.call-start = ((), (), s32[]{:S(2)}) async-start(), calls=%async_computation.7 | async-start | bytes 2621440 | tf_op jit(solution)/shard_map/reduce_scatter | solution.py:218
  194.8 30.4 %all-to-all-start.2 = ((bf16[64,16,256]{2,1,0:T(8,128)(2,1)}), bf16[64,16,256]{2,1,0:T(8,128)(2,1)S(1)}, u32[]{:S(2)}, u32[]{:S(2)}) async-start(bf16[64,16,256]{2,1,0:T(8,128)(2,1)} %bitcast.44), calls=%async_computation.4 | async-start | bytes 1048576 | tf_op jit(solution)/shard_map/all_to_all | solution.py:220
Sparse Core Ops, SparseCore 0:
  71.7 29.2 all-gather.3
  103.1 24.1 all-gather.5
  136.1 21.4 reduce-scatter.2
  160.6 34.1 reduce-scatter.4

commit v11 on v9

--- a/solution.py
+++ b/solution.py
@@ -14,7 +14,7 @@
 MASKED = -1e30
 
 
-def attention_kernel(len_ref, q_ref, kn_ref, vn_ref, cache_ref, out_ref):
+def attention_kernel(len_ref, q_ref, kn_ref, vn_ref, cache_ref, wout_ref, out_ref, blocks_ref):
     tokens, width = q_ref.shape
     cache_rows = cache_ref.shape[1]
     length = len_ref[lax.axis_index("ep")]
@@ -55,10 +55,15 @@
         )
         heads.append((weighted / denominator).astype(jnp.bfloat16))
     out_ref[...] = jnp.concatenate(heads, axis=1)
-
-
-def attention(cache_len, query, key_new, value_new, cache_kv):
+    block_width = blocks_ref.shape[-1]
+    for j in range(blocks_ref.shape[0]):
+        blocks_ref[j] = wout_ref[:, j * block_width:(j + 1) * block_width]
+
+
+def attention(cache_len, query, key_new, value_new, cache_kv, w_out, groups):
     whole = lambda shape: pl.BlockSpec(shape, lambda i: (0,) * len(shape))
+    rows, cols = w_out.shape
+    blocks_shape = (groups, rows, cols // groups)
     return pl.pallas_call(
         attention_kernel,
         grid=(1,),
@@ -68,28 +73,14 @@
             whole(key_new.shape),
             whole(value_new.shape),
             whole(cache_kv.shape),
+            whole(w_out.shape),
         ],
-        out_specs=whole(query.shape),
-        out_shape=jax.ShapeDtypeStruct(query.shape, jnp.bfloat16),
-    )(cache_len, query, key_new, value_new, cache_kv)
-
-
-def blocks_kernel(x_ref, out_ref):
-    width = out_ref.shape[-1]
-    for j in range(out_ref.shape[0]):
-        out_ref[j] = x_ref[:, j * width:(j + 1) * width]
-
-
-def column_blocks(matrix, groups):
-    rows, cols = matrix.shape
-    shape = (groups, rows, cols // groups)
-    return pl.pallas_call(
-        blocks_kernel,
-        grid=(1,),
-        in_specs=[pl.BlockSpec(matrix.shape, lambda i: (0, 0))],
-        out_specs=pl.BlockSpec(shape, lambda i: (0, 0, 0)),
-        out_shape=jax.ShapeDtypeStruct(shape, matrix.dtype),
-    )(matrix)
+        out_specs=[whole(query.shape), whole(blocks_shape)],
+        out_shape=[
+            jax.ShapeDtypeStruct(query.shape, jnp.bfloat16),
+            jax.ShapeDtypeStruct(blocks_shape, w_out.dtype),
+        ],
+    )(cache_len, query, key_new, value_new, cache_kv, w_out)
 
 
 def ffn_kernel(x_ref, gain_ref, gu_ref, down_ref, out_ref):
@@ -159,10 +150,9 @@
     score_scale = float(HD) ** (-0.5)
     column_start = group_index * column_width
     groups = lax.axis_size("grp")
-    out_blocks = column_blocks(w_out, groups)
+    attended, out_blocks = attention(cache_len, query, key_new, value_new, cache_kv, w_out, groups)
     out_cols = lax.all_to_all(out_blocks, "grp", split_axis=0, concat_axis=0, tiled=True)
     out_cols = out_cols.reshape(groups * w_out.shape[0], column_width)
-    attended = attention(cache_len, query, key_new, value_new, cache_kv)
     attended_full = lax.all_gather(attended, "grp", axis=1, tiled=True)
     attn_share = jnp.dot(attended_full, out_cols, preferred_element_type=jnp.float32)
     after_cols = (resid.astype(jnp.float32) + attn_share).astype(jnp.bfloat16)
@@ -178,8 +168,10 @@
     chosen = jnp.sum(jnp.where(route_hits, logits[:, None, :], 0.0), axis=-1)
     route_weight = jax.nn.softmax(chosen, axis=-1).astype(jnp.bfloat16)
     flat_hits = route_hits.reshape(tokens_here * TOP, experts_all).astype(jnp.int32)
-    earlier = jnp.cumsum(flat_hits, axis=0) - flat_hits
-    slot_index = jnp.sum(earlier * flat_hits, axis=1)
+    pair_ids = jnp.arange(tokens_here * TOP, dtype=jnp.int32)
+    before = (pair_ids[None, :] < pair_ids[:, None]).astype(jnp.bfloat16)
+    earlier = jnp.dot(before, flat_hits.astype(jnp.bfloat16), preferred_element_type=jnp.float32)
+    slot_index = jnp.sum(earlier * flat_hits.astype(jnp.float32), axis=1).astype(jnp.int32)
     slot_row = (routes.reshape(-1) * capacity + slot_index).reshape(tokens_here, TOP)
     slot_ids = jnp.arange(experts_all * capacity, dtype=jnp.int32)
     matches = slot_row[:, :, None] == slot_ids[None, None, :]

time: 195 us -> 196 us (level)
  blocking collectives: 59.2 us -> 63.1 us
    all_gather x1, blocking collectives: 16.6 us -> 20.4 us  [body(): attended_full = lax.all_gather(attended, 'grp', axis=1, tiled=True)]
    pallas_call x1 -> x0, Pallas kernels: 2.34 us -> none  [column_blocks(): pl.pallas_call(blocks_kernel, grid=(1,), in_specs=[pl.BlockSpec(matrix.sh...]
  transfers between devices with their start and end apart: 4 -> 4, of which waited for: 3 -> 3; matrix products, arithmetic and copies ran while one was open for 2% -> 1% of each run, Pallas kernels for 2% -> 0%
where the time goes in v11:
time: 196 us; the launch traced here: 195 us
  waiting for transfers between devices  78.9 us (40%)
  blocking collectives  63.1 us (32%)
  starting transfers between devices  22.2 us (11%)
  between operations  14.2 us (7%)
  Pallas kernels  12.3 us (6%)
  matrix products  2.35 us (1%)
    all_gather x1, waiting for transfers between devices, body(): gathered = lax.all_gather(arrived, 'grp', axis=0, tiled=False)  30.9 us
    reduce_scatter x1, waiting for transfers between devices, body(): lax.psum_scatter(slice_out, 'grp', scatter_dimension=0, tiled=True)  30.5 us
    all_to_all x1, blocking collectives, body(): lax.all_to_all(outgoing, 'ep', split_axis=0, concat_axis=0, tiled=True)  29.5 us
    all_gather x1, blocking collectives, body(): attended_full = lax.all_gather(attended, 'grp', axis=1, tiled=True)  20.4 us
    all_to_all x1, waiting for transfers between devices, body(): lax.all_to_all(expert_out, 'ep', split_axis=0, concat_axis=0, tiled=True)  17.4 us
    all_gather x1, blocking collectives, body(): after_full = lax.all_gather(after_cols, 'grp', axis=1, tiled=True)  13.2 us
    all_to_all x1, starting transfers between devices, body(): lax.all_to_all(expert_out, 'ep', split_axis=0, concat_axis=0, tiled=True)  12.4 us
    all_to_all x1, starting transfers between devices, body(): lax.all_to_all(out_blocks, 'grp', split_axis=0, concat_axis=0, tiled=True)  9.79 us
  transfers between devices with their start and end apart: 4, of which 3 were waited for; matrix products, arithmetic and copies ran while one was open for 1% of the time, Pallas kernels for 0%

profile of v11, /device:TPU:7, one launch (start us, length us, event | category | flops | bytes accessed | tf_op | source)
XLA Modules:
  0.0 195.1 jit_solution(17662987544121036413)
XLA Ops:
  7.2 0.0 copy-start
  7.2 3.6 %shard_map.131 = (bf16[128,256]{1,0:T(8,128)(2,1)}, bf16[8,256,256]{2,1,0:T(8,128)(2,1)}) custom-call(s32[64]{0:T(128)} %len_ref.1, bf16[128,256]{1,0:T(8,128)(2,1)} %q_ref.1, bf16[128,256]{1,0:T(8,128)(2,1)} %kn_ref.1, bf16[128,256]{1,0:T(8,128)(2,1)} %vn_ref.1, bf16[2,1024,256]{2,1,0:T(8,128)(2,1)} %cache_ref.1, bf16[256,2048]{1,0:T(8,128)(2,1)} %wout_ref.1), custom_call_target="tpu_custom_call" | custom-call | tf_op jit(solution)/shard_map/pallas_call | solution.py:67
  10.8 9.8 %all-to-all-start = ((bf16[8,256,256]{2,1,0:T(8,128)(2,1)}), bf16[8,256,256]{2,1,0:T(8,128)(2,1)S(1)}, u32[]{:S(2)}, u32[]{:S(2)}) async-start(bf16[8,256,256]{2,1,0:T(8,128)(2,1)} %get-tuple-element.5), calls=%async_computation | async-start | bytes 2097152 | tf_op jit(solution)/shard_map/all_to_all | solution.py:154
  20.6 0.1 copy.31
  20.7 0.1 eq.35
  20.8 0.3 fusion.2
  21.1 0.1 convert_element_type.62
  21.3 0.1 copy.32
  21.3 0.4 fusion
  21.7 0.0 copy-done.2
  21.7 20.4 %all_gather.9 = bf16[128,2048]{1,0:T(8,128)(2,1)S(1)} all-gather(bf16[128,256]{1,0:T(8,128)(2,1)S(1)} %copy-done.2), channel_id=1, replica_groups=mesh['grp'=8,'ep'=64] {'grp'}, dimensions={1}, use_global_device_ids=true | all-gather | bytes 589824 | tf_op jit(solution)/shard_map/all_gather | solution.py:156
  42.2 0.0 all-to-all-done
  42.2 0.3 fusion.1
  42.5 0.0 copy-start.1
  42.5 0.4 convolution_convert_fusion
  42.9 29.5 %all_to_all.15 = bf16[64,16,256]{2,1,0:T(8,128)(2,1)} all-to-all(bf16[64,16,256]{2,1,0:T(8,128)(2,1)S(1)} %bitcast.19), channel_id=1, replica_groups=mesh['grp'=8,'ep'=64] {'ep'}, dimensions={0} | all-to-all | bytes 1048576 | tf_op jit(solution)/shard_map/all_to_all | solution.py:186
  72.4 0.0 all-gather.2.cloned.1.call-update
  72.4 0.0 reduce-scatter.2.cloned.1.call-start
  72.4 0.0 copy-done.5
  72.4 0.6 reshape.79.gain_ref
  73.0 30.9 %all-gather.2.cloned.1.call-done.x_ref = bf16[8,1024,256]{2,1,0:T(8,128)(2,1)} async-done(((bf16[1,1024,256]{2,1,0:T(8,128)(2,1)}), bf16[8,1024,256]{2,1,0:T(8,128)(2,1)}) %all-gather.2.cloned.1.call-update) | async-done | bytes 4194320 | tf_op jit(solution)/shard_map/all_gather | solution.py:188
  104.0 8.6 %shard_map.132 = bf16[8,1024,256]{2,1,0:T(8,128)(2,1)} custom-call(bf16[8,1024,256]{2,1,0:T(8,128)(2,1)} %all-gather.2.cloned.1.call-done.x_ref, f32[8,256]{1,0:T(8,128)} %reshape.79.gain_ref, bf16[2,176,2048]{2,1,0:T(8,128)(2,1)} %bitcast.20, bf16[176,2048]{1,0:T(8,128)(2,1)} %bitcast.21), custom_call_target="tpu_custom_call" | custom-call | tf_op jit(solution)/shard_map/pallas_call | solution.py:115
  112.6 0.0 reduce-scatter.2.cloned.1.call-update
  112.7 0.0 copy-done.1
  112.7 13.2 %all_gather.10 = bf16[128,2048]{1,0:T(8,128)(2,1)S(1)} all-gather(bf16[128,256]{1,0:T(8,128)(2,1)S(1)} %fusion.1), channel_id=1, replica_groups=mesh['grp'=8,'ep'=64] {'grp'}, dimensions={1}, use_global_device_ids=true | all-gather | bytes 589824 | tf_op jit(solution)/shard_map/all_gather | solution.py:159
  125.9 0.2 fusion.3
  126.1 30.5 %reduce-scatter.2.cloned.1.call-done = bf16[1,1024,256]{2,1,0:T(8,128)(2,1)} async-done(((bf16[8,1024,256]{2,1,0:T(8,128)(2,1)}), bf16[1,1024,256]{2,1,0:T(8,128)(2,1)}) %reduce-scatter.2.cloned.1.call-update) | async-done | bytes 524304 | tf_op jit(solution)/shard_map/reduce_scatter | solution.py:191
  156.6 12.4 %all-to-all-start.2 = ((bf16[64,16,256]{2,1,0:T(8,128)(2,1)}), bf16[64,16,256]{2,1,0:T(8,128)(2,1)S(1)}, u32[]{:S(2)}, u32[]{:S(2)}) async-start(bf16[64,16,256]{2,1,0:T(8,128)(2,1)} %bitcast.22), calls=%async_computation.3 | async-start | bytes 1048576 | tf_op jit(solution)/shard_map/all_to_all | solution.py:193
  169.0 0.4 fusion.6
  169.5 0.3 select_reduce_fusion
  169.8 17.4 %all-to-all-done.2 = bf16[64,16,256]{2,1,0:T(8,128)(2,1)S(1)} async-done(((bf16[64,16,256]{2,1,0:T(8,128)(2,1)}), bf16[64,16,256]{2,1,0:T(8,128)(2,1)S(1)}, u32[]{:S(2)}, u32[]{:S(2)}) %all-to-all-start.2) | async-done | bytes 524320 | tf_op jit(solution)/shard_map/all_to_all | solution.py:193
  187.2 1.0 convolution_convert_fusion.1
  (16 shorter events, 0.1 us)
Async XLA Ops:
  7.2 161.9 %copy-start = (bf16[2048,64]{0,1:T(8,128)(2,1)S(1)}, bf16[2048,64]{0,1:T(8,128)(2,1)}, u32[]{:S(2)}) copy-start(bf16[2048,64]{0,1:T(8,128)(2,1)} %param.20) | copy-start | bytes 786436
  7.2 13.4 %copy-start.4 = (s32[128,4]{0,1:T(4,128)S(1)}, s32[128,4]{0,1:T(4,128)}, u32[]{:S(2)}) copy-start(s32[128,4]{0,1:T(4,128)} %param.21) | copy-start | bytes 6148
  10.8 10.9 %copy-start.2 = (bf16[128,256]{1,0:T(8,128)(2,1)S(1)}, bf16[128,256]{1,0:T(8,128)(2,1)}, u32[]{:S(2)}) copy-start(bf16[128,256]{1,0:T(8,128)(2,1)} %get-tuple-element.4) | copy-start | bytes 196612
  10.8 31.4 %copy-start.3 = (bf16[128,256]{1,0:T(8,128)(2,1)S(1)}, bf16[128,256]{1,0:T(8,128)(2,1)}, u32[]{:S(2)}) copy-start(bf16[128,256]{1,0:T(8,128)(2,1)} %param.12) | copy-start | bytes 196612
  10.8 31.4 %all-to-all-start = ((bf16[8,256,256]{2,1,0:T(8,128)(2,1)}), bf16[8,256,256]{2,1,0:T(8,128)(2,1)S(1)}, u32[]{:S(2)}, u32[]{:S(2)}) async-start(bf16[8,256,256]{2,1,0:T(8,128)(2,1)} %get-tuple-element.5), calls=%async_computation | async-start | bytes 2097152 | tf_op jit(solution)/shard_map/all_to_all | solution.py:154
  20.6 83.4 %all-gather.2.cloned.1.call-start = ((), (), s32[]{:S(2)}) async-start(), calls=%async_computation.4 | async-start | bytes 4718592 | tf_op jit(solution)/shard_map/all_gather | solution.py:188
  42.2 30.3 %copy-start.5 = (bf16[2048]{0:T(1024)(128)(2,1)S(1)}, bf16[2048]{0:T(1024)(128)(2,1)}, u32[]{:S(2)}) copy-start(bf16[2048]{0:T(1024)(128)(2,1)} %param.19) | copy-start | bytes 12292
  42.5 70.2 %copy-start.1 = (bf16[128,256]{1,0:T(8,128)(2,1)}, bf16[128,256]{1,0:T(8,128)(2,1)S(1)}, u32[]{:S(2)}) copy-start(bf16[128,256]{1,0:T(8,128)(2,1)S(1)} %fusion.1) | copy-start | bytes 196612
  72.4 84.2 %reduce-scatter.2.cloned.1.call-start = ((), (), s32[]{:S(2)}) async-start(), calls=%async_computation.5 | async-start | bytes 4718592 | tf_op jit(solution)/shard_map/reduce_scatter | solution.py:191
  156.6 30.6 %all-to-all-start.2 = ((bf16[64,16,256]{2,1,0:T(8,128)(2,1)}), bf16[64,16,256]{2,1,0:T(8,128)(2,1)S(1)}, u32[]{:S(2)}, u32[]{:S(2)}) async-start(bf16[64,16,256]{2,1,0:T(8,128)(2,1)} %bitcast.22), calls=%async_computation.3 | async-start | bytes 1048576 | tf_op jit(solution)/shard_map/all_to_all | solution.py:193
Sparse Core Ops, SparseCore 0:
  72.5 31.4 all-gather.1
  112.8 43.7 reduce-scatter.1

commit v12 on v9

--- a/solution.py
+++ b/solution.py
@@ -119,7 +119,7 @@
         ).astype(out_ref.dtype)
 
 
-def expert_ffn(gathered, gain_blocks, gate_up, down, row_tile=256):
+def expert_ffn(gathered, gain_blocks, gate_up, down, row_tile=512):
     groups, rows, width = gathered.shape
     return pl.pallas_call(
         ffn_kernel,
@@ -178,8 +178,10 @@
     chosen = jnp.sum(jnp.where(route_hits, logits[:, None, :], 0.0), axis=-1)
     route_weight = jax.nn.softmax(chosen, axis=-1).astype(jnp.bfloat16)
     flat_hits = route_hits.reshape(tokens_here * TOP, experts_all).astype(jnp.int32)
-    earlier = jnp.cumsum(flat_hits, axis=0) - flat_hits
-    slot_index = jnp.sum(earlier * flat_hits, axis=1)
+    pair_ids = jnp.arange(tokens_here * TOP, dtype=jnp.int32)
+    before = (pair_ids[None, :] < pair_ids[:, None]).astype(jnp.bfloat16)
+    earlier = jnp.dot(before, flat_hits.astype(jnp.bfloat16), preferred_element_type=jnp.float32)
+    slot_index = jnp.sum(earlier * flat_hits.astype(jnp.float32), axis=1).astype(jnp.int32)
     slot_row = (routes.reshape(-1) * capacity + slot_index).reshape(tokens_here, TOP)
     slot_ids = jnp.arange(experts_all * capacity, dtype=jnp.int32)
     matches = slot_row[:, :, None] == slot_ids[None, None, :]

time: 195 us -> 194 us (level)
  transfers between devices with their start and end apart: 4 -> 4, of which waited for: 3 -> 3; matrix products, arithmetic and copies ran while one was open for 2% -> 1% of each run, Pallas kernels for 2% -> 2%
where the time goes in v12:
time: 194 us; the launch traced here: 193 us
  waiting for transfers between devices  78.9 us (41%)
  blocking collectives  60.2 us (31%)
  starting transfers between devices  22.3 us (11%)
  between operations  14.2 us (7%)
  Pallas kernels  13.4 us (7%)
  matrix products  2.35 us (1%)
    all_gather x1, waiting for transfers between devices, body(): gathered = lax.all_gather(arrived, 'grp', axis=0, tiled=False)  31 us
    reduce_scatter x1, waiting for transfers between devices, body(): lax.psum_scatter(slice_out, 'grp', scatter_dimension=0, tiled=True)  30.5 us
    all_to_all x1, blocking collectives, body(): lax.all_to_all(outgoing, 'ep', split_axis=0, concat_axis=0, tiled=True)  29.5 us
    all_gather x1, blocking collectives, body(): attended_full = lax.all_gather(attended, 'grp', axis=1, tiled=True)  17.5 us
    all_to_all x1, waiting for transfers between devices, body(): lax.all_to_all(expert_out, 'ep', split_axis=0, concat_axis=0, tiled=True)  17.4 us
    all_gather x1, blocking collectives, body(): after_full = lax.all_gather(after_cols, 'grp', axis=1, tiled=True)  13.2 us
    all_to_all x1, starting transfers between devices, body(): lax.all_to_all(expert_out, 'ep', split_axis=0, concat_axis=0, tiled=True)  12.4 us
    all_to_all x1, starting transfers between devices, body(): lax.all_to_all(out_blocks, 'grp', split_axis=0, concat_axis=0, tiled=True)  9.79 us
  transfers between devices with their start and end apart: 4, of which 3 were waited for; matrix products, arithmetic and copies ran while one was open for 1% of the time, Pallas kernels for 2%

profile of v12, /device:TPU:7, one launch (start us, length us, event | category | flops | bytes accessed | tf_op | source)
XLA Modules:
  0.0 193.3 jit_solution(13317426883594782140)
XLA Ops:
  7.2 0.0 copy-start
  7.2 0.0 copy-start.3
  7.2 2.3 %shard_map.132 = bf16[8,256,256]{2,1,0:T(8,128)(2,1)} custom-call(bf16[256,2048]{1,0:T(8,128)(2,1)} %x_ref.1), custom_call_target="tpu_custom_call" | custom-call | tf_op jit(solution)/shard_map/pallas_call | solution.py:86
  9.5 9.8 %all-to-all-start = ((bf16[8,256,256]{2,1,0:T(8,128)(2,1)}), bf16[8,256,256]{2,1,0:T(8,128)(2,1)S(1)}, u32[]{:S(2)}, u32[]{:S(2)}) async-start(bf16[8,256,256]{2,1,0:T(8,128)(2,1)} %shard_map.132), calls=%async_computation | async-start | bytes 2097152 | tf_op jit(solution)/shard_map/all_to_all | solution.py:163
  19.3 0.1 copy.31
  19.4 0.1 eq.35
  19.6 0.3 fusion.2
  19.9 0.1 convert_element_type.62
  20.0 0.1 copy.32
  20.0 3.0 %shard_map.131 = bf16[128,256]{1,0:T(8,128)(2,1)} custom-call(s32[64]{0:T(128)} %len_ref.1, bf16[128,256]{1,0:T(8,128)(2,1)} %q_ref.1, bf16[128,256]{1,0:T(8,128)(2,1)} %kn_ref.1, bf16[128,256]{1,0:T(8,128)(2,1)} %vn_ref.1, bf16[2,1024,256]{2,1,0:T(8,128)(2,1)} %cache_ref.1), custom_call_target="tpu_custom_call" | custom-call | tf_op jit(solution)/shard_map/pallas_call | solution.py:62
  23.0 0.4 fusion
  23.4 17.5 %all_gather.9 = bf16[128,2048]{1,0:T(8,128)(2,1)S(1)} all-gather(bf16[128,256]{1,0:T(8,128)(2,1)} %shard_map.131), channel_id=1, replica_groups=mesh['grp'=8,'ep'=64] {'grp'}, dimensions={1}, use_global_device_ids=true | all-gather | bytes 589824 | tf_op jit(solution)/shard_map/all_gather | solution.py:166
  40.9 0.0 all-to-all-done
  40.9 0.3 fusion.1
  41.2 0.0 copy-start.1
  41.2 0.4 convolution_convert_fusion
  41.6 29.5 %all_to_all.15 = bf16[64,16,256]{2,1,0:T(8,128)(2,1)} all-to-all(bf16[64,16,256]{2,1,0:T(8,128)(2,1)S(1)} %bitcast.19), channel_id=1, replica_groups=mesh['grp'=8,'ep'=64] {'ep'}, dimensions={0} | all-to-all | bytes 1048576 | tf_op jit(solution)/shard_map/all_to_all | solution.py:196
  71.1 0.0 all-gather.2.cloned.1.call-update
  71.1 0.0 reduce-scatter.2.cloned.1.call-start
  71.1 0.6 reshape.79.gain_ref
  71.7 31.0 %all-gather.2.cloned.1.call-done.x_ref = bf16[8,1024,256]{2,1,0:T(8,128)(2,1)} async-done(((bf16[1,1024,256]{2,1,0:T(8,128)(2,1)}), bf16[8,1024,256]{2,1,0:T(8,128)(2,1)}) %all-gather.2.cloned.1.call-update) | async-done | bytes 4194320 | tf_op jit(solution)/shard_map/all_gather | solution.py:198
  102.7 8.1 %shard_map.133 = bf16[8,1024,256]{2,1,0:T(8,128)(2,1)} custom-call(bf16[8,1024,256]{2,1,0:T(8,128)(2,1)} %all-gather.2.cloned.1.call-done.x_ref, f32[8,256]{1,0:T(8,128)} %reshape.79.gain_ref, bf16[2,176,2048]{2,1,0:T(8,128)(2,1)} %bitcast.20, bf16[176,2048]{1,0:T(8,128)(2,1)} %bitcast.21), custom_call_target="tpu_custom_call" | custom-call | tf_op jit(solution)/shard_map/pallas_call | solution.py:124
  110.8 0.0 reduce-scatter.2.cloned.1.call-update
  110.8 0.0 copy-done.1
  110.8 13.2 %all_gather.10 = bf16[128,2048]{1,0:T(8,128)(2,1)S(1)} all-gather(bf16[128,256]{1,0:T(8,128)(2,1)S(1)} %fusion.1), channel_id=1, replica_groups=mesh['grp'=8,'ep'=64] {'grp'}, dimensions={1}, use_global_device_ids=true | all-gather | bytes 589824 | tf_op jit(solution)/shard_map/all_gather | solution.py:169
  124.0 0.2 fusion.3
  124.2 30.5 %reduce-scatter.2.cloned.1.call-done = bf16[1,1024,256]{2,1,0:T(8,128)(2,1)} async-done(((bf16[8,1024,256]{2,1,0:T(8,128)(2,1)}), bf16[1,1024,256]{2,1,0:T(8,128)(2,1)}) %reduce-scatter.2.cloned.1.call-update) | async-done | bytes 524304 | tf_op jit(solution)/shard_map/reduce_scatter | solution.py:201
  154.8 12.4 %all-to-all-start.2 = ((bf16[64,16,256]{2,1,0:T(8,128)(2,1)}), bf16[64,16,256]{2,1,0:T(8,128)(2,1)S(1)}, u32[]{:S(2)}, u32[]{:S(2)}) async-start(bf16[64,16,256]{2,1,0:T(8,128)(2,1)} %bitcast.22), calls=%async_computation.3 | async-start | bytes 1048576 | tf_op jit(solution)/shard_map/all_to_all | solution.py:203
  167.2 0.4 fusion.6
  167.7 0.3 select_reduce_fusion
  168.0 17.4 %all-to-all-done.2 = bf16[64,16,256]{2,1,0:T(8,128)(2,1)S(1)} async-done(((bf16[64,16,256]{2,1,0:T(8,128)(2,1)}), bf16[64,16,256]{2,1,0:T(8,128)(2,1)S(1)}, u32[]{:S(2)}, u32[]{:S(2)}) %all-to-all-start.2) | async-done | bytes 524320 | tf_op jit(solution)/shard_map/all_to_all | solution.py:203
  185.4 1.0 convolution_convert_fusion.1
  (15 shorter events, 0.1 us)
Async XLA Ops:
  7.2 160.0 %copy-start = (bf16[2048,64]{0,1:T(8,128)(2,1)S(1)}, bf16[2048,64]{0,1:T(8,128)(2,1)}, u32[]{:S(2)}) copy-start(bf16[2048,64]{0,1:T(8,128)(2,1)} %param.20) | copy-start | bytes 786436
  7.2 12.1 %copy-start.3 = (s32[128,4]{0,1:T(4,128)S(1)}, s32[128,4]{0,1:T(4,128)}, u32[]{:S(2)}) copy-start(s32[128,4]{0,1:T(4,128)} %param.21) | copy-start | bytes 6148
  9.5 31.4 %copy-start.2 = (bf16[128,256]{1,0:T(8,128)(2,1)S(1)}, bf16[128,256]{1,0:T(8,128)(2,1)}, u32[]{:S(2)}) copy-start(bf16[128,256]{1,0:T(8,128)(2,1)} %param.12) | copy-start | bytes 196612
  9.5 31.4 %all-to-all-start = ((bf16[8,256,256]{2,1,0:T(8,128)(2,1)}), bf16[8,256,256]{2,1,0:T(8,128)(2,1)S(1)}, u32[]{:S(2)}, u32[]{:S(2)}) async-start(bf16[8,256,256]{2,1,0:T(8,128)(2,1)} %shard_map.132), calls=%async_computation | async-start | bytes 2097152 | tf_op jit(solution)/shard_map/all_to_all | solution.py:163
  19.3 83.4 %all-gather.2.cloned.1.call-start = ((), (), s32[]{:S(2)}) async-start(), calls=%async_computation.4 | async-start | bytes 4718592 | tf_op jit(solution)/shard_map/all_gather | solution.py:198
  40.9 30.2 %copy-start.4 = (bf16[2048]{0:T(1024)(128)(2,1)S(1)}, bf16[2048]{0:T(1024)(128)(2,1)}, u32[]{:S(2)}) copy-start(bf16[2048]{0:T(1024)(128)(2,1)} %param.19) | copy-start | bytes 12292
  41.2 69.6 %copy-start.1 = (bf16[128,256]{1,0:T(8,128)(2,1)}, bf16[128,256]{1,0:T(8,128)(2,1)S(1)}, u32[]{:S(2)}) copy-start(bf16[128,256]{1,0:T(8,128)(2,1)S(1)} %fusion.1) | copy-start | bytes 196612
  71.1 83.7 %reduce-scatter.2.cloned.1.call-start = ((), (), s32[]{:S(2)}) async-start(), calls=%async_computation.5 | async-start | bytes 4718592 | tf_op jit(solution)/shard_map/reduce_scatter | solution.py:201
  154.8 30.6 %all-to-all-start.2 = ((bf16[64,16,256]{2,1,0:T(8,128)(2,1)}), bf16[64,16,256]{2,1,0:T(8,128)(2,1)S(1)}, u32[]{:S(2)}, u32[]{:S(2)}) async-start(bf16[64,16,256]{2,1,0:T(8,128)(2,1)} %bitcast.22), calls=%async_computation.3 | async-start | bytes 1048576 | tf_op jit(solution)/shard_map/all_to_all | solution.py:203
Sparse Core Ops, SparseCore 0:
  71.2 31.4 all-gather.1
  110.9 43.7 reduce-scatter.1

commit v13 on v12

--- a/solution.py
+++ b/solution.py
@@ -163,8 +163,13 @@
     out_cols = lax.all_to_all(out_blocks, "grp", split_axis=0, concat_axis=0, tiled=True)
     out_cols = out_cols.reshape(groups * w_out.shape[0], column_width)
     attended = attention(cache_len, query, key_new, value_new, cache_kv)
-    attended_full = lax.all_gather(attended, "grp", axis=1, tiled=True)
-    attn_share = jnp.dot(attended_full, out_cols, preferred_element_type=jnp.float32)
+    attended_all = lax.all_gather(attended, "grp", axis=0, tiled=False)
+    attn_share = jnp.einsum(
+        "gtd,gdc->tc",
+        attended_all,
+        out_cols.reshape(groups, column_width, column_width),
+        preferred_element_type=jnp.float32,
+    )
     after_cols = (resid.astype(jnp.float32) + attn_share).astype(jnp.bfloat16)
     after_full = lax.all_gather(after_cols, "grp", axis=1, tiled=True)
     after_wide = after_full.astype(jnp.float32)

time: 194 us -> 194 us (level)
  no operation moved by 1% of the time
where the time goes in v13:
time: 194 us; the launch traced here: 193 us
  waiting for transfers between devices  78.9 us (41%)
  blocking collectives  60.2 us (31%)
  starting transfers between devices  22.3 us (11%)
  between operations  14.2 us (7%)
  Pallas kernels  13.4 us (7%)
  matrix products  2.35 us (1%)
    all_gather x1, waiting for transfers between devices, body(): gathered = lax.all_gather(arrived, 'grp', axis=0, tiled=False)  31 us
    reduce_scatter x1, waiting for transfers between devices, body(): lax.psum_scatter(slice_out, 'grp', scatter_dimension=0, tiled=True)  30.5 us
    all_to_all x1, blocking collectives, body(): lax.all_to_all(outgoing, 'ep', split_axis=0, concat_axis=0, tiled=True)  29.5 us
    all_gather x1, blocking collectives, body(): attended_all = lax.all_gather(attended, 'grp', axis=0, tiled=False)  17.5 us
    all_to_all x1, waiting for transfers between devices, body(): lax.all_to_all(expert_out, 'ep', split_axis=0, concat_axis=0, tiled=True)  17.4 us
    all_gather x1, blocking collectives, body(): after_full = lax.all_gather(after_cols, 'grp', axis=1, tiled=True)  13.2 us
    all_to_all x1, starting transfers between devices, body(): lax.all_to_all(expert_out, 'ep', split_axis=0, concat_axis=0, tiled=True)  12.4 us
    all_to_all x1, starting transfers between devices, body(): lax.all_to_all(out_blocks, 'grp', split_axis=0, concat_axis=0, tiled=True)  9.79 us
  transfers between devices with their start and end apart: 4, of which 3 were waited for; matrix products, arithmetic and copies ran while one was open for 1% of the time, Pallas kernels for 2%

profile of v13, /device:TPU:7, one launch (start us, length us, event | category | flops | bytes accessed | tf_op | source)
XLA Modules:
  0.0 193.3 jit_solution(2748002629086928122)
XLA Ops:
  7.2 0.0 copy-start
  7.2 0.0 copy-start.3
  7.2 2.3 %shard_map.132 = bf16[8,256,256]{2,1,0:T(8,128)(2,1)} custom-call(bf16[256,2048]{1,0:T(8,128)(2,1)} %x_ref.1), custom_call_target="tpu_custom_call" | custom-call | tf_op jit(solution)/shard_map/pallas_call | solution.py:86
  9.5 9.8 %all-to-all-start = ((bf16[8,256,256]{2,1,0:T(8,128)(2,1)}), bf16[8,256,256]{2,1,0:T(8,128)(2,1)S(1)}, u32[]{:S(2)}, u32[]{:S(2)}) async-start(bf16[8,256,256]{2,1,0:T(8,128)(2,1)} %shard_map.132), calls=%async_computation | async-start | bytes 2097152 | tf_op jit(solution)/shard_map/all_to_all | solution.py:163
  19.3 0.1 copy.31
  19.4 0.1 eq.35
  19.6 0.3 fusion.3
  19.9 0.1 convert_element_type.62
  20.0 0.1 copy.32
  20.0 3.0 %shard_map.131 = bf16[128,256]{1,0:T(8,128)(2,1)} custom-call(s32[64]{0:T(128)} %len_ref.1, bf16[128,256]{1,0:T(8,128)(2,1)} %q_ref.1, bf16[128,256]{1,0:T(8,128)(2,1)} %kn_ref.1, bf16[128,256]{1,0:T(8,128)(2,1)} %vn_ref.1, bf16[2,1024,256]{2,1,0:T(8,128)(2,1)} %cache_ref.1), custom_call_target="tpu_custom_call" | custom-call | tf_op jit(solution)/shard_map/pallas_call | solution.py:62
  23.0 0.4 fusion
  23.4 17.5 %all-gather = bf16[1024,256]{1,0:T(8,128)(2,1)S(1)} all-gather(bf16[128,256]{1,0:T(8,128)(2,1)} %shard_map.131), channel_id=2, replica_groups=mesh['grp'=8,'ep'=64] {'grp'}, dimensions={0}, use_global_device_ids=true | all-gather | bytes 589824 | tf_op jit(solution)/shard_map/all_gather | solution.py:166
  40.9 0.0 all-to-all-done
  40.9 0.3 fusion.2
  41.2 0.0 copy-start.1
  41.2 0.4 convolution_convert_fusion
  41.6 29.5 %all_to_all.15 = bf16[64,16,256]{2,1,0:T(8,128)(2,1)} all-to-all(bf16[64,16,256]{2,1,0:T(8,128)(2,1)S(1)} %bitcast.25), channel_id=1, replica_groups=mesh['grp'=8,'ep'=64] {'ep'}, dimensions={0} | all-to-all | bytes 1048576 | tf_op jit(solution)/shard_map/all_to_all | solution.py:201
  71.1 0.0 all-gather.3.cloned.1.call-update
  71.1 0.0 reduce-scatter.2.cloned.1.call-start
  71.1 0.6 reshape.75.gain_ref
  71.7 31.0 %all-gather.3.cloned.1.call-done.x_ref = bf16[8,1024,256]{2,1,0:T(8,128)(2,1)} async-done(((bf16[1,1024,256]{2,1,0:T(8,128)(2,1)}), bf16[8,1024,256]{2,1,0:T(8,128)(2,1)}) %all-gather.3.cloned.1.call-update) | async-done | bytes 4194320 | tf_op jit(solution)/shard_map/all_gather | solution.py:203
  102.7 8.1 %shard_map.133 = bf16[8,1024,256]{2,1,0:T(8,128)(2,1)} custom-call(bf16[8,1024,256]{2,1,0:T(8,128)(2,1)} %all-gather.3.cloned.1.call-done.x_ref, f32[8,256]{1,0:T(8,128)} %reshape.75.gain_ref, bf16[2,176,2048]{2,1,0:T(8,128)(2,1)} %bitcast.26, bf16[176,2048]{1,0:T(8,128)(2,1)} %bitcast.27), custom_call_target="tpu_custom_call" | custom-call | tf_op jit(solution)/shard_map/pallas_call | solution.py:124
  110.8 0.0 reduce-scatter.2.cloned.1.call-update
  110.8 0.0 copy-done.1
  110.8 13.2 %all_gather.14 = bf16[128,2048]{1,0:T(8,128)(2,1)S(1)} all-gather(bf16[128,256]{1,0:T(8,128)(2,1)S(1)} %fusion.2), channel_id=1, replica_groups=mesh['grp'=8,'ep'=64] {'grp'}, dimensions={1}, use_global_device_ids=true | all-gather | bytes 589824 | tf_op jit(solution)/shard_map/all_gather | solution.py:174
  124.0 0.2 fusion.4
  124.2 30.5 %reduce-scatter.2.cloned.1.call-done = bf16[1,1024,256]{2,1,0:T(8,128)(2,1)} async-done(((bf16[8,1024,256]{2,1,0:T(8,128)(2,1)}), bf16[1,1024,256]{2,1,0:T(8,128)(2,1)}) %reduce-scatter.2.cloned.1.call-update) | async-done | bytes 524304 | tf_op jit(solution)/shard_map/reduce_scatter | solution.py:206
  154.8 12.4 %all-to-all-start.2 = ((bf16[64,16,256]{2,1,0:T(8,128)(2,1)}), bf16[64,16,256]{2,1,0:T(8,128)(2,1)S(1)}, u32[]{:S(2)}, u32[]{:S(2)}) async-start(bf16[64,16,256]{2,1,0:T(8,128)(2,1)} %bitcast.28), calls=%async_computation.3 | async-start | bytes 1048576 | tf_op jit(solution)/shard_map/all_to_all | solution.py:208
  167.2 0.4 fusion.7
  167.7 0.3 select_reduce_fusion
  168.0 17.4 %all-to-all-done.2 = bf16[64,16,256]{2,1,0:T(8,128)(2,1)S(1)} async-done(((bf16[64,16,256]{2,1,0:T(8,128)(2,1)}), bf16[64,16,256]{2,1,0:T(8,128)(2,1)S(1)}, u32[]{:S(2)}, u32[]{:S(2)}) %all-to-all-start.2) | async-done | bytes 524320 | tf_op jit(solution)/shard_map/all_to_all | solution.py:208
  185.4 1.0 convolution_convert_fusion.1
  (15 shorter events, 0.1 us)
Async XLA Ops:
  7.2 160.0 %copy-start = (bf16[2048,64]{0,1:T(8,128)(2,1)S(1)}, bf16[2048,64]{0,1:T(8,128)(2,1)}, u32[]{:S(2)}) copy-start(bf16[2048,64]{0,1:T(8,128)(2,1)} %param.20) | copy-start | bytes 786436
  7.2 12.1 %copy-start.3 = (s32[128,4]{0,1:T(4,128)S(1)}, s32[128,4]{0,1:T(4,128)}, u32[]{:S(2)}) copy-start(s32[128,4]{0,1:T(4,128)} %param.21) | copy-start | bytes 6148
  9.5 31.4 %copy-start.2 = (bf16[128,256]{1,0:T(8,128)(2,1)S(1)}, bf16[128,256]{1,0:T(8,128)(2,1)}, u32[]{:S(2)}) copy-start(bf16[128,256]{1,0:T(8,128)(2,1)} %param.12) | copy-start | bytes 196612
  9.5 31.4 %all-to-all-start = ((bf16[8,256,256]{2,1,0:T(8,128)(2,1)}), bf16[8,256,256]{2,1,0:T(8,128)(2,1)S(1)}, u32[]{:S(2)}, u32[]{:S(2)}) async-start(bf16[8,256,256]{2,1,0:T(8,128)(2,1)} %shard_map.132), calls=%async_computation | async-start | bytes 2097152 | tf_op jit(solution)/shard_map/all_to_all | solution.py:163
  19.3 83.4 %all-gather.3.cloned.1.call-start = ((), (), s32[]{:S(2)}) async-start(), calls=%async_computation.4 | async-start | bytes 4718592 | tf_op jit(solution)/shard_map/all_gather | solution.py:203
  40.9 30.2 %copy-start.4 = (bf16[2048]{0:T(1024)(128)(2,1)S(1)}, bf16[2048]{0:T(1024)(128)(2,1)}, u32[]{:S(2)}) copy-start(bf16[2048]{0:T(1024)(128)(2,1)} %param.19) | copy-start | bytes 12292
  41.2 69.6 %copy-start.1 = (bf16[128,256]{1,0:T(8,128)(2,1)}, bf16[128,256]{1,0:T(8,128)(2,1)S(1)}, u32[]{:S(2)}) copy-start(bf16[128,256]{1,0:T(8,128)(2,1)S(1)} %fusion.2) | copy-start | bytes 196612
  71.1 83.7 %reduce-scatter.2.cloned.1.call-start = ((), (), s32[]{:S(2)}) async-start(), calls=%async_computation.5 | async-start | bytes 4718592 | tf_op jit(solution)/shard_map/reduce_scatter | solution.py:206
  154.8 30.6 %all-to-all-start.2 = ((bf16[64,16,256]{2,1,0:T(8,128)(2,1)}), bf16[64,16,256]{2,1,0:T(8,128)(2,1)S(1)}, u32[]{:S(2)}, u32[]{:S(2)}) async-start(bf16[64,16,256]{2,1,0:T(8,128)(2,1)} %bitcast.28), calls=%async_computation.3 | async-start | bytes 1048576 | tf_op jit(solution)/shard_map/all_to_all | solution.py:208
Sparse Core Ops, SparseCore 0:
  71.2 31.4 all-gather.2
  110.9 43.7 reduce-scatter.1

commit v14 on v13

--- a/solution.py
+++ b/solution.py
@@ -74,10 +74,16 @@
     )(cache_len, query, key_new, value_new, cache_kv)
 
 
-def blocks_kernel(x_ref, out_ref):
+def blocks_kernel(x_ref, out_ref, sems):
     width = out_ref.shape[-1]
-    for j in range(out_ref.shape[0]):
-        out_ref[j] = x_ref[:, j * width:(j + 1) * width]
+    copies = [
+        pltpu.make_async_copy(x_ref.at[:, j * width:(j + 1) * width], out_ref.at[j], sems.at[j])
+        for j in range(out_ref.shape[0])
+    ]
+    for copy in copies:
+        copy.start()
+    for copy in copies:
+        copy.wait()
 
 
 def column_blocks(matrix, groups):
@@ -85,10 +91,10 @@
     shape = (groups, rows, cols // groups)
     return pl.pallas_call(
         blocks_kernel,
-        grid=(1,),
-        in_specs=[pl.BlockSpec(matrix.shape, lambda i: (0, 0))],
-        out_specs=pl.BlockSpec(shape, lambda i: (0, 0, 0)),
+        in_specs=[pl.BlockSpec(memory_space=pl.ANY)],
+        out_specs=pl.BlockSpec(memory_space=pl.ANY),
         out_shape=jax.ShapeDtypeStruct(shape, matrix.dtype),
+        scratch_shapes=[pltpu.SemaphoreType.DMA((groups,))],
     )(matrix)
 
 

time: 194 us -> 225 us (1.16)
  Pallas kernels: 13.4 us -> 44 us
    pallas_call x1, Pallas kernels: 2.34 us -> 32.9 us  [column_blocks(): pl.pallas_call(blocks_kernel, in_specs=[pl.BlockSpec(memory_space=pl.ANY)...]
  transfers between devices with their start and end apart: 4 -> 4, of which waited for: 3 -> 3; matrix products, arithmetic and copies ran while one was open for 1% -> 1% of each run, Pallas kernels for 2% -> 1%
where the time goes in v14:
time: 225 us; the launch traced here: 224 us
  waiting for transfers between devices  78.9 us (35%)
  blocking collectives  60.2 us (27%)
  Pallas kernels  44 us (20%)
  starting transfers between devices  22.3 us (10%)
  between operations  14.2 us (6%)
  matrix products  2.35 us (1%)
    pallas_call x1, Pallas kernels, column_blocks(): pl.pallas_call(blocks_kernel, in_specs=[pl.BlockSpec(memory_space=pl.ANY)...  32.9 us
    all_gather x1, waiting for transfers between devices, body(): gathered = lax.all_gather(arrived, 'grp', axis=0, tiled=False)  31 us
    reduce_scatter x1, waiting for transfers between devices, body(): lax.psum_scatter(slice_out, 'grp', scatter_dimension=0, tiled=True)  30.5 us
    all_to_all x1, blocking collectives, body(): lax.all_to_all(outgoing, 'ep', split_axis=0, concat_axis=0, tiled=True)  29.5 us
    all_gather x1, blocking collectives, body(): attended_all = lax.all_gather(attended, 'grp', axis=0, tiled=False)  17.5 us
    all_to_all x1, waiting for transfers between devices, body(): lax.all_to_all(expert_out, 'ep', split_axis=0, concat_axis=0, tiled=True)  17.4 us
    all_gather x1, blocking collectives, body(): after_full = lax.all_gather(after_cols, 'grp', axis=1, tiled=True)  13.2 us
    all_to_all x1, starting transfers between devices, body(): lax.all_to_all(expert_out, 'ep', split_axis=0, concat_axis=0, tiled=True)  12.4 us
  transfers between devices with their start and end apart: 4, of which 3 were waited for; matrix products, arithmetic and copies ran while one was open for 1% of the time, Pallas kernels for 1%

profile of v14, /device:TPU:7, one launch (start us, length us, event | category | flops | bytes accessed | tf_op | source)
XLA Modules:
  0.0 223.9 jit_solution(4587520782596771760)
XLA Ops:
  7.2 0.0 copy-start
  7.2 32.9 %shard_map.132 = bf16[8,256,256]{2,1,0:T(8,128)(2,1)} custom-call(bf16[256,2048]{1,0:T(8,128)(2,1)} %x_ref.1), custom_call_target="tpu_custom_call" | custom-call | tf_op jit(solution)/shard_map/pallas_call | solution.py:92
  40.1 0.0 copy-start.2
  40.1 9.8 %all-to-all-start = ((bf16[8,256,256]{2,1,0:T(8,128)(2,1)}), bf16[8,256,256]{2,1,0:T(8,128)(2,1)S(1)}, u32[]{:S(2)}, u32[]{:S(2)}) async-start(bf16[8,256,256]{2,1,0:T(8,128)(2,1)} %shard_map.132), calls=%async_computation | async-start | bytes 2097152 | tf_op jit(solution)/shard_map/all_to_all | solution.py:169
  50.0 0.1 copy.31
  50.1 0.1 eq.35
  50.2 0.3 fusion.3
  50.5 0.1 convert_element_type.62
  50.6 0.1 copy.32
  50.7 3.0 %shard_map.131 = bf16[128,256]{1,0:T(8,128)(2,1)} custom-call(s32[64]{0:T(128)} %len_ref.1, bf16[128,256]{1,0:T(8,128)(2,1)} %q_ref.1, bf16[128,256]{1,0:T(8,128)(2,1)} %kn_ref.1, bf16[128,256]{1,0:T(8,128)(2,1)} %vn_ref.1, bf16[2,1024,256]{2,1,0:T(8,128)(2,1)} %cache_ref.1), custom_call_target="tpu_custom_call" | custom-call | tf_op jit(solution)/shard_map/pallas_call | solution.py:62
  53.6 0.4 fusion
  54.0 17.5 %all-gather = bf16[1024,256]{1,0:T(8,128)(2,1)S(1)} all-gather(bf16[128,256]{1,0:T(8,128)(2,1)} %shard_map.131), channel_id=2, replica_groups=mesh['grp'=8,'ep'=64] {'grp'}, dimensions={0}, use_global_device_ids=true | all-gather | bytes 589824 | tf_op jit(solution)/shard_map/all_gather | solution.py:172
  71.5 0.0 all-to-all-done
  71.5 0.0 copy-done.2
  71.5 0.3 fusion.2
  71.8 0.0 copy-start.1
  71.9 0.4 convolution_convert_fusion
  72.2 29.5 %all_to_all.15 = bf16[64,16,256]{2,1,0:T(8,128)(2,1)} all-to-all(bf16[64,16,256]{2,1,0:T(8,128)(2,1)S(1)} %bitcast.25), channel_id=1, replica_groups=mesh['grp'=8,'ep'=64] {'ep'}, dimensions={0} | all-to-all | bytes 1048576 | tf_op jit(solution)/shard_map/all_to_all | solution.py:207
  101.7 0.0 all-gather.3.cloned.1.call-update
  101.7 0.0 reduce-scatter.2.cloned.1.call-start
  101.8 0.6 reshape.75.gain_ref
  102.4 31.0 %all-gather.3.cloned.1.call-done.x_ref = bf16[8,1024,256]{2,1,0:T(8,128)(2,1)} async-done(((bf16[1,1024,256]{2,1,0:T(8,128)(2,1)}), bf16[8,1024,256]{2,1,0:T(8,128)(2,1)}) %all-gather.3.cloned.1.call-update) | async-done | bytes 4194320 | tf_op jit(solution)/shard_map/all_gather | solution.py:209
  133.3 8.1 %shard_map.133 = bf16[8,1024,256]{2,1,0:T(8,128)(2,1)} custom-call(bf16[8,1024,256]{2,1,0:T(8,128)(2,1)} %all-gather.3.cloned.1.call-done.x_ref, f32[8,256]{1,0:T(8,128)} %reshape.75.gain_ref, bf16[2,176,2048]{2,1,0:T(8,128)(2,1)} %bitcast.26, bf16[176,2048]{1,0:T(8,128)(2,1)} %bitcast.27), custom_call_target="tpu_custom_call" | custom-call | tf_op jit(solution)/shard_map/pallas_call | solution.py:130
  141.4 0.0 reduce-scatter.2.cloned.1.call-update
  141.5 13.2 %all_gather.14 = bf16[128,2048]{1,0:T(8,128)(2,1)S(1)} all-gather(bf16[128,256]{1,0:T(8,128)(2,1)S(1)} %fusion.2), channel_id=1, replica_groups=mesh['grp'=8,'ep'=64] {'grp'}, dimensions={1}, use_global_device_ids=true | all-gather | bytes 589824 | tf_op jit(solution)/shard_map/all_gather | solution.py:180
  154.7 0.2 fusion.4
  154.9 30.5 %reduce-scatter.2.cloned.1.call-done = bf16[1,1024,256]{2,1,0:T(8,128)(2,1)} async-done(((bf16[8,1024,256]{2,1,0:T(8,128)(2,1)}), bf16[1,1024,256]{2,1,0:T(8,128)(2,1)}) %reduce-scatter.2.cloned.1.call-update) | async-done | bytes 524304 | tf_op jit(solution)/shard_map/reduce_scatter | solution.py:212
  185.4 12.4 %all-to-all-start.2 = ((bf16[64,16,256]{2,1,0:T(8,128)(2,1)}), bf16[64,16,256]{2,1,0:T(8,128)(2,1)S(1)}, u32[]{:S(2)}, u32[]{:S(2)}) async-start(bf16[64,16,256]{2,1,0:T(8,128)(2,1)} %bitcast.28), calls=%async_computation.3 | async-start | bytes 1048576 | tf_op jit(solution)/shard_map/all_to_all | solution.py:214
  197.8 0.4 fusion.7
  198.3 0.3 select_reduce_fusion
  198.6 17.4 %all-to-all-done.2 = bf16[64,16,256]{2,1,0:T(8,128)(2,1)S(1)} async-done(((bf16[64,16,256]{2,1,0:T(8,128)(2,1)}), bf16[64,16,256]{2,1,0:T(8,128)(2,1)S(1)}, u32[]{:S(2)}, u32[]{:S(2)}) %all-to-all-start.2) | async-done | bytes 524320 | tf_op jit(solution)/shard_map/all_to_all | solution.py:214
  216.0 1.0 convolution_convert_fusion.1
  (15 shorter events, 0.1 us)
Async XLA Ops:
  7.2 190.7 %copy-start = (bf16[2048,64]{0,1:T(8,128)(2,1)S(1)}, bf16[2048,64]{0,1:T(8,128)(2,1)}, u32[]{:S(2)}) copy-start(bf16[2048,64]{0,1:T(8,128)(2,1)} %param.20) | copy-start | bytes 786436
  7.2 42.8 %copy-start.3 = (s32[128,4]{0,1:T(4,128)S(1)}, s32[128,4]{0,1:T(4,128)}, u32[]{:S(2)}) copy-start(s32[128,4]{0,1:T(4,128)} %param.21) | copy-start | bytes 6148
  40.1 31.4 %copy-start.2 = (bf16[128,256]{1,0:T(8,128)(2,1)S(1)}, bf16[128,256]{1,0:T(8,128)(2,1)}, u32[]{:S(2)}) copy-start(bf16[128,256]{1,0:T(8,128)(2,1)} %param.12) | copy-start | bytes 196612
  40.1 31.4 %all-to-all-start = ((bf16[8,256,256]{2,1,0:T(8,128)(2,1)}), bf16[8,256,256]{2,1,0:T(8,128)(2,1)S(1)}, u32[]{:S(2)}, u32[]{:S(2)}) async-start(bf16[8,256,256]{2,1,0:T(8,128)(2,1)} %shard_map.132), calls=%async_computation | async-start | bytes 2097152 | tf_op jit(solution)/shard_map/all_to_all | solution.py:169
  49.9 83.4 %all-gather.3.cloned.1.call-start = ((), (), s32[]{:S(2)}) async-start(), calls=%async_computation.4 | async-start | bytes 4718592 | tf_op jit(solution)/shard_map/all_gather | solution.py:209
  71.5 30.2 %copy-start.4 = (bf16[2048]{0:T(1024)(128)(2,1)S(1)}, bf16[2048]{0:T(1024)(128)(2,1)}, u32[]{:S(2)}) copy-start(bf16[2048]{0:T(1024)(128)(2,1)} %param.19) | copy-start | bytes 12292
  71.8 69.6 %copy-start.1 = (bf16[128,256]{1,0:T(8,128)(2,1)}, bf16[128,256]{1,0:T(8,128)(2,1)S(1)}, u32[]{:S(2)}) copy-start(bf16[128,256]{1,0:T(8,128)(2,1)S(1)} %fusion.2) | copy-start | bytes 196612
  101.7 83.7 %reduce-scatter.2.cloned.1.call-start = ((), (), s32[]{:S(2)}) async-start(), calls=%async_computation.5 | async-start | bytes 4718592 | tf_op jit(solution)/shard_map/reduce_scatter | solution.py:212
  185.4 30.6 %all-to-all-start.2 = ((bf16[64,16,256]{2,1,0:T(8,128)(2,1)}), bf16[64,16,256]{2,1,0:T(8,128)(2,1)S(1)}, u32[]{:S(2)}, u32[]{:S(2)}) async-start(bf16[64,16,256]{2,1,0:T(8,128)(2,1)} %bitcast.28), calls=%async_computation.3 | async-start | bytes 1048576 | tf_op jit(solution)/shard_map/all_to_all | solution.py:214
Sparse Core Ops, SparseCore 0:
  101.8 31.4 all-gather.2
  141.6 43.7 reduce-scatter.1

commit v15 on v13

--- a/solution.py
+++ b/solution.py
@@ -192,7 +192,7 @@
     matches = slot_row[:, :, None] == slot_ids[None, None, :]
     selection = jnp.any(matches, axis=1).astype(jnp.bfloat16)
     combine = jnp.sum(
-        jnp.where(matches, route_weight[:, :, None].astype(jnp.float32), 0.0), axis=1
+        jnp.where(matches, route_weight[:, :, None], jnp.zeros((), jnp.bfloat16)), axis=1
     )
     outgoing = jnp.einsum(
         "tj,td->jd", selection, after_cols, preferred_element_type=jnp.float32
@@ -209,7 +209,6 @@
     mixed_cols = jnp.dot(
         combine,
         returned.reshape(experts_all * capacity, column_width),
-        precision=lax.Precision.HIGHEST,
         preferred_element_type=jnp.float32,
     )
     return (after_cols, mixed_cols.astype(jnp.bfloat16))

time: 194 us -> 194 us (level)
  no operation moved by 1% of the time
where the time goes in v15:
time: 194 us; the launch traced here: 193 us
  waiting for transfers between devices  78.9 us (41%)
  blocking collectives  60.2 us (31%)
  starting transfers between devices  22.3 us (11%)
  between operations  14.2 us (7%)
  Pallas kernels  13.4 us (7%)
  matrix products  2.19 us (1%)
    all_gather x1, waiting for transfers between devices, body(): gathered = lax.all_gather(arrived, 'grp', axis=0, tiled=False)  31 us
    reduce_scatter x1, waiting for transfers between devices, body(): lax.psum_scatter(slice_out, 'grp', scatter_dimension=0, tiled=True)  30.5 us
    all_to_all x1, blocking collectives, body(): lax.all_to_all(outgoing, 'ep', split_axis=0, concat_axis=0, tiled=True)  29.5 us
    all_gather x1, blocking collectives, body(): attended_all = lax.all_gather(attended, 'grp', axis=0, tiled=False)  17.5 us
    all_to_all x1, waiting for transfers between devices, body(): lax.all_to_all(expert_out, 'ep', split_axis=0, concat_axis=0, tiled=True)  17.4 us
    all_gather x1, blocking collectives, body(): after_full = lax.all_gather(after_cols, 'grp', axis=1, tiled=True)  13.2 us
    all_to_all x1, starting transfers between devices, body(): lax.all_to_all(expert_out, 'ep', split_axis=0, concat_axis=0, tiled=True)  12.4 us
    all_to_all x1, starting transfers between devices, body(): lax.all_to_all(out_blocks, 'grp', split_axis=0, concat_axis=0, tiled=True)  9.79 us
  transfers between devices with their start and end apart: 4, of which 3 were waited for; matrix products, arithmetic and copies ran while one was open for 1% of the time, Pallas kernels for 2%

profile of v15, /device:TPU:7, one launch (start us, length us, event | category | flops | bytes accessed | tf_op | source)
XLA Modules:
  0.0 193.1 jit_solution(10991840610743797392)
XLA Ops:
  7.2 0.0 copy-start
  7.2 0.0 copy-start.3
  7.2 2.3 %shard_map.132 = bf16[8,256,256]{2,1,0:T(8,128)(2,1)} custom-call(bf16[256,2048]{1,0:T(8,128)(2,1)} %x_ref.1), custom_call_target="tpu_custom_call" | custom-call | tf_op jit(solution)/shard_map/pallas_call | solution.py:86
  9.5 9.8 %all-to-all-start = ((bf16[8,256,256]{2,1,0:T(8,128)(2,1)}), bf16[8,256,256]{2,1,0:T(8,128)(2,1)S(1)}, u32[]{:S(2)}, u32[]{:S(2)}) async-start(bf16[8,256,256]{2,1,0:T(8,128)(2,1)} %shard_map.132), calls=%async_computation | async-start | bytes 2097152 | tf_op jit(solution)/shard_map/all_to_all | solution.py:163
  19.3 0.1 copy.31
  19.4 0.1 eq.35
  19.6 0.3 fusion.4
  19.9 0.1 convert_element_type.56
  20.0 0.1 copy.32
  20.0 3.0 %shard_map.131 = bf16[128,256]{1,0:T(8,128)(2,1)} custom-call(s32[64]{0:T(128)} %len_ref.1, bf16[128,256]{1,0:T(8,128)(2,1)} %q_ref.1, bf16[128,256]{1,0:T(8,128)(2,1)} %kn_ref.1, bf16[128,256]{1,0:T(8,128)(2,1)} %vn_ref.1, bf16[2,1024,256]{2,1,0:T(8,128)(2,1)} %cache_ref.1), custom_call_target="tpu_custom_call" | custom-call | tf_op jit(solution)/shard_map/pallas_call | solution.py:62
  23.0 0.4 fusion
  23.4 17.5 %all-gather = bf16[1024,256]{1,0:T(8,128)(2,1)S(1)} all-gather(bf16[128,256]{1,0:T(8,128)(2,1)} %shard_map.131), channel_id=2, replica_groups=mesh['grp'=8,'ep'=64] {'grp'}, dimensions={0}, use_global_device_ids=true | all-gather | bytes 589824 | tf_op jit(solution)/shard_map/all_gather | solution.py:166
  40.9 0.0 all-to-all-done
  40.9 0.3 fusion.3
  41.2 0.0 copy-start.1
  41.2 0.4 convolution_convert_fusion
  41.6 29.5 %all_to_all.15 = bf16[64,16,256]{2,1,0:T(8,128)(2,1)} all-to-all(bf16[64,16,256]{2,1,0:T(8,128)(2,1)S(1)} %bitcast.25), channel_id=1, replica_groups=mesh['grp'=8,'ep'=64] {'ep'}, dimensions={0} | all-to-all | bytes 1048576 | tf_op jit(solution)/shard_map/all_to_all | solution.py:201
  71.1 0.0 all-gather.3.cloned.1.call-update
  71.1 0.0 reduce-scatter.2.cloned.1.call-start
  71.1 0.6 reshape.73.gain_ref
  71.7 31.0 %all-gather.3.cloned.1.call-done.x_ref = bf16[8,1024,256]{2,1,0:T(8,128)(2,1)} async-done(((bf16[1,1024,256]{2,1,0:T(8,128)(2,1)}), bf16[8,1024,256]{2,1,0:T(8,128)(2,1)}) %all-gather.3.cloned.1.call-update) | async-done | bytes 4194320 | tf_op jit(solution)/shard_map/all_gather | solution.py:203
  102.7 8.1 %shard_map.133 = bf16[8,1024,256]{2,1,0:T(8,128)(2,1)} custom-call(bf16[8,1024,256]{2,1,0:T(8,128)(2,1)} %all-gather.3.cloned.1.call-done.x_ref, f32[8,256]{1,0:T(8,128)} %reshape.73.gain_ref, bf16[2,176,2048]{2,1,0:T(8,128)(2,1)} %bitcast.26, bf16[176,2048]{1,0:T(8,128)(2,1)} %bitcast.27), custom_call_target="tpu_custom_call" | custom-call | tf_op jit(solution)/shard_map/pallas_call | solution.py:124
  110.8 0.0 reduce-scatter.2.cloned.1.call-update
  110.8 0.0 copy-done.1
  110.8 13.2 %all_gather.14 = bf16[128,2048]{1,0:T(8,128)(2,1)S(1)} all-gather(bf16[128,256]{1,0:T(8,128)(2,1)S(1)} %fusion.3), channel_id=1, replica_groups=mesh['grp'=8,'ep'=64] {'grp'}, dimensions={1}, use_global_device_ids=true | all-gather | bytes 589824 | tf_op jit(solution)/shard_map/all_gather | solution.py:174
  124.0 0.2 fusion.5
  124.2 30.5 %reduce-scatter.2.cloned.1.call-done = bf16[1,1024,256]{2,1,0:T(8,128)(2,1)} async-done(((bf16[8,1024,256]{2,1,0:T(8,128)(2,1)}), bf16[1,1024,256]{2,1,0:T(8,128)(2,1)}) %reduce-scatter.2.cloned.1.call-update) | async-done | bytes 524304 | tf_op jit(solution)/shard_map/reduce_scatter | solution.py:206
  154.8 12.4 %all-to-all-start.2 = ((bf16[64,16,256]{2,1,0:T(8,128)(2,1)}), bf16[64,16,256]{2,1,0:T(8,128)(2,1)S(1)}, u32[]{:S(2)}, u32[]{:S(2)}) async-start(bf16[64,16,256]{2,1,0:T(8,128)(2,1)} %bitcast.28), calls=%async_computation.3 | async-start | bytes 1048576 | tf_op jit(solution)/shard_map/all_to_all | solution.py:208
  167.2 0.4 fusion.9
  167.7 0.3 fusion.8
  168.0 17.4 %all-to-all-done.2 = bf16[64,16,256]{2,1,0:T(8,128)(2,1)S(1)} async-done(((bf16[64,16,256]{2,1,0:T(8,128)(2,1)}), bf16[64,16,256]{2,1,0:T(8,128)(2,1)S(1)}, u32[]{:S(2)}, u32[]{:S(2)}) %all-to-all-start.2) | async-done | bytes 524320 | tf_op jit(solution)/shard_map/all_to_all | solution.py:208
  185.4 0.9 convolution_convert_fusion.1
  (15 shorter events, 0.1 us)
Async XLA Ops:
  7.2 160.0 %copy-start = (bf16[2048,64]{0,1:T(8,128)(2,1)S(1)}, bf16[2048,64]{0,1:T(8,128)(2,1)}, u32[]{:S(2)}) copy-start(bf16[2048,64]{0,1:T(8,128)(2,1)} %param.20) | copy-start | bytes 786436
  7.2 12.1 %copy-start.3 = (s32[128,4]{0,1:T(4,128)S(1)}, s32[128,4]{0,1:T(4,128)}, u32[]{:S(2)}) copy-start(s32[128,4]{0,1:T(4,128)} %param.21) | copy-start | bytes 6148
  9.5 31.4 %copy-start.2 = (bf16[128,256]{1,0:T(8,128)(2,1)S(1)}, bf16[128,256]{1,0:T(8,128)(2,1)}, u32[]{:S(2)}) copy-start(bf16[128,256]{1,0:T(8,128)(2,1)} %param.12) | copy-start | bytes 196612
  9.5 31.4 %all-to-all-start = ((bf16[8,256,256]{2,1,0:T(8,128)(2,1)}), bf16[8,256,256]{2,1,0:T(8,128)(2,1)S(1)}, u32[]{:S(2)}, u32[]{:S(2)}) async-start(bf16[8,256,256]{2,1,0:T(8,128)(2,1)} %shard_map.132), calls=%async_computation | async-start | bytes 2097152 | tf_op jit(solution)/shard_map/all_to_all | solution.py:163
  19.3 83.4 %all-gather.3.cloned.1.call-start = ((), (), s32[]{:S(2)}) async-start(), calls=%async_computation.4 | async-start | bytes 4718592 | tf_op jit(solution)/shard_map/all_gather | solution.py:203
  40.9 30.2 %copy-start.4 = (bf16[2048]{0:T(1024)(128)(2,1)S(1)}, bf16[2048]{0:T(1024)(128)(2,1)}, u32[]{:S(2)}) copy-start(bf16[2048]{0:T(1024)(128)(2,1)} %param.19) | copy-start | bytes 12292
  41.2 69.6 %copy-start.1 = (bf16[128,256]{1,0:T(8,128)(2,1)}, bf16[128,256]{1,0:T(8,128)(2,1)S(1)}, u32[]{:S(2)}) copy-start(bf16[128,256]{1,0:T(8,128)(2,1)S(1)} %fusion.3) | copy-start | bytes 196612
  71.1 83.7 %reduce-scatter.2.cloned.1.call-start = ((), (), s32[]{:S(2)}) async-start(), calls=%async_computation.5 | async-start | bytes 4718592 | tf_op jit(solution)/shard_map/reduce_scatter | solution.py:206
  154.8 30.6 %all-to-all-start.2 = ((bf16[64,16,256]{2,1,0:T(8,128)(2,1)}), bf16[64,16,256]{2,1,0:T(8,128)(2,1)S(1)}, u32[]{:S(2)}, u32[]{:S(2)}) async-start(bf16[64,16,256]{2,1,0:T(8,128)(2,1)} %bitcast.28), calls=%async_computation.3 | async-start | bytes 1048576 | tf_op jit(solution)/shard_map/all_to_all | solution.py:208
Sparse Core Ops, SparseCore 0:
  71.2 31.4 all-gather.2
  110.9 43.7 reduce-scatter.1

commit v16 on v11

--- a/solution.py
+++ b/solution.py
@@ -14,7 +14,7 @@
 MASKED = -1e30
 
 
-def attention_kernel(len_ref, q_ref, kn_ref, vn_ref, cache_ref, wout_ref, out_ref, blocks_ref):
+def attention_kernel(len_ref, q_ref, kn_ref, vn_ref, cache_ref, wout_ref, out_ref):
     tokens, width = q_ref.shape
     cache_rows = cache_ref.shape[1]
     length = len_ref[lax.axis_index("ep")]
@@ -54,16 +54,16 @@
             old_probs.astype(jnp.bfloat16), cache_ref[1, :, cols], preferred_element_type=jnp.float32
         )
         heads.append((weighted / denominator).astype(jnp.bfloat16))
-    out_ref[...] = jnp.concatenate(heads, axis=1)
-    block_width = blocks_ref.shape[-1]
-    for j in range(blocks_ref.shape[0]):
-        blocks_ref[j] = wout_ref[:, j * block_width:(j + 1) * block_width]
+    attended = jnp.concatenate(heads, axis=1)
+    for j in range(out_ref.shape[0]):
+        out_ref[j, :tokens, :] = attended
+        out_ref[j, tokens:, :] = wout_ref[:, j * width:(j + 1) * width]
 
 
 def attention(cache_len, query, key_new, value_new, cache_kv, w_out, groups):
     whole = lambda shape: pl.BlockSpec(shape, lambda i: (0,) * len(shape))
-    rows, cols = w_out.shape
-    blocks_shape = (groups, rows, cols // groups)
+    tokens, width = query.shape
+    packed_shape = (groups, tokens + w_out.shape[0], width)
     return pl.pallas_call(
         attention_kernel,
         grid=(1,),
@@ -75,11 +75,8 @@
             whole(cache_kv.shape),
             whole(w_out.shape),
         ],
-        out_specs=[whole(query.shape), whole(blocks_shape)],
-        out_shape=[
-            jax.ShapeDtypeStruct(query.shape, jnp.bfloat16),
-            jax.ShapeDtypeStruct(blocks_shape, w_out.dtype),
-        ],
+        out_specs=whole(packed_shape),
+        out_shape=jax.ShapeDtypeStruct(packed_shape, jnp.bfloat16),
     )(cache_len, query, key_new, value_new, cache_kv, w_out)
 
 
@@ -110,7 +107,7 @@
         ).astype(out_ref.dtype)
 
 
-def expert_ffn(gathered, gain_blocks, gate_up, down, row_tile=256):
+def expert_ffn(gathered, gain_blocks, gate_up, down, row_tile=512):
     groups, rows, width = gathered.shape
     return pl.pallas_call(
         ffn_kernel,
@@ -150,11 +147,16 @@
     score_scale = float(HD) ** (-0.5)
     column_start = group_index * column_width
     groups = lax.axis_size("grp")
-    attended, out_blocks = attention(cache_len, query, key_new, value_new, cache_kv, w_out, groups)
-    out_cols = lax.all_to_all(out_blocks, "grp", split_axis=0, concat_axis=0, tiled=True)
-    out_cols = out_cols.reshape(groups * w_out.shape[0], column_width)
-    attended_full = lax.all_gather(attended, "grp", axis=1, tiled=True)
-    attn_share = jnp.dot(attended_full, out_cols, preferred_element_type=jnp.float32)
+    packed = attention(cache_len, query, key_new, value_new, cache_kv, w_out, groups)
+    packed = lax.all_to_all(packed, "grp", split_axis=0, concat_axis=0, tiled=True)
+    attended_all = packed[:, :tokens_here, :]
+    out_cols = packed[:, tokens_here:, :]
+    attn_share = jnp.einsum(
+        "gtd,gdc->tc",
+        attended_all,
+        out_cols.reshape(groups, column_width, column_width),
+        preferred_element_type=jnp.float32,
+    )
     after_cols = (resid.astype(jnp.float32) + attn_share).astype(jnp.bfloat16)
     after_full = lax.all_gather(after_cols, "grp", axis=1, tiled=True)
     after_wide = after_full.astype(jnp.float32)

time: 196 us -> 193 us (0.985)
  blocking collectives: 63.1 us -> 41.8 us
  waiting for transfers between devices: 78.9 us -> 97.2 us
    all_gather x1 -> x0, blocking collectives: 20.4 us -> none  [body(): attended_full = lax.all_gather(attended, 'grp', axis=1, tiled=True)]
    all_to_all x1, waiting for transfers between devices: 0.01 us -> 17.8 us  [body(): lax.all_to_all(packed, 'grp', split_axis=0, concat_axis=0, tiled=True)]
  transfers between devices with their start and end apart: 4 -> 4, of which waited for: 3 -> 4; matrix products, arithmetic and copies ran while one was open for 1% -> 1% of each run, Pallas kernels for 0% -> 0%
where the time goes in v16:
time: 193 us; the launch traced here: 192 us
  waiting for transfers between devices  97.2 us (50%)
  blocking collectives  41.8 us (22%)
  starting transfers between devices  22.1 us (11%)
  between operations  14.2 us (7%)
  Pallas kernels  11.9 us (6%)
  matrix products  2.35 us (1%)
    all_gather x1, waiting for transfers between devices, body(): gathered = lax.all_gather(arrived, 'grp', axis=0, tiled=False)  31.2 us
    reduce_scatter x1, waiting for transfers between devices, body(): lax.psum_scatter(slice_out, 'grp', scatter_dimension=0, tiled=True)  30.6 us
    all_to_all x1, blocking collectives, body(): lax.all_to_all(outgoing, 'ep', split_axis=0, concat_axis=0, tiled=True)  28.6 us
    all_to_all x1, waiting for transfers between devices, body(): lax.all_to_all(packed, 'grp', split_axis=0, concat_axis=0, tiled=True)  17.8 us
    all_to_all x1, waiting for transfers between devices, body(): lax.all_to_all(expert_out, 'ep', split_axis=0, concat_axis=0, tiled=True)  17.5 us
    all_gather x1, blocking collectives, body(): after_full = lax.all_gather(after_cols, 'grp', axis=1, tiled=True)  13.2 us
    all_to_all x1, starting transfers between devices, body(): lax.all_to_all(expert_out, 'ep', split_axis=0, concat_axis=0, tiled=True)  12.2 us
    all_to_all x1, starting transfers between devices, body(): lax.all_to_all(packed, 'grp', split_axis=0, concat_axis=0, tiled=True)  9.81 us
  transfers between devices with their start and end apart: 4, of which 4 were waited for; matrix products, arithmetic and copies ran while one was open for 1% of the time, Pallas kernels for 0%

profile of v16, /device:TPU:7, one launch (start us, length us, event | category | flops | bytes accessed | tf_op | source)
XLA Modules:
  0.0 191.5 jit_solution(13060604778545451662)
XLA Ops:
  7.2 0.0 copy-start
  7.2 3.8 %shard_map.131 = bf16[8,384,256]{2,1,0:T(8,128)(2,1)} custom-call(s32[64]{0:T(128)} %len_ref.1, bf16[128,256]{1,0:T(8,128)(2,1)} %q_ref.1, bf16[128,256]{1,0:T(8,128)(2,1)} %kn_ref.1, bf16[128,256]{1,0:T(8,128)(2,1)} %vn_ref.1, bf16[2,1024,256]{2,1,0:T(8,128)(2,1)} %cache_ref.1, bf16[256,2048]{1,0:T(8,128)(2,1)} %wout_ref.1), custom_call_target="tpu_custom_call" | custom-call | tf_op jit(solution)/shard_map/pallas_call | solution.py:67
  11.0 9.8 %all-to-all-start = ((bf16[8,384,256]{2,1,0:T(8,128)(2,1)}), bf16[8,384,256]{2,1,0:T(8,128)(2,1)S(1)}, u32[]{:S(2)}, u32[]{:S(2)}) async-start(bf16[8,384,256]{2,1,0:T(8,128)(2,1)} %shard_map.131), calls=%async_computation | async-start | bytes 3145728 | tf_op jit(solution)/shard_map/all_to_all | solution.py:151
  20.8 0.1 copy.31
  20.9 0.1 eq.35
  21.0 0.3 fusion.3
  21.3 0.1 convert_element_type.62
  21.5 0.1 copy.32
  21.5 0.4 fusion
  21.9 0.0 copy-start.3
  21.9 17.8 %all-to-all-done = bf16[8,384,256]{2,1,0:T(8,128)(2,1)S(1)} async-done(((bf16[8,384,256]{2,1,0:T(8,128)(2,1)}), bf16[8,384,256]{2,1,0:T(8,128)(2,1)S(1)}, u32[]{:S(2)}, u32[]{:S(2)}) %all-to-all-start) | async-done | bytes 1572896 | tf_op jit(solution)/shard_map/all_to_all | solution.py:151
  39.8 0.0 copy-done.4
  39.8 0.3 fusion.2
  40.1 0.0 copy-start.1
  40.1 0.4 convolution_convert_fusion
  40.5 28.6 %all_to_all.15 = bf16[64,16,256]{2,1,0:T(8,128)(2,1)} all-to-all(bf16[64,16,256]{2,1,0:T(8,128)(2,1)S(1)} %bitcast.21), channel_id=1, replica_groups=mesh['grp'=8,'ep'=64] {'ep'}, dimensions={0} | all-to-all | bytes 1048576 | tf_op jit(solution)/shard_map/all_to_all | solution.py:188
  69.1 0.0 all-gather.2.cloned.1.call-update
  69.2 0.0 reduce-scatter.2.cloned.1.call-start
  69.2 0.6 reshape.75.gain_ref
  69.8 31.2 %all-gather.2.cloned.1.call-done.x_ref = bf16[8,1024,256]{2,1,0:T(8,128)(2,1)} async-done(((bf16[1,1024,256]{2,1,0:T(8,128)(2,1)}), bf16[8,1024,256]{2,1,0:T(8,128)(2,1)}) %all-gather.2.cloned.1.call-update) | async-done | bytes 4194320 | tf_op jit(solution)/shard_map/all_gather | solution.py:190
  101.0 8.1 %shard_map.132 = bf16[8,1024,256]{2,1,0:T(8,128)(2,1)} custom-call(bf16[8,1024,256]{2,1,0:T(8,128)(2,1)} %all-gather.2.cloned.1.call-done.x_ref, f32[8,256]{1,0:T(8,128)} %reshape.75.gain_ref, bf16[2,176,2048]{2,1,0:T(8,128)(2,1)} %bitcast.22, bf16[176,2048]{1,0:T(8,128)(2,1)} %bitcast.23), custom_call_target="tpu_custom_call" | custom-call | tf_op jit(solution)/shard_map/pallas_call | solution.py:112
  109.1 0.0 reduce-scatter.2.cloned.1.call-update
  109.1 0.0 copy-done.1
  109.2 13.2 %all_gather.6 = bf16[128,2048]{1,0:T(8,128)(2,1)S(1)} all-gather(bf16[128,256]{1,0:T(8,128)(2,1)S(1)} %fusion.2), channel_id=1, replica_groups=mesh['grp'=8,'ep'=64] {'grp'}, dimensions={1}, use_global_device_ids=true | all-gather | bytes 589824 | tf_op jit(solution)/shard_map/all_gather | solution.py:161
  122.4 0.2 fusion.4
  122.5 30.6 %reduce-scatter.2.cloned.1.call-done = bf16[1,1024,256]{2,1,0:T(8,128)(2,1)} async-done(((bf16[8,1024,256]{2,1,0:T(8,128)(2,1)}), bf16[1,1024,256]{2,1,0:T(8,128)(2,1)}) %reduce-scatter.2.cloned.1.call-update) | async-done | bytes 524304 | tf_op jit(solution)/shard_map/reduce_scatter | solution.py:193
  153.1 12.2 %all-to-all-start.2 = ((bf16[64,16,256]{2,1,0:T(8,128)(2,1)}), bf16[64,16,256]{2,1,0:T(8,128)(2,1)S(1)}, u32[]{:S(2)}, u32[]{:S(2)}) async-start(bf16[64,16,256]{2,1,0:T(8,128)(2,1)} %bitcast.24), calls=%async_computation.3 | async-start | bytes 1048576 | tf_op jit(solution)/shard_map/all_to_all | solution.py:195
  165.4 0.0 copy-done
  165.4 0.4 fusion.8
  165.8 0.3 select_reduce_fusion
  166.1 17.5 %all-to-all-done.2 = bf16[64,16,256]{2,1,0:T(8,128)(2,1)S(1)} async-done(((bf16[64,16,256]{2,1,0:T(8,128)(2,1)}), bf16[64,16,256]{2,1,0:T(8,128)(2,1)S(1)}, u32[]{:S(2)}, u32[]{:S(2)}) %all-to-all-start.2) | async-done | bytes 524320 | tf_op jit(solution)/shard_map/all_to_all | solution.py:195
  183.6 1.0 convolution_convert_fusion.1
  (13 shorter events, 0.1 us)
Async XLA Ops:
  7.2 158.2 %copy-start = (bf16[2048,64]{0,1:T(8,128)(2,1)S(1)}, bf16[2048,64]{0,1:T(8,128)(2,1)}, u32[]{:S(2)}) copy-start(bf16[2048,64]{0,1:T(8,128)(2,1)} %param.20) | copy-start | bytes 786436
  11.0 9.8 %copy-start.2 = (s32[128,4]{0,1:T(4,128)S(1)}, s32[128,4]{0,1:T(4,128)}, u32[]{:S(2)}) copy-start(s32[128,4]{0,1:T(4,128)} %param.21) | copy-start | bytes 6148
  11.0 28.8 %copy-start.4 = (bf16[128,256]{1,0:T(8,128)(2,1)S(1)}, bf16[128,256]{1,0:T(8,128)(2,1)}, u32[]{:S(2)}) copy-start(bf16[128,256]{1,0:T(8,128)(2,1)} %param.12) | copy-start | bytes 196612
  11.0 28.8 %all-to-all-start = ((bf16[8,384,256]{2,1,0:T(8,128)(2,1)}), bf16[8,384,256]{2,1,0:T(8,128)(2,1)S(1)}, u32[]{:S(2)}, u32[]{:S(2)}) async-start(bf16[8,384,256]{2,1,0:T(8,128)(2,1)} %shard_map.131), calls=%async_computation | async-start | bytes 3145728 | tf_op jit(solution)/shard_map/all_to_all | solution.py:151
  20.8 80.2 %all-gather.2.cloned.1.call-start = ((), (), s32[]{:S(2)}) async-start(), calls=%async_computation.4 | async-start | bytes 4718592 | tf_op jit(solution)/shard_map/all_gather | solution.py:190
  21.9 47.3 %copy-start.3 = (bf16[2048]{0:T(1024)(128)(2,1)S(1)}, bf16[2048]{0:T(1024)(128)(2,1)}, u32[]{:S(2)}) copy-start(bf16[2048]{0:T(1024)(128)(2,1)} %param.19) | copy-start | bytes 12292
  40.1 69.0 %copy-start.1 = (bf16[128,256]{1,0:T(8,128)(2,1)}, bf16[128,256]{1,0:T(8,128)(2,1)S(1)}, u32[]{:S(2)}) copy-start(bf16[128,256]{1,0:T(8,128)(2,1)S(1)} %fusion.2) | copy-start | bytes 196612
  69.2 84.0 %reduce-scatter.2.cloned.1.call-start = ((), (), s32[]{:S(2)}) async-start(), calls=%async_computation.5 | async-start | bytes 4718592 | tf_op jit(solution)/shard_map/reduce_scatter | solution.py:193
  153.1 30.5 %all-to-all-start.2 = ((bf16[64,16,256]{2,1,0:T(8,128)(2,1)}), bf16[64,16,256]{2,1,0:T(8,128)(2,1)S(1)}, u32[]{:S(2)}, u32[]{:S(2)}) async-start(bf16[64,16,256]{2,1,0:T(8,128)(2,1)} %bitcast.24), calls=%async_computation.3 | async-start | bytes 1048576 | tf_op jit(solution)/shard_map/all_to_all | solution.py:195
Sparse Core Ops, SparseCore 0:
  69.3 31.7 all-gather.1
  109.3 43.8 reduce-scatter.1

commit v17 on v16

--- a/solution.py
+++ b/solution.py
@@ -107,7 +107,7 @@
         ).astype(out_ref.dtype)
 
 
-def expert_ffn(gathered, gain_blocks, gate_up, down, row_tile=512):
+def expert_ffn(gathered, gain_blocks, gate_up, down, row_tile=1024):
     groups, rows, width = gathered.shape
     return pl.pallas_call(
         ffn_kernel,

time: 193 us -> 194 us (level)
  no operation moved by 1% of the time
where the time goes in v17:
time: 194 us; the launch traced here: 193 us
  waiting for transfers between devices  97 us (50%)
  blocking collectives  41.8 us (22%)
  starting transfers between devices  22.2 us (11%)
  between operations  14.2 us (7%)
  Pallas kernels  12.9 us (7%)
  matrix products  2.35 us (1%)
    all_gather x1, waiting for transfers between devices, body(): gathered = lax.all_gather(arrived, 'grp', axis=0, tiled=False)  31.2 us
    reduce_scatter x1, waiting for transfers between devices, body(): lax.psum_scatter(slice_out, 'grp', scatter_dimension=0, tiled=True)  30.6 us
    all_to_all x1, blocking collectives, body(): lax.all_to_all(outgoing, 'ep', split_axis=0, concat_axis=0, tiled=True)  28.6 us
    all_to_all x1, waiting for transfers between devices, body(): lax.all_to_all(packed, 'grp', split_axis=0, concat_axis=0, tiled=True)  17.8 us
    all_to_all x1, waiting for transfers between devices, body(): lax.all_to_all(expert_out, 'ep', split_axis=0, concat_axis=0, tiled=True)  17.4 us
    all_gather x1, blocking collectives, body(): after_full = lax.all_gather(after_cols, 'grp', axis=1, tiled=True)  13.2 us
    all_to_all x1, starting transfers between devices, body(): lax.all_to_all(expert_out, 'ep', split_axis=0, concat_axis=0, tiled=True)  12.4 us
    all_to_all x1, starting transfers between devices, body(): lax.all_to_all(packed, 'grp', split_axis=0, concat_axis=0, tiled=True)  9.81 us
  transfers between devices with their start and end apart: 4, of which 4 were waited for; matrix products, arithmetic and copies ran while one was open for 1% of the time, Pallas kernels for 0%

profile of v17, /device:TPU:7, one launch (start us, length us, event | category | flops | bytes accessed | tf_op | source)
XLA Modules:
  0.0 192.5 jit_solution(8410658271600669137)
XLA Ops:
  7.2 0.0 copy-start
  7.2 3.8 %shard_map.131 = bf16[8,384,256]{2,1,0:T(8,128)(2,1)} custom-call(s32[64]{0:T(128)} %len_ref.1, bf16[128,256]{1,0:T(8,128)(2,1)} %q_ref.1, bf16[128,256]{1,0:T(8,128)(2,1)} %kn_ref.1, bf16[128,256]{1,0:T(8,128)(2,1)} %vn_ref.1, bf16[2,1024,256]{2,1,0:T(8,128)(2,1)} %cache_ref.1, bf16[256,2048]{1,0:T(8,128)(2,1)} %wout_ref.1), custom_call_target="tpu_custom_call" | custom-call | tf_op jit(solution)/shard_map/pallas_call | solution.py:67
  11.0 9.8 %all-to-all-start = ((bf16[8,384,256]{2,1,0:T(8,128)(2,1)}), bf16[8,384,256]{2,1,0:T(8,128)(2,1)S(1)}, u32[]{:S(2)}, u32[]{:S(2)}) async-start(bf16[8,384,256]{2,1,0:T(8,128)(2,1)} %shard_map.131), calls=%async_computation | async-start | bytes 3145728 | tf_op jit(solution)/shard_map/all_to_all | solution.py:151
  20.8 0.0 all-gather.2.cloned.1.call-start
  20.8 0.0 copy-done.2
  20.8 0.1 copy.31
  20.9 0.1 eq.35
  21.0 0.3 fusion.3
  21.3 0.1 convert_element_type.62
  21.5 0.1 copy.32
  21.5 0.4 fusion
  21.9 0.0 copy-start.3
  21.9 17.8 %all-to-all-done = bf16[8,384,256]{2,1,0:T(8,128)(2,1)S(1)} async-done(((bf16[8,384,256]{2,1,0:T(8,128)(2,1)}), bf16[8,384,256]{2,1,0:T(8,128)(2,1)S(1)}, u32[]{:S(2)}, u32[]{:S(2)}) %all-to-all-start) | async-done | bytes 1572896 | tf_op jit(solution)/shard_map/all_to_all | solution.py:151
  39.8 0.3 fusion.2
  40.1 0.0 copy-start.1
  40.1 0.4 convolution_convert_fusion
  40.5 28.6 %all_to_all.15 = bf16[64,16,256]{2,1,0:T(8,128)(2,1)} all-to-all(bf16[64,16,256]{2,1,0:T(8,128)(2,1)S(1)} %bitcast.21), channel_id=1, replica_groups=mesh['grp'=8,'ep'=64] {'ep'}, dimensions={0} | all-to-all | bytes 1048576 | tf_op jit(solution)/shard_map/all_to_all | solution.py:188
  69.1 0.0 all-gather.2.cloned.1.call-update
  69.2 0.0 reduce-scatter.2.cloned.1.call-start
  69.2 0.6 reshape.75.gain_ref
  69.8 31.2 %all-gather.2.cloned.1.call-done.x_ref = bf16[8,1024,256]{2,1,0:T(8,128)(2,1)} async-done(((bf16[1,1024,256]{2,1,0:T(8,128)(2,1)}), bf16[8,1024,256]{2,1,0:T(8,128)(2,1)}) %all-gather.2.cloned.1.call-update) | async-done | bytes 4194320 | tf_op jit(solution)/shard_map/all_gather | solution.py:190
  101.0 9.1 %shard_map.132 = bf16[8,1024,256]{2,1,0:T(8,128)(2,1)} custom-call(bf16[8,1024,256]{2,1,0:T(8,128)(2,1)} %all-gather.2.cloned.1.call-done.x_ref, f32[8,256]{1,0:T(8,128)} %reshape.75.gain_ref, bf16[2,176,2048]{2,1,0:T(8,128)(2,1)} %bitcast.22, bf16[176,2048]{1,0:T(8,128)(2,1)} %bitcast.23), custom_call_target="tpu_custom_call" | custom-call | tf_op jit(solution)/shard_map/pallas_call | solution.py:112
  110.1 0.0 reduce-scatter.2.cloned.1.call-update
  110.1 0.0 copy-done.1
  110.1 13.2 %all_gather.6 = bf16[128,2048]{1,0:T(8,128)(2,1)S(1)} all-gather(bf16[128,256]{1,0:T(8,128)(2,1)S(1)} %fusion.2), channel_id=1, replica_groups=mesh['grp'=8,'ep'=64] {'grp'}, dimensions={1}, use_global_device_ids=true | all-gather | bytes 589824 | tf_op jit(solution)/shard_map/all_gather | solution.py:161
  123.3 0.2 fusion.4
  123.5 30.6 %reduce-scatter.2.cloned.1.call-done = bf16[1,1024,256]{2,1,0:T(8,128)(2,1)} async-done(((bf16[8,1024,256]{2,1,0:T(8,128)(2,1)}), bf16[1,1024,256]{2,1,0:T(8,128)(2,1)}) %reduce-scatter.2.cloned.1.call-update) | async-done | bytes 524304 | tf_op jit(solution)/shard_map/reduce_scatter | solution.py:193
  154.1 12.4 %all-to-all-start.2 = ((bf16[64,16,256]{2,1,0:T(8,128)(2,1)}), bf16[64,16,256]{2,1,0:T(8,128)(2,1)S(1)}, u32[]{:S(2)}, u32[]{:S(2)}) async-start(bf16[64,16,256]{2,1,0:T(8,128)(2,1)} %bitcast.24), calls=%async_computation.3 | async-start | bytes 1048576 | tf_op jit(solution)/shard_map/all_to_all | solution.py:195
  166.5 0.4 fusion.8
  167.0 0.3 select_reduce_fusion
  167.3 17.4 %all-to-all-done.2 = bf16[64,16,256]{2,1,0:T(8,128)(2,1)S(1)} async-done(((bf16[64,16,256]{2,1,0:T(8,128)(2,1)}), bf16[64,16,256]{2,1,0:T(8,128)(2,1)S(1)}, u32[]{:S(2)}, u32[]{:S(2)}) %all-to-all-start.2) | async-done | bytes 524320 | tf_op jit(solution)/shard_map/all_to_all | solution.py:195
  184.6 1.0 convolution_convert_fusion.1
  (13 shorter events, 0.1 us)
Async XLA Ops:
  7.2 159.3 %copy-start = (bf16[2048,64]{0,1:T(8,128)(2,1)S(1)}, bf16[2048,64]{0,1:T(8,128)(2,1)}, u32[]{:S(2)}) copy-start(bf16[2048,64]{0,1:T(8,128)(2,1)} %param.20) | copy-start | bytes 786436
  11.0 9.8 %copy-start.2 = (s32[128,4]{0,1:T(4,128)S(1)}, s32[128,4]{0,1:T(4,128)}, u32[]{:S(2)}) copy-start(s32[128,4]{0,1:T(4,128)} %param.21) | copy-start | bytes 6148
  11.0 28.8 %copy-start.4 = (bf16[128,256]{1,0:T(8,128)(2,1)S(1)}, bf16[128,256]{1,0:T(8,128)(2,1)}, u32[]{:S(2)}) copy-start(bf16[128,256]{1,0:T(8,128)(2,1)} %param.12) | copy-start | bytes 196612
  11.0 28.8 %all-to-all-start = ((bf16[8,384,256]{2,1,0:T(8,128)(2,1)}), bf16[8,384,256]{2,1,0:T(8,128)(2,1)S(1)}, u32[]{:S(2)}, u32[]{:S(2)}) async-start(bf16[8,384,256]{2,1,0:T(8,128)(2,1)} %shard_map.131), calls=%async_computation | async-start | bytes 3145728 | tf_op jit(solution)/shard_map/all_to_all | solution.py:151
  20.8 80.2 %all-gather.2.cloned.1.call-start = ((), (), s32[]{:S(2)}) async-start(), calls=%async_computation.4 | async-start | bytes 4718592 | tf_op jit(solution)/shard_map/all_gather | solution.py:190
  21.9 47.3 %copy-start.3 = (bf16[2048]{0:T(1024)(128)(2,1)S(1)}, bf16[2048]{0:T(1024)(128)(2,1)}, u32[]{:S(2)}) copy-start(bf16[2048]{0:T(1024)(128)(2,1)} %param.19) | copy-start | bytes 12292
  40.1 70.0 %copy-start.1 = (bf16[128,256]{1,0:T(8,128)(2,1)}, bf16[128,256]{1,0:T(8,128)(2,1)S(1)}, u32[]{:S(2)}) copy-start(bf16[128,256]{1,0:T(8,128)(2,1)S(1)} %fusion.2) | copy-start | bytes 196612
  69.2 84.9 %reduce-scatter.2.cloned.1.call-start = ((), (), s32[]{:S(2)}) async-start(), calls=%async_computation.5 | async-start | bytes 4718592 | tf_op jit(solution)/shard_map/reduce_scatter | solution.py:193
  154.1 30.6 %all-to-all-start.2 = ((bf16[64,16,256]{2,1,0:T(8,128)(2,1)}), bf16[64,16,256]{2,1,0:T(8,128)(2,1)S(1)}, u32[]{:S(2)}, u32[]{:S(2)}) async-start(bf16[64,16,256]{2,1,0:T(8,128)(2,1)} %bitcast.24), calls=%async_computation.3 | async-start | bytes 1048576 | tf_op jit(solution)/shard_map/all_to_all | solution.py:195
Sparse Core Ops, SparseCore 0:
  69.3 31.7 all-gather.1
  110.2 43.8 reduce-scatter.1

commit v18 on v16

--- a/solution.py
+++ b/solution.py
@@ -181,9 +181,7 @@
     combine = jnp.sum(
         jnp.where(matches, route_weight[:, :, None].astype(jnp.float32), 0.0), axis=1
     )
-    outgoing = jnp.einsum(
-        "tj,td->jd", selection, after_cols, preferred_element_type=jnp.float32
-    ).astype(jnp.bfloat16)
+    outgoing = jnp.einsum("tj,td->jd", selection, after_cols, preferred_element_type=jnp.bfloat16)
     outgoing = outgoing.reshape(experts_all, capacity, column_width)
     arrived = lax.all_to_all(outgoing, "ep", split_axis=0, concat_axis=0, tiled=True)
     arrived = arrived.reshape(experts_all * capacity, column_width)

time: 193 us -> 193 us (level)
  transfers between devices with their start and end apart: 4 -> 4, of which waited for: 4 -> 4; matrix products, arithmetic and copies ran while one was open for 1% -> 2% of each run, Pallas kernels for 0% -> 0%
where the time goes in v18:
time: 193 us; the launch traced here: 192 us
  waiting for transfers between devices  96.8 us (50%)
  blocking collectives  41.8 us (22%)
  starting transfers between devices  22.3 us (12%)
  between operations  14.2 us (7%)
  Pallas kernels  11.9 us (6%)
  matrix products  2.29 us (1%)
    all_gather x1, waiting for transfers between devices, body(): gathered = lax.all_gather(arrived, 'grp', axis=0, tiled=False)  31.2 us
    reduce_scatter x1, waiting for transfers between devices, body(): lax.psum_scatter(slice_out, 'grp', scatter_dimension=0, tiled=True)  30.5 us
    all_to_all x1, blocking collectives, body(): lax.all_to_all(outgoing, 'ep', split_axis=0, concat_axis=0, tiled=True)  28.6 us
    all_to_all x1, waiting for transfers between devices, body(): lax.all_to_all(packed, 'grp', split_axis=0, concat_axis=0, tiled=True)  17.6 us
    all_to_all x1, waiting for transfers between devices, body(): lax.all_to_all(expert_out, 'ep', split_axis=0, concat_axis=0, tiled=True)  17.4 us
    all_gather x1, blocking collectives, body(): after_full = lax.all_gather(after_cols, 'grp', axis=1, tiled=True)  13.2 us
    all_to_all x1, starting transfers between devices, body(): lax.all_to_all(expert_out, 'ep', split_axis=0, concat_axis=0, tiled=True)  12.4 us
    all_to_all x1, starting transfers between devices, body(): lax.all_to_all(packed, 'grp', split_axis=0, concat_axis=0, tiled=True)  9.81 us
  transfers between devices with their start and end apart: 4, of which 4 were waited for; matrix products, arithmetic and copies ran while one was open for 2% of the time, Pallas kernels for 0%

profile of v18, /device:TPU:7, one launch (start us, length us, event | category | flops | bytes accessed | tf_op | source)
XLA Modules:
  0.0 191.5 jit_solution(5604728180199358530)
XLA Ops:
  7.2 0.0 copy-start
  7.2 3.8 %shard_map.131 = bf16[8,384,256]{2,1,0:T(8,128)(2,1)} custom-call(s32[64]{0:T(128)} %len_ref.1, bf16[128,256]{1,0:T(8,128)(2,1)} %q_ref.1, bf16[128,256]{1,0:T(8,128)(2,1)} %kn_ref.1, bf16[128,256]{1,0:T(8,128)(2,1)} %vn_ref.1, bf16[2,1024,256]{2,1,0:T(8,128)(2,1)} %cache_ref.1, bf16[256,2048]{1,0:T(8,128)(2,1)} %wout_ref.1), custom_call_target="tpu_custom_call" | custom-call | tf_op jit(solution)/shard_map/pallas_call | solution.py:67
  11.0 9.8 %all-to-all-start = ((bf16[8,384,256]{2,1,0:T(8,128)(2,1)}), bf16[8,384,256]{2,1,0:T(8,128)(2,1)S(1)}, u32[]{:S(2)}, u32[]{:S(2)}) async-start(bf16[8,384,256]{2,1,0:T(8,128)(2,1)} %shard_map.131), calls=%async_computation | async-start | bytes 3145728 | tf_op jit(solution)/shard_map/all_to_all | solution.py:151
  20.8 0.0 all-gather.2.cloned.1.call-start
  20.8 0.1 copy.37
  20.9 0.1 eq.35
  21.0 0.3 fusion.3
  21.3 0.1 convert_element_type.59
  21.5 0.1 copy.38
  21.5 0.4 fusion
  21.9 0.3 copy.39
  22.2 0.0 copy-start.3
  22.2 17.6 %all-to-all-done = bf16[8,384,256]{2,1,0:T(8,128)(2,1)S(1)} async-done(((bf16[8,384,256]{2,1,0:T(8,128)(2,1)}), bf16[8,384,256]{2,1,0:T(8,128)(2,1)S(1)}, u32[]{:S(2)}, u32[]{:S(2)}) %all-to-all-start) | async-done | bytes 1572896 | tf_op jit(solution)/shard_map/all_to_all | solution.py:151
  39.8 0.3 fusion.2
  40.1 0.0 copy-start.1
  40.1 0.3 fusion.13
  40.4 28.6 %all_to_all.15 = bf16[64,16,256]{2,1,0:T(8,128)(2,1)} all-to-all(bf16[64,16,256]{2,1,0:T(8,128)(2,1)S(1)} %fusion.13), channel_id=1, replica_groups=mesh['grp'=8,'ep'=64] {'ep'}, dimensions={0} | all-to-all | bytes 1048576 | tf_op jit(solution)/shard_map/all_to_all | solution.py:186
  69.0 0.0 all-gather.2.cloned.1.call-update
  69.1 0.0 reduce-scatter.2.cloned.1.call-start
  69.1 0.6 reshape.73.gain_ref
  69.7 31.2 %all-gather.2.cloned.1.call-done.x_ref = bf16[8,1024,256]{2,1,0:T(8,128)(2,1)} async-done(((bf16[1,1024,256]{2,1,0:T(8,128)(2,1)}), bf16[8,1024,256]{2,1,0:T(8,128)(2,1)}) %all-gather.2.cloned.1.call-update) | async-done | bytes 4194320 | tf_op jit(solution)/shard_map/all_gather | solution.py:188
  101.0 8.1 %shard_map.132 = bf16[8,1024,256]{2,1,0:T(8,128)(2,1)} custom-call(bf16[8,1024,256]{2,1,0:T(8,128)(2,1)} %all-gather.2.cloned.1.call-done.x_ref, f32[8,256]{1,0:T(8,128)} %reshape.73.gain_ref, bf16[2,176,2048]{2,1,0:T(8,128)(2,1)} %bitcast.24, bf16[176,2048]{1,0:T(8,128)(2,1)} %bitcast.25), custom_call_target="tpu_custom_call" | custom-call | tf_op jit(solution)/shard_map/pallas_call | solution.py:112
  109.0 0.0 reduce-scatter.2.cloned.1.call-update
  109.1 13.2 %all_gather.6 = bf16[128,2048]{1,0:T(8,128)(2,1)S(1)} all-gather(bf16[128,256]{1,0:T(8,128)(2,1)S(1)} %fusion.2), channel_id=1, replica_groups=mesh['grp'=8,'ep'=64] {'grp'}, dimensions={1}, use_global_device_ids=true | all-gather | bytes 589824 | tf_op jit(solution)/shard_map/all_gather | solution.py:161
  122.3 0.2 fusion.4
  122.5 30.5 %reduce-scatter.2.cloned.1.call-done = bf16[1,1024,256]{2,1,0:T(8,128)(2,1)} async-done(((bf16[8,1024,256]{2,1,0:T(8,128)(2,1)}), bf16[1,1024,256]{2,1,0:T(8,128)(2,1)}) %reduce-scatter.2.cloned.1.call-update) | async-done | bytes 524304 | tf_op jit(solution)/shard_map/reduce_scatter | solution.py:191
  153.0 12.4 %all-to-all-start.2 = ((bf16[64,16,256]{2,1,0:T(8,128)(2,1)}), bf16[64,16,256]{2,1,0:T(8,128)(2,1)S(1)}, u32[]{:S(2)}, u32[]{:S(2)}) async-start(bf16[64,16,256]{2,1,0:T(8,128)(2,1)} %bitcast.26), calls=%async_computation.3 | async-start | bytes 1048576 | tf_op jit(solution)/shard_map/all_to_all | solution.py:193
  165.5 0.0 copy-done
  165.5 0.4 fusion.8
  165.9 0.3 select_reduce_fusion
  166.2 17.4 %all-to-all-done.2 = bf16[64,16,256]{2,1,0:T(8,128)(2,1)S(1)} async-done(((bf16[64,16,256]{2,1,0:T(8,128)(2,1)}), bf16[64,16,256]{2,1,0:T(8,128)(2,1)S(1)}, u32[]{:S(2)}, u32[]{:S(2)}) %all-to-all-start.2) | async-done | bytes 524320 | tf_op jit(solution)/shard_map/all_to_all | solution.py:193
  183.7 1.0 convolution_convert_fusion
  (14 shorter events, 0.1 us)
Async XLA Ops:
  7.2 158.3 %copy-start = (bf16[2048,64]{0,1:T(8,128)(2,1)S(1)}, bf16[2048,64]{0,1:T(8,128)(2,1)}, u32[]{:S(2)}) copy-start(bf16[2048,64]{0,1:T(8,128)(2,1)} %param.20) | copy-start | bytes 786436
  11.0 9.8 %copy-start.2 = (s32[128,4]{0,1:T(4,128)S(1)}, s32[128,4]{0,1:T(4,128)}, u32[]{:S(2)}) copy-start(s32[128,4]{0,1:T(4,128)} %param.21) | copy-start | bytes 6148
  11.0 28.8 %copy-start.4 = (bf16[128,256]{1,0:T(8,128)(2,1)S(1)}, bf16[128,256]{1,0:T(8,128)(2,1)}, u32[]{:S(2)}) copy-start(bf16[128,256]{1,0:T(8,128)(2,1)} %param.12) | copy-start | bytes 196612
  11.0 28.8 %all-to-all-start = ((bf16[8,384,256]{2,1,0:T(8,128)(2,1)}), bf16[8,384,256]{2,1,0:T(8,128)(2,1)S(1)}, u32[]{:S(2)}, u32[]{:S(2)}) async-start(bf16[8,384,256]{2,1,0:T(8,128)(2,1)} %shard_map.131), calls=%async_computation | async-start | bytes 3145728 | tf_op jit(solution)/shard_map/all_to_all | solution.py:151
  20.8 80.1 %all-gather.2.cloned.1.call-start = ((), (), s32[]{:S(2)}) async-start(), calls=%async_computation.4 | async-start | bytes 4718592 | tf_op jit(solution)/shard_map/all_gather | solution.py:188
  22.2 46.9 %copy-start.3 = (bf16[2048]{0:T(1024)(128)(2,1)S(1)}, bf16[2048]{0:T(1024)(128)(2,1)}, u32[]{:S(2)}) copy-start(bf16[2048]{0:T(1024)(128)(2,1)} %param.19) | copy-start | bytes 12292
  40.1 69.0 %copy-start.1 = (bf16[128,256]{1,0:T(8,128)(2,1)}, bf16[128,256]{1,0:T(8,128)(2,1)S(1)}, u32[]{:S(2)}) copy-start(bf16[128,256]{1,0:T(8,128)(2,1)S(1)} %fusion.2) | copy-start | bytes 196612
  69.1 84.0 %reduce-scatter.2.cloned.1.call-start = ((), (), s32[]{:S(2)}) async-start(), calls=%async_computation.5 | async-start | bytes 4718592 | tf_op jit(solution)/shard_map/reduce_scatter | solution.py:191
  153.0 30.6 %all-to-all-start.2 = ((bf16[64,16,256]{2,1,0:T(8,128)(2,1)}), bf16[64,16,256]{2,1,0:T(8,128)(2,1)S(1)}, u32[]{:S(2)}, u32[]{:S(2)}) async-start(bf16[64,16,256]{2,1,0:T(8,128)(2,1)} %bitcast.26), calls=%async_computation.3 | async-start | bytes 1048576 | tf_op jit(solution)/shard_map/all_to_all | solution.py:193
Sparse Core Ops, SparseCore 0:
  69.2 31.7 all-gather.1
  109.2 43.7 reduce-scatter.1
